TPU v7x, 128 devices: a whole 4x4x4 slice. The times are simulated.
128 devices in a mesh: dp: 64 (over x, y, z_hi, core), tensor: 2 (over z_lo).
Axes of the slice: x: 4, y: 4, z: 4 (z_hi: 2, z_lo: 2; z = z_hi * 2 + z_lo), core: 2. Of those that a mesh axis runs over, the one named last changes fastest.
Arguments:
- block_input: bfloat16 [8192, 1024], P('dp'), may hold values from -120 to 120
- cotangent: bfloat16 [8192, 1024], P('dp'), may hold values from -16 to 16
- qkv_weight: bfloat16 [1, 1024, 3072], P(None, None, 'tensor'), may hold values from -2 to 2
- dense_weight: bfloat16 [1, 1024, 1024], P(None, None, 'tensor'), may hold values from -1 to 1
- up_weight: bfloat16 [1, 1024, 4096], P(None, None, 'tensor'), may hold values from -0.1875 to 0.1875
- down_weight: bfloat16 [1, 1024, 4096], P(None, None, 'tensor'), may hold values from -0.09375 to 0.09375
- up_bias: float32 [1, 4096], P(None, 'tensor'), may hold values from -3 to 3
- down_bias: float32 [1, 1024], replicated, may hold values from -3 to 3
- norm_gain: float32 [1, 2, 1024], replicated, may hold values from 0.1 to 1.9
- norm_bias: float32 [1, 2, 1024], replicated, may hold values from -3 to 3
- lengths: int32 [96], replicated, may hold values from 32 to 128, as said below
- owner_group: int32 [96], replicated, may hold values from 0 to 63
- row_offset: int32 [96], replicated, may hold values from 0 to 64
Outputs:
- block_output: float32 [8192, 1024], P('dp')
- input_grad: float32 [8192, 1024], P('dp')
- qkv_grad: float32 [1, 1024, 3072], P(None, 'dp', 'tensor')
- dense_grad: float32 [1, 1024, 1024], P(None, 'dp', 'tensor')
- up_grad: float32 [1, 1024, 4096], P(None, 'dp', 'tensor')
- down_grad: float32 [1, 1024, 4096], P(None, 'dp', 'tensor')
- up_bias_grad: float32 [1, 4, 1024], P(None, 'tensor', 'dp')
- down_bias_grad: float32 [1, 1024], P(None, 'dp')
- norm_gain_grad: float32 [1, 2, 1024], P(None, None, 'dp')
- norm_bias_grad: float32 [1, 2, 1024], P(None, None, 'dp')
Inputs may be any that keep to these rules, and one draw needn't show every extreme that they name: Sequence s occupies rows row_offset[s] to row_offset[s] + lengths[s] - 1 of data group owner_group[s]; sequences of one group do not meet, owner_group never falls along s, and every group holds one or two sequences with 64 or more tokens together.
All inputs are finite; a program needn't handle non-finite values.
Results may differ from a plain program's by a relative error of at most 0.0087.
Values sent between devices are 32-bit elements; how exact they have to be, the bound alone decides.
No kernel may reach another device: no remote copies, remote signals or barrier semaphores. Data moves between devices by JAX's collectives and lax.ppermute only.
A program may use at most 128 MiB of HBM per device.

v0:
```python
import jax
import jax.numpy as jnp
from jax import lax
from jax.sharding import Mesh
from jax.sharding import PartitionSpec as P

HEAD_DIM = 64
ROTARY = 16
LAYERS = 1
DP = ("dp_0", "dp_1", "dp_2", "dp_3")


epsilon = 1e-05


def copy_for_each(shard, axis):
    copies = jnp.broadcast_to(shard, (lax.axis_size(axis), *shard.shape))
    return lax.all_to_all(copies, axis, split_axis=0, concat_axis=0, tiled=True)


def over_copies(shard, axis):
    return copy_for_each(shard, axis).sum(axis=0)


def packed_total(arrays, axis):
    line, at, outs = (jnp.concatenate([a.reshape(-1) for a in arrays]), 0, [])
    so_far = over_copies(line, axis)
    for a in arrays:
        outs.append(so_far[at : at + a.size].reshape(a.shape))
        at += a.size
    return tuple(outs)


def cut_along(shard, dim, count):
    shape = shard.shape
    parts = shard.reshape(*shape[:dim], count, shape[dim] // count, *shape[dim + 1 :])
    return jnp.moveaxis(parts, dim, 0)


def sum_by_chip(shard, chips, core, dim):
    sizes = (lax.axis_size(chips), lax.axis_size(core))
    parts = cut_along(shard, dim, sizes[0] * sizes[1])
    inside = parts.shape[1:]
    parts = parts.reshape(*sizes, *inside).swapaxes(0, 1).reshape(-1, *inside)
    parts = lax.psum_scatter(parts, core, scatter_dimension=0, tiled=True)
    return lax.psum_scatter(parts, chips, scatter_dimension=0, tiled=True)[0]


def layout_rows(lengths, owner_group, row_offset, row_index, group_rows):
    first_row = owner_group * group_rows + row_offset
    inside = (row_index[:, None] >= first_row[None, :]) & (
        row_index[:, None] < (first_row + lengths)[None, :]
    )
    number = jnp.arange(lengths.shape[0], dtype=jnp.int32) + 1
    segment = jnp.sum(jnp.where(inside, number[None, :], 0), axis=1) - 1
    position = jnp.sum(jnp.where(inside, row_index[:, None] - first_row[None, :], 0), axis=1)
    return (segment, position)


def rotary_tables(position):
    half_rot = ROTARY // 2
    frequency = 1.0 / 10000.0 ** (jnp.arange(half_rot, dtype=jnp.float32) * 2.0 / ROTARY)
    angles = position.astype(jnp.float32)[:, None] * frequency[None, :]
    angles = jnp.concatenate([angles, angles], axis=1)
    return (jnp.cos(angles), jnp.sin(angles))


def rotate(tensor_rows, cosine_table, sine_table):
    rotary_part = tensor_rows[..., :ROTARY]
    first_half = rotary_part[..., : ROTARY // 2]
    second_half = rotary_part[..., ROTARY // 2 :]
    turned = jnp.concatenate([-second_half, first_half], axis=-1)
    moved = rotary_part * cosine_table[:, None, :] + turned * sine_table[:, None, :]
    return jnp.concatenate([moved, tensor_rows[..., ROTARY:]], axis=-1)


def rotate_back(grad_rows, cosine_table, sine_table):
    rotary_part = grad_rows[..., :ROTARY]
    scaled = rotary_part * sine_table[:, None, :]
    first_half = scaled[..., : ROTARY // 2]
    second_half = scaled[..., ROTARY // 2 :]
    moved = rotary_part * cosine_table[:, None, :] + jnp.concatenate(
        [second_half, -first_half], axis=-1
    )
    return jnp.concatenate([moved, grad_rows[..., ROTARY:]], axis=-1)


def normalize(hidden, gain_row, bias_row):
    row_mean = jnp.mean(hidden, axis=-1, keepdims=True)
    centred = hidden - row_mean
    inv_scale = lax.rsqrt(jnp.mean(centred * centred, axis=-1, keepdims=True) + epsilon)
    unit_rows = centred * inv_scale
    return (unit_rows * gain_row + bias_row, unit_rows, inv_scale)


def normalize_back(grad_rows, unit_rows, inv_scale, gain_row):
    scaled = grad_rows * gain_row
    return inv_scale * (
        scaled
        - jnp.mean(scaled, axis=-1, keepdims=True)
        - unit_rows * jnp.mean(scaled * unit_rows, axis=-1, keepdims=True)
    )


def gelu_exact(values):
    return 0.5 * values * (1.0 + lax.erf(values * 0.7071067811865476))


def gelu_slope(values):
    return (
        0.5 * (1.0 + lax.erf(values * 0.7071067811865476))
        + values * jnp.exp(-0.5 * values * values) * 0.3989422804014327
    )


def attend(queries, key_rows, value_rows, allowed):
    scores = jnp.einsum("qhd,khd->hqk", queries, key_rows, preferred_element_type=jnp.float32)
    scores = jnp.where(allowed[None], scores, -1e30)
    highest = jnp.max(scores, axis=-1, keepdims=True)
    weights = jnp.where(allowed[None], jnp.exp(scores - highest), 0.0)
    totals = jnp.sum(weights, axis=-1, keepdims=True)
    probs = (weights / totals).astype(jnp.bfloat16)
    context = jnp.einsum(
        "hqk,khd->qhd", probs, value_rows, preferred_element_type=jnp.float32
    ).astype(jnp.bfloat16)
    return (context, (highest + jnp.log(totals))[..., 0])


def attend_back(queries, key_rows, value_rows, allowed, log_total, context, context_grad):
    scores = jnp.einsum("qhd,khd->hqk", queries, key_rows, preferred_element_type=jnp.float32)
    scores = jnp.where(allowed[None], scores, -1e30)
    probs = jnp.where(allowed[None], jnp.exp(scores - log_total[..., None]), 0.0)
    probs_grad = jnp.einsum(
        "qhd,khd->hqk", context_grad, value_rows, preferred_element_type=jnp.float32
    )
    offset_terms = jnp.sum(
        context_grad.astype(jnp.float32) * context.astype(jnp.float32), axis=-1
    ).T
    score_grad = (probs * (probs_grad - offset_terms[..., None])).astype(jnp.bfloat16)
    query_grad = jnp.einsum(
        "hqk,khd->qhd", score_grad, key_rows, preferred_element_type=jnp.float32
    )
    key_grad = jnp.einsum("hqk,qhd->khd", score_grad, queries, preferred_element_type=jnp.float32)
    value_grad = jnp.einsum(
        "hqk,qhd->khd", probs.astype(jnp.bfloat16), context_grad, preferred_element_type=jnp.float32
    )
    return (query_grad, key_grad, value_grad)


def shards(
    block_input,
    cotangent,
    qkv_weight,
    dense_weight,
    up_weight,
    down_weight,
    up_bias,
    down_bias,
    norm_gain,
    norm_bias,
    lengths,
    owner_group,
    row_offset,
):
    row_count = block_input.shape[0]
    model_width = block_input.shape[1]
    qkv_cols = qkv_weight.shape[2]
    head_cols = dense_weight.shape[2]
    hidden_cols = up_weight.shape[2]
    local_heads = head_cols // HEAD_DIM
    table_rows = hidden_cols // model_width
    contract_rows = (((0,), (0,)), ((), ()))
    contract_cols = (((1,), (1,)), ((), ()))
    row_index = lax.axis_index(DP) * row_count + jnp.arange(row_count, dtype=jnp.int32)
    segment, position = layout_rows(lengths, owner_group, row_offset, row_index, row_count)
    valid_rows = (segment >= 0).astype(jnp.float32)[:, None]
    cosine_table, sine_table = rotary_tables(position)
    order_rows = jnp.arange(row_count)
    allowed = (segment[:, None] == segment[None, :]) & (order_rows[None, :] <= order_rows[:, None])
    hidden = block_input.astype(jnp.float32)
    layer_index = 0
    heads_norm, heads_unit, heads_inv = normalize(
        hidden, norm_gain[layer_index, 0], norm_bias[layer_index, 0]
    )
    units_norm, units_unit, units_inv = normalize(
        hidden, norm_gain[layer_index, 1], norm_bias[layer_index, 1]
    )
    heads_in = heads_norm.astype(jnp.bfloat16)
    units_in = units_norm.astype(jnp.bfloat16)
    projected = jnp.dot(heads_in, qkv_weight[layer_index], preferred_element_type=jnp.float32)
    hidden_pre = (
        jnp.dot(units_in, up_weight[layer_index], preferred_element_type=jnp.float32)
        + up_bias[layer_index]
    )
    projected = projected.reshape(row_count, local_heads, 3, HEAD_DIM)
    queries = (rotate(projected[:, :, 0], cosine_table, sine_table) * HEAD_DIM ** (-0.5)).astype(
        jnp.bfloat16
    )
    key_rows = rotate(projected[:, :, 1], cosine_table, sine_table).astype(jnp.bfloat16)
    value_rows = projected[:, :, 2].astype(jnp.bfloat16)
    context, log_total = attend(queries, key_rows, value_rows, allowed)
    activated = gelu_exact(hidden_pre).astype(jnp.bfloat16)
    partial_rows = lax.dot_general(
        context.reshape(row_count, head_cols),
        dense_weight[layer_index],
        contract_cols,
        preferred_element_type=jnp.float32,
    )
    partial_rows = partial_rows + lax.dot_general(
        activated, down_weight[layer_index], contract_cols, preferred_element_type=jnp.float32
    )
    branch = over_copies(partial_rows, "tensor")
    output = hidden + valid_rows * (branch + down_bias[layer_index])
    joined = jnp.concatenate([context.reshape(row_count, head_cols), activated], axis=1)
    saved = (
        heads_in,
        units_in,
        heads_unit,
        heads_inv,
        units_unit,
        units_inv,
        queries,
        key_rows,
        value_rows,
        context,
        log_total,
        hidden_pre,
        joined,
    )
    hidden, saved = (output, saved)
    saved_list = [saved]
    grad_rows = cotangent.astype(jnp.float32)
    per_layer = [None] * LAYERS
    for layer_index in reversed(range(LAYERS)):
        backward_saved = saved_list[layer_index]
        (
            backward_heads_in,
            backward_units_in,
            backward_heads_unit,
            backward_heads_inv,
            backward_units_unit,
            backward_units_inv,
            backward_queries,
            backward_key_rows,
            backward_value_rows,
            backward_context,
            backward_log_total,
            backward_hidden_pre,
            backward_joined,
        ) = backward_saved
        branch_grad = grad_rows * valid_rows
        backward_branch_in = branch_grad.astype(jnp.bfloat16)
        output_weights = jnp.concatenate(
            [dense_weight[layer_index], down_weight[layer_index]], axis=1
        )
        joined_grad = jnp.dot(
            backward_branch_in, output_weights, preferred_element_type=jnp.float32
        )
        context_grad = (
            joined_grad[:, :head_cols]
            .astype(jnp.bfloat16)
            .reshape(row_count, local_heads, HEAD_DIM)
        )
        pre_grad = joined_grad[:, head_cols:] * gelu_slope(backward_hidden_pre)
        backward_pre_in = pre_grad.astype(jnp.bfloat16)
        query_grad, key_grad, value_grad = attend_back(
            backward_queries,
            backward_key_rows,
            backward_value_rows,
            allowed,
            backward_log_total,
            backward_context,
            context_grad,
        )
        query_grad = rotate_back(query_grad * HEAD_DIM ** (-0.5), cosine_table, sine_table)
        key_grad = rotate_back(key_grad, cosine_table, sine_table)
        backward_projected_grad = (
            jnp.stack([query_grad, key_grad, value_grad], axis=2)
            .reshape(row_count, qkv_cols)
            .astype(jnp.bfloat16)
        )
        heads_grad = lax.dot_general(
            backward_projected_grad,
            qkv_weight[layer_index],
            contract_cols,
            preferred_element_type=jnp.float32,
        )
        units_grad = lax.dot_general(
            backward_pre_in,
            up_weight[layer_index],
            contract_cols,
            preferred_element_type=jnp.float32,
        )
        local_back = normalize_back(
            heads_grad, backward_heads_unit, backward_heads_inv, norm_gain[layer_index, 0]
        ) + normalize_back(
            units_grad, backward_units_unit, backward_units_inv, norm_gain[layer_index, 1]
        )
        local_norms = jnp.stack(
            [
                jnp.sum(heads_grad * backward_heads_unit, axis=0),
                jnp.sum(units_grad * backward_units_unit, axis=0),
                jnp.sum(heads_grad, axis=0),
                jnp.sum(units_grad, axis=0),
            ]
        )
        summed_back, summed_norms = packed_total((local_back, local_norms), "tensor")
        backward_small_terms = jnp.concatenate(
            [
                summed_norms,
                jnp.sum(branch_grad, axis=0)[None, :],
                jnp.sum(pre_grad, axis=0).reshape(table_rows, model_width),
            ],
            axis=0,
        )
        qkv_part = lax.dot_general(
            backward_heads_in,
            backward_projected_grad,
            contract_rows,
            preferred_element_type=jnp.float32,
        )
        up_part = lax.dot_general(
            backward_units_in, backward_pre_in, contract_rows, preferred_element_type=jnp.float32
        )
        small_part = backward_small_terms.T
        small_part = jnp.pad(small_part, ((0, 0), (0, 128 - small_part.shape[1])))
        reduced = sum_by_chip(
            jnp.concatenate(
                [
                    jnp.concatenate([qkv_part, up_part, small_part], axis=1),
                    lax.dot_general(
                        backward_branch_in,
                        backward_joined,
                        contract_rows,
                        preferred_element_type=jnp.float32,
                    ),
                ],
                axis=1,
            ),
            ("dp_0", "dp_1", "dp_2"),
            "dp_3",
            0,
        )
        in_width = qkv_cols + hidden_cols + 128
        in_reduced = reduced[:, :in_width]
        out_reduced = reduced[:, in_width:]
        edge_two = qkv_cols + hidden_cols
        backward_small_part = in_reduced[:, edge_two : edge_two + 5 + table_rows]
        layer_grads = (
            in_reduced[:, :qkv_cols],
            out_reduced[:, :head_cols],
            in_reduced[:, qkv_cols:edge_two],
            out_reduced[:, head_cols:],
            backward_small_part[:, 5:].T,
            backward_small_part[:, 4],
            backward_small_part[:, 0:2].T,
            backward_small_part[:, 2:4].T,
        )
        grad_rows, per_layer[layer_index] = (grad_rows + summed_back, layer_grads)
    stacked = [jnp.stack([per_layer[0][member]]) for member in range(8)]
    return (
        hidden,
        grad_rows,
        stacked[0],
        stacked[1],
        stacked[2],
        stacked[3],
        stacked[4],
        stacked[5],
        stacked[6],
        stacked[7],
    )


def solution(mesh):
    split = Mesh(
        mesh.devices.reshape(4, 4, 2, 2, mesh.shape["tensor"]),
        ("dp_0", "dp_1", "dp_2", "dp_3", "tensor"),
    )
    in_specs = (
        P(DP, None),
        P(DP, None),
        P(None, None, "tensor"),
        P(None, None, "tensor"),
        P(None, None, "tensor"),
        P(None, None, "tensor"),
        P(None, "tensor"),
        P(),
        P(),
        P(),
        P(),
        P(),
        P(),
    )
    out_specs = (
        P(DP, None),
        P(DP, None),
        P(None, DP, "tensor"),
        P(None, DP, "tensor"),
        P(None, DP, "tensor"),
        P(None, DP, "tensor"),
        P(None, "tensor", DP),
        P(None, DP),
        P(None, None, DP),
        P(None, None, DP),
    )
    return jax.shard_map(
        shards, mesh=split, in_specs=in_specs, out_specs=out_specs, check_vma=False
    )
```

profile of v0, /device:TPU:0, one launch (start us, length us, event | category | flops | bytes accessed | tf_op | source)
XLA Modules:
  0.0 444.1 jit_solution(2964128059224219452)
XLA Ops:
  13.1 3.2 copy.83
  21.4 5.4 %fusion.97 = (f32[2048]{0:T(1024)}, bf16[128,2048]{1,0:T(8,128)(2,1)}, bf16[128,2048]{1,0:T(8,128)(2,1)S(1)}) fusion(f32[128,2560]{1,0:T(8,128)} %copy-done.44, f32[2048]{0:T(1024)S(1)} %bitcast.158, bf16[1,1024,2048]{2,1,0:T(8,128)(2,1)} %param.17, bf16[128,1024]{1,0:T(8,128)(2,1)S(1)} %copy-done, f32[1024]{0:T(1024)S(1)} %bitcast.144, ...), kind=kOutput, calls=%fused_computation.161 | convolution fusion | flops 541587456 | bytes 6579200 | tf_op jit(solution)/shard_map/dot_general | solution.py:192
  26.8 1.5 fusion.83
  29.5 1.8 multiply_reduce_fusion.2
  33.6 4.5 %all-to-all-start = ((f32[2,128,1024]{2,1,0:T(8,128)}), f32[2,128,1024]{2,1,0:T(8,128)}, u32[]{:S(2)}, u32[]{:S(2)}) async-start(f32[2,128,1024]{2,1,0:T(8,128)} %broadcast_in_dim.51), calls=%async_computation | async-start | bytes 2097152 | tf_op jit(solution)/shard_map/all_to_all | solution.py:18
  40.2 1.6 fusion.16
  47.1 1.8 fusion.48
  49.1 4.7 %fusion.59 = f32[1024,2048]{1,0:T(8,128)} fusion(bf16[128,2048]{1,0:T(8,128)(2,1)S(1)} %copy-done.18, bf16[128,1024]{1,0:T(8,128)(2,1)S(1)} %copy-done, f32[1024]{0:T(1024)S(1)} %bitcast.145, f32[1024]{0:T(1024)S(1)} %bitcast.142, f32[128]{0:T(128)S(1)} %copy-done.41, f32[128]{0:T(128)S(1)} %copy-done.37), kind=kOutput, calls=%fused_computation.88 | convolution fusion | flops 537657344 | bytes 9184256 | tf_op jit(solution)/shard_map/dot_general | solution.py:322
  53.8 1.4 reduce_sum.175
  55.2 2.2 fusion.47
  57.6 1.4 broadcast_in_dim.52
  59.0 3.8 all-to-all-start.1
  62.9 3.7 fusion.94
  66.8 5.6 %fusion.23 = f32[1024,2560]{1,0:T(8,128)} fusion(bf16[128,2048]{1,0:T(8,128)(2,1)S(1)} %copy-done.9, bf16[128,512]{1,0:T(8,128)(2,1)S(1)} %copy.94, bf16[128,1024]{1,0:T(8,128)(2,1)S(1)} %copy-done.13, f32[128]{0:T(128)S(1)} %copy-done.46), kind=kOutput, calls=%fused_computation.40 | convolution fusion | flops 672792576 | bytes 11403776 | tf_op jit(solution)/shard_map/dot_general | solution.py:331
  72.4 4.9 %all-to-all-done.1 = f32[2,1,135168]{2,1,0:T(1,128)S(1)} async-done(((f32[2,1,135168]{2,1,0:T(1,128)}), f32[2,1,135168]{2,1,0:T(1,128)S(1)}, u32[]{:S(2)}, u32[]{:S(2)}) %all-to-all-start.1) | async-done | bytes 1081376 | tf_op jit(solution)/shard_map/all_to_all | solution.py:18
  77.2 5.0 %reduce_sum.185 = f32[135168]{0:T(1024)S(1)} reduce(f32[2,1,135168]{2,1,0:T(1,128)S(1)} %all-to-all-done.1, f32[]{:T(128)} %constant.57.clone.1), dimensions={0,1}, to_apply=%region_16.17 | reduce | flops 135168 | bytes 1622020 | tf_op jit(solution)/shard_map/reduce_sum | solution.py:22
  83.5 9.2 %fusion = f32[1024,6272]{1,0:T(8,128)S(1)} fusion(f32[1024,7]{1,0:T(8,128)S(1)} %bitcast.122, f32[1024,2560]{1,0:T(8,128)} %fusion.23, f32[1024,2048]{1,0:T(8,128)} %fusion.59, f32[1024,1536]{1,0:T(8,128)} %fusion.94), kind=kLoop, calls=%fused_computation.3 | loop fusion | flops 44957696 | bytes 50884608 | tf_op jit(solution)/shard_map/concatenate | solution.py:328
  92.7 8.8 %copy.95 = f32[2,32,16,6272]{3,2,1,0:T(8,128)} copy(f32[2,32,16,6272]{3,2,0,1:T(8,128)S(1)} %bitcast.117) | data formatting | bytes 51380224 | tf_op jit(solution)/shard_map/transpose | solution.py:44
  101.6 40.8 %reduce-scatter.3.cloned.1.call-done = f32[32,16,6272]{2,1,0:T(8,128)} async-done(((f32[64,16,6272]{2,1,0:T(8,128)}), f32[32,16,6272]{2,1,0:T(8,128)}) %reduce-scatter.3.cloned.1.call-update) | async-done | bytes 12845072 | tf_op jit(solution)/shard_map/reduce_scatter | solution.py:45
  142.4 286.1 %reduce-scatter.5.cloned.1.call-done = f32[1,16,6272]{2,1,0:T(8,128)} async-done(((f32[32,16,6272]{2,1,0:T(8,128)}), f32[1,16,6272]{2,1,0:T(8,128)}) %reduce-scatter.5.cloned.1.call-update) | async-done | bytes 401424 | tf_op jit(solution)/shard_map/reduce_scatter | solution.py:46
  428.5 1.4 slice_reduce_fusion
  430.8 1.4 slice_bitcast_fusion.5
  432.2 1.5 slice_bitcast_fusion.4
  433.7 1.7 slice_bitcast_fusion.2
  (172 shorter events, 25.7 us)
Async XLA Ops:
  7.2 9.2 %copy-start = (bf16[128,1024]{1,0:T(8,128)(2,1)S(1)}, bf16[128,1024]{1,0:T(8,128)(2,1)}, u32[]{:S(2)}) copy-start(bf16[128,1024]{1,0:T(8,128)(2,1)} %param.13) | copy-start | bytes 786436
  8.1 10.7 %copy-start.45 = (f32[128]{0:T(128)}, f32[128]{0:T(128)S(1)}, u32[]{:S(2)}) copy-start(f32[128]{0:T(128)S(1)} %compare_convert_fusion) | copy-start | bytes 1540
  9.2 8.3 %copy-start.35 = (f32[128]{0:T(128)}, f32[128]{0:T(128)S(1)}, u32[]{:S(2)}) copy-start(f32[128]{0:T(128)S(1)} %broadcast_multiply_fusion.5) | copy-start | bytes 1540
  10.4 7.1 %copy-start.39 = (f32[128]{0:T(128)}, f32[128]{0:T(128)S(1)}, u32[]{:S(2)}) copy-start(f32[128]{0:T(128)S(1)} %add_rsqrt_fusion) | copy-start | bytes 1540
  18.5 9.9 %copy-start.16 = (bf16[128,8,48]{0,2,1:T(8,128)(2,1)}, bf16[128,8,48]{0,2,1:T(8,128)(2,1)S(1)}, u32[]{:S(2)}) copy-start(bf16[128,8,48]{0,2,1:T(8,128)(2,1)S(1)} %slice.249) | copy-start | bytes 294916
  18.5 9.9 %copy-start.11 = (f32[128,8,48]{0,2,1:T(8,128)}, f32[128,8,48]{0,2,1:T(8,128)S(1)}, u32[]{:S(2)}) copy-start(f32[128,8,48]{0,2,1:T(8,128)S(1)} %slice.188) | copy-start | bytes 589828
  18.6 9.6 %copy-start.32 = (f32[128,16]{0,1:T(8,128)}, f32[128,16]{0,1:T(8,128)S(1)}, u32[]{:S(2)}) copy-start(f32[128,16]{0,1:T(8,128)S(1)} %get-tuple-element.59) | copy-start | bytes 24580
  18.7 9.6 %copy-start.33 = (f32[128,16]{0,1:T(8,128)}, f32[128,16]{0,1:T(8,128)S(1)}, u32[]{:S(2)}) copy-start(f32[128,16]{0,1:T(8,128)S(1)} %get-tuple-element.58) | copy-start | bytes 24580
  32.5 13.4 %copy-start.1 = (bf16[1,1024,1536]{2,1,0:T(8,128)(2,1)S(1)}, bf16[1,1024,1536]{2,1,0:T(8,128)(2,1)}, u32[]{:S(2)}) copy-start(bf16[1,1024,1536]{2,1,0:T(8,128)(2,1)} %param.15) | copy-start | bytes 9437188
  33.6 20.2 %all-to-all-start = ((f32[2,128,1024]{2,1,0:T(8,128)}), f32[2,128,1024]{2,1,0:T(8,128)}, u32[]{:S(2)}, u32[]{:S(2)}) async-start(f32[2,128,1024]{2,1,0:T(8,128)} %broadcast_in_dim.51), calls=%async_computation | async-start | bytes 2097152 | tf_op jit(solution)/shard_map/all_to_all | solution.py:18
  40.2 6.9 %copy-start.18 = (bf16[128,2048]{1,0:T(8,128)(2,1)S(1)}, bf16[128,2048]{1,0:T(8,128)(2,1)}, u32[]{:S(2)}) copy-start(bf16[128,2048]{1,0:T(8,128)(2,1)} %get-tuple-element.25) | copy-start | bytes 1572868
  40.2 6.9 %copy-start.23 = (f32[1,1,1024]{2,1,0:T(1,128)S(1)}, f32[1,1,1024]{2,1,0:T(1,128)}, u32[]{:S(2)}) copy-start(f32[1,1,1024]{2,1,0:T(1,128)} %copy-done.22) | copy-start | bytes 12292
  40.2 6.9 %copy-start.28 = (f32[1,1,1024]{2,1,0:T(1,128)S(1)}, f32[1,1,1024]{2,1,0:T(1,128)}, u32[]{:S(2)}) copy-start(f32[1,1,1024]{2,1,0:T(1,128)} %get-tuple-element.55) | copy-start | bytes 12292
  40.2 6.9 %copy-start.37 = (f32[128]{0:T(128)S(1)}, f32[128]{0:T(128)}, u32[]{:S(2)}) copy-start(f32[128]{0:T(128)} %copy-done.35) | copy-start | bytes 1540
  40.2 6.9 %copy-start.41 = (f32[128]{0:T(128)S(1)}, f32[128]{0:T(128)}, u32[]{:S(2)}) copy-start(f32[128]{0:T(128)} %copy-done.39) | copy-start | bytes 1540
  40.2 6.9 %copy-start.49 = (bf16[1,1024,2048]{2,1,0:T(8,128)(2,1)S(1)}, bf16[1,1024,2048]{2,1,0:T(8,128)(2,1)}, u32[]{:S(2)}) copy-start(bf16[1,1024,2048]{2,1,0:T(8,128)(2,1)} %param.17) | copy-start | bytes 12582916
  49.0 6.2 %copy-start.24 = (f32[1,1,1024]{2,1,0:T(1,128)S(1)}, f32[1,1,1024]{2,1,0:T(1,128)}, u32[]{:S(2)}) copy-start(f32[1,1,1024]{2,1,0:T(1,128)} %copy-done.22) | copy-start | bytes 12292
  49.0 6.2 %copy-start.29 = (f32[1,1,1024]{2,1,0:T(1,128)S(1)}, f32[1,1,1024]{2,1,0:T(1,128)}, u32[]{:S(2)}) copy-start(f32[1,1,1024]{2,1,0:T(1,128)} %get-tuple-element.55) | copy-start | bytes 12292
  49.0 6.2 %copy-start.38 = (f32[128]{0:T(128)S(1)}, f32[128]{0:T(128)}, u32[]{:S(2)}) copy-start(f32[128]{0:T(128)} %copy-done.35) | copy-start | bytes 1540
  53.8 9.1 %copy-start.6 = (bf16[128,8,3,64]{0,3,2,1:T(8,128)(2,1)S(1)}, bf16[128,8,3,64]{0,3,2,1:T(8,128)(2,1)}, u32[]{:S(2)}) copy-start(bf16[128,8,3,64]{0,3,2,1:T(8,128)(2,1)} %copy-done.5) | copy-start | bytes 1179652
  53.8 9.1 %copy-start.26 = (f32[1,1,1024]{2,1,0:T(1,128)S(1)}, f32[1,1,1024]{2,1,0:T(1,128)}, u32[]{:S(2)}) copy-start(f32[1,1,1024]{2,1,0:T(1,128)} %copy-done.25) | copy-start | bytes 12292
  59.0 18.2 %all-to-all-start.1 = ((f32[2,1,135168]{2,1,0:T(1,128)}), f32[2,1,135168]{2,1,0:T(1,128)S(1)}, u32[]{:S(2)}, u32[]{:S(2)}) async-start(f32[2,1,135168]{2,1,0:T(1,128)} %broadcast_in_dim.52), calls=%async_computation.1 | async-start | bytes 2162688 | tf_op jit(solution)/shard_map/all_to_all | solution.py:18
  62.8 79.6 %reduce-scatter.3.cloned.1.call-start = ((), (), s32[]{:S(2)}) async-start(), calls=%async_computation.4 | async-start | bytes 38535168 | tf_op jit(solution)/shard_map/reduce_scatter | solution.py:45
  101.5 327.0 %reduce-scatter.5.cloned.1.call-start = ((), (), s32[]{:S(2)}) async-start(), calls=%async_computation.5 | async-start | bytes 13246464 | tf_op jit(solution)/shard_map/reduce_scatter | solution.py:46
  (31 other events, 101.3 us)
Sparse Core Ops, SparseCore 0:
  101.7 40.6 reduce-scatter.2
  144.8 283.6 reduce-scatter.4
where the time goes:
time: 445 us; the launch traced here: 444 us
  waiting for transfers between devices  332 us (75%)
  matrix products  33.8 us (8%)
  local copies, waits for them, and re-layouts  30.7 us (7%)
  other arithmetic  24.4 us (5%)
  between operations  15.1 us (3%)
  starting transfers between devices  8.38 us (2%)
    reduce_scatter x1, waiting for transfers between devices, sum_by_chip(): return lax.psum_scatter(parts, chips, scatter_dimension=0, tiled=True)[0]  286 us
    reduce_scatter x1, waiting for transfers between devices, sum_by_chip(): parts = lax.psum_scatter(parts, core, scatter_dimension=0, tiled=True)  40.8 us
    concatenate x1, other arithmetic, shards(): jnp.concatenate([jnp.concatenate([qkv_part, up_part, small_part], axis=1)...  9.22 us
  transfers between devices with their start and end apart: 4, of which 3 were waited for; matrix products, arithmetic and copies ran while one was open for 6% of the time, Pallas kernels for 0%

commit v1 on v0

v1 whole, which is shorter than its diff:
```python
import jax
import jax.numpy as jnp
from jax import lax
from jax.sharding import Mesh
from jax.sharding import PartitionSpec as P

HEAD_DIM = 64
ROTARY = 16
DP = ("dp_0", "dp_1", "dp_2", "dp_3")
X, Y, ZH, CORE = DP
TENSOR = "tensor"

epsilon = 1e-05

CONTRACT_COLS = (((1,), (1,)), ((), ()))


def shift(array, axis, step):
    size = lax.axis_size(axis)
    return lax.ppermute(array, axis, [(i, (i + step) % size) for i in range(size)])


def layout_rows(lengths, owner_group, row_offset, row_index, group_rows):
    first_row = owner_group * group_rows + row_offset
    inside = (row_index[:, None] >= first_row[None, :]) & (
        row_index[:, None] < (first_row + lengths)[None, :]
    )
    number = jnp.arange(lengths.shape[0], dtype=jnp.int32) + 1
    segment = jnp.sum(jnp.where(inside, number[None, :], 0), axis=1) - 1
    position = jnp.sum(jnp.where(inside, row_index[:, None] - first_row[None, :], 0), axis=1)
    return (segment, position)


def rotary_tables(position):
    half_rot = ROTARY // 2
    frequency = 1.0 / 10000.0 ** (jnp.arange(half_rot, dtype=jnp.float32) * 2.0 / ROTARY)
    angles = position.astype(jnp.float32)[:, None] * frequency[None, :]
    angles = jnp.concatenate([angles, angles], axis=1)
    return (jnp.cos(angles), jnp.sin(angles))


def rotate(tensor_rows, cosine_table, sine_table):
    rotary_part = tensor_rows[..., :ROTARY]
    first_half = rotary_part[..., : ROTARY // 2]
    second_half = rotary_part[..., ROTARY // 2 :]
    turned = jnp.concatenate([-second_half, first_half], axis=-1)
    moved = rotary_part * cosine_table[:, None, :] + turned * sine_table[:, None, :]
    return jnp.concatenate([moved, tensor_rows[..., ROTARY:]], axis=-1)


def rotate_back(grad_rows, cosine_table, sine_table):
    rotary_part = grad_rows[..., :ROTARY]
    scaled = rotary_part * sine_table[:, None, :]
    first_half = scaled[..., : ROTARY // 2]
    second_half = scaled[..., ROTARY // 2 :]
    moved = rotary_part * cosine_table[:, None, :] + jnp.concatenate(
        [second_half, -first_half], axis=-1
    )
    return jnp.concatenate([moved, grad_rows[..., ROTARY:]], axis=-1)


def unit(hidden):
    row_mean = jnp.mean(hidden, axis=-1, keepdims=True)
    centred = hidden - row_mean
    inv_scale = lax.rsqrt(jnp.mean(centred * centred, axis=-1, keepdims=True) + epsilon)
    return (centred * inv_scale, inv_scale)


def normalize_back(grad_rows, unit_rows, inv_scale, gain_row):
    scaled = grad_rows * gain_row
    return inv_scale * (
        scaled
        - jnp.mean(scaled, axis=-1, keepdims=True)
        - unit_rows * jnp.mean(scaled * unit_rows, axis=-1, keepdims=True)
    )


def gelu_exact(values):
    return 0.5 * values * (1.0 + lax.erf(values * 0.7071067811865476))


def gelu_slope(values):
    return (
        0.5 * (1.0 + lax.erf(values * 0.7071067811865476))
        + values * jnp.exp(-0.5 * values * values) * 0.3989422804014327
    )


def attend(queries, key_rows, value_rows, allowed):
    scores = jnp.einsum("qhd,khd->hqk", queries, key_rows, preferred_element_type=jnp.float32)
    scores = jnp.where(allowed[None], scores, -1e30)
    highest = jnp.max(scores, axis=-1, keepdims=True)
    weights = jnp.where(allowed[None], jnp.exp(scores - highest), 0.0)
    totals = jnp.sum(weights, axis=-1, keepdims=True)
    probs = (weights / totals).astype(jnp.bfloat16)
    context = jnp.einsum(
        "hqk,khd->qhd", probs, value_rows, preferred_element_type=jnp.float32
    ).astype(jnp.bfloat16)
    return (context, (highest + jnp.log(totals))[..., 0])


def attend_back(queries, key_rows, value_rows, allowed, log_total, context, context_grad):
    scores = jnp.einsum("qhd,khd->hqk", queries, key_rows, preferred_element_type=jnp.float32)
    scores = jnp.where(allowed[None], scores, -1e30)
    probs = jnp.where(allowed[None], jnp.exp(scores - log_total[..., None]), 0.0)
    probs_grad = jnp.einsum(
        "qhd,khd->hqk", context_grad, value_rows, preferred_element_type=jnp.float32
    )
    offset_terms = jnp.sum(
        context_grad.astype(jnp.float32) * context.astype(jnp.float32), axis=-1
    ).T
    score_grad = (probs * (probs_grad - offset_terms[..., None])).astype(jnp.bfloat16)
    query_grad = jnp.einsum(
        "hqk,khd->qhd", score_grad, key_rows, preferred_element_type=jnp.float32
    )
    key_grad = jnp.einsum("hqk,qhd->khd", score_grad, queries, preferred_element_type=jnp.float32)
    value_grad = jnp.einsum(
        "hqk,qhd->khd", probs.astype(jnp.bfloat16), context_grad, preferred_element_type=jnp.float32
    )
    return (query_grad, key_grad, value_grad)


def selection(width):
    ix, iy, core = lax.axis_index(X), lax.axis_index(Y), lax.axis_index(CORE)
    row = jnp.arange(width, dtype=jnp.int32)
    half = width // 2
    block = width // 64
    inner = row % block
    zh = (row // block) % 2
    minor = (row // (2 * block)) % 4
    major = (row % half) // (8 * block)
    x_first = row < half
    at_x = jnp.where(x_first, (ix + major + 1) % 4, minor)
    at_y = jnp.where(x_first, minor, (iy + major + 1) % 4)
    feature = (((at_x * 4 + at_y) * 2 + zh) * 2 + core) * block + inner
    column = jnp.arange(width, dtype=jnp.int32)
    return (feature[:, None] == column[None, :]).astype(jnp.bfloat16)


def pick(chosen, rows):
    return lax.dot_general(
        chosen, rows, CONTRACT_COLS, preferred_element_type=jnp.float32
    ).astype(jnp.bfloat16)


def ring_sum(left, right, axis):
    quarter = left.shape[0] // 4
    half = quarter // 2

    def part(start, stop):
        return jnp.dot(left[start:stop], right, preferred_element_type=jnp.float32)

    from_minus = shift(part(half, 3 * half), axis, 1)
    from_plus = shift(part(3 * half, 5 * half), axis, -1)
    low = shift(part(0, half) + from_minus[half:], axis, 1)
    high = shift(part(5 * half, 6 * half) + from_plus[:half], axis, -1)
    own = part(6 * half, 8 * half)
    return (
        own
        + jnp.concatenate([from_plus[half:], from_minus[:half]], axis=0)
        + jnp.concatenate([low, high], axis=0)
    )


def spread_sum(rows, axes):
    count = 1
    for axis in axes:
        count *= lax.axis_size(axis)
    parts = rows.reshape(count, rows.shape[0] // count, rows.shape[1])
    parts = lax.all_to_all(parts, axes, split_axis=0, concat_axis=0, tiled=True)
    return parts.sum(axis=0)


def shards(
    block_input,
    cotangent,
    qkv_weight,
    dense_weight,
    up_weight,
    down_weight,
    up_bias,
    down_bias,
    norm_gain,
    norm_bias,
    lengths,
    owner_group,
    row_offset,
):
    row_count, model_width = block_input.shape
    qkv_weight, dense_weight = qkv_weight[0], dense_weight[0]
    up_weight, down_weight = up_weight[0], down_weight[0]
    norm_gain, norm_bias = norm_gain[0], norm_bias[0]
    qkv_cols = qkv_weight.shape[1]
    head_cols = dense_weight.shape[1]
    hidden_cols = up_weight.shape[1]
    local_heads = head_cols // HEAD_DIM
    table_rows = hidden_cols // model_width

    group = lax.axis_index(DP)
    hidden = block_input.astype(jnp.float32)
    grad_rows = cotangent.astype(jnp.float32)
    near_hidden, near_grad = lax.optimization_barrier(
        (shift(hidden, CORE, 1), shift(grad_rows, CORE, 1))
    )
    own_index = group * row_count + jnp.arange(row_count, dtype=jnp.int32)
    near_index = (group ^ 1) * row_count + jnp.arange(row_count, dtype=jnp.int32)
    segment, position = layout_rows(lengths, owner_group, row_offset, own_index, row_count)
    near_segment, _ = layout_rows(lengths, owner_group, row_offset, near_index, row_count)
    valid_rows = (segment >= 0).astype(jnp.float32)[:, None]
    near_valid = (near_segment >= 0).astype(jnp.float32)[:, None]
    cosine_table, sine_table = rotary_tables(position)
    order_rows = jnp.arange(row_count)
    allowed = (segment[:, None] == segment[None, :]) & (order_rows[None, :] <= order_rows[:, None])

    unit_rows, inv_scale = unit(hidden)
    heads_in = (unit_rows * norm_gain[0] + norm_bias[0]).astype(jnp.bfloat16)
    units_in = (unit_rows * norm_gain[1] + norm_bias[1]).astype(jnp.bfloat16)
    branch_grad = grad_rows * valid_rows
    branch_in = branch_grad.astype(jnp.bfloat16)

    near_unit, _ = unit(near_hidden)
    near_heads_in = (near_unit * norm_gain[0] + norm_bias[0]).astype(jnp.bfloat16)
    near_units_in = (near_unit * norm_gain[1] + norm_bias[1]).astype(jnp.bfloat16)
    near_branch_in = (near_grad * near_valid).astype(jnp.bfloat16)

    chosen = selection(model_width)
    half = model_width // 2
    branch_left = pick(chosen, jnp.concatenate([branch_in, near_branch_in], axis=0))
    units_left = pick(chosen, jnp.concatenate([units_in, near_units_in], axis=0))
    heads_left = pick(chosen, jnp.concatenate([heads_in, near_heads_in], axis=0))

    def both(rows):
        near = lax.optimization_barrier(shift(rows, CORE, 1)) * near_valid
        return jnp.concatenate([rows.astype(jnp.bfloat16), near.astype(jnp.bfloat16)], axis=0)

    hidden_pre = jnp.dot(units_in, up_weight, preferred_element_type=jnp.float32) + up_bias
    activated_wide = gelu_exact(hidden_pre)
    activated = activated_wide.astype(jnp.bfloat16)
    down_right = both(activated_wide)
    column = hidden_cols // 2
    down_x = ring_sum(branch_left[:half], down_right[:, :column], X)
    down_y = ring_sum(branch_left[half:], down_right[:, column:], Y)

    pre_grad = jnp.dot(branch_in, down_weight, preferred_element_type=jnp.float32) * gelu_slope(
        hidden_pre
    )
    pre_in = pre_grad.astype(jnp.bfloat16)
    up_right = both(pre_grad)
    up_x = ring_sum(units_left[:half], up_right[:, :column], X)
    up_y = ring_sum(units_left[half:], up_right[:, column:], Y)

    projected = jnp.dot(heads_in, qkv_weight, preferred_element_type=jnp.float32)
    projected = projected.reshape(row_count, local_heads, 3, HEAD_DIM)
    queries = (rotate(projected[:, :, 0], cosine_table, sine_table) * HEAD_DIM ** (-0.5)).astype(
        jnp.bfloat16
    )
    key_rows = rotate(projected[:, :, 1], cosine_table, sine_table).astype(jnp.bfloat16)
    value_rows = projected[:, :, 2].astype(jnp.bfloat16)
    context, log_total = attend(queries, key_rows, value_rows, allowed)
    context_flat = context.reshape(row_count, head_cols)
    context_right = both(context_flat.astype(jnp.float32))
    partial_rows = lax.dot_general(
        context_flat, dense_weight, CONTRACT_COLS, preferred_element_type=jnp.float32
    ) + lax.dot_general(
        activated, down_weight, CONTRACT_COLS, preferred_element_type=jnp.float32
    )
    branch = partial_rows + shift(partial_rows, TENSOR, 1)
    output = hidden + valid_rows * (branch + down_bias)

    context_grad = (
        jnp.dot(branch_in, dense_weight, preferred_element_type=jnp.float32)
        .astype(jnp.bfloat16)
        .reshape(row_count, local_heads, HEAD_DIM)
    )
    query_grad, key_grad, value_grad = attend_back(
        queries, key_rows, value_rows, allowed, log_total, context, context_grad
    )
    query_grad = rotate_back(query_grad * HEAD_DIM ** (-0.5), cosine_table, sine_table)
    key_grad = rotate_back(key_grad, cosine_table, sine_table)
    projected_wide = jnp.stack([query_grad, key_grad, value_grad], axis=2).reshape(
        row_count, qkv_cols
    )
    projected_grad = projected_wide.astype(jnp.bfloat16)
    qkv_right = both(projected_wide)
    first = (qkv_cols + head_cols) // 2 - head_cols
    none_a = jnp.zeros((2 * row_count, first), jnp.bfloat16)
    none_b = jnp.zeros((2 * row_count, head_cols), jnp.bfloat16)
    mixed_right = jnp.concatenate(
        [
            jnp.concatenate([context_right, none_a], axis=1),
            jnp.concatenate([none_b, qkv_right[:, :first]], axis=1),
        ],
        axis=0,
    )
    mixed_left = jnp.concatenate([branch_left[:half], heads_left[:half]], axis=1)
    qkv_x = ring_sum(mixed_left, mixed_right, X)
    qkv_y = ring_sum(heads_left[half:], qkv_right[:, first:], Y)

    heads_grad = lax.dot_general(
        projected_grad, qkv_weight, CONTRACT_COLS, preferred_element_type=jnp.float32
    )
    units_grad = lax.dot_general(
        pre_in, up_weight, CONTRACT_COLS, preferred_element_type=jnp.float32
    )
    local_back = normalize_back(
        heads_grad, unit_rows, inv_scale, norm_gain[0]
    ) + normalize_back(units_grad, unit_rows, inv_scale, norm_gain[1])
    input_grad = grad_rows + (local_back + shift(local_back, TENSOR, 1))

    small = jnp.concatenate(
        [
            jnp.sum(heads_grad * unit_rows, axis=0)[None],
            jnp.sum(units_grad * unit_rows, axis=0)[None],
            jnp.sum(heads_grad, axis=0)[None],
            jnp.sum(units_grad, axis=0)[None],
            jnp.sum(branch_grad, axis=0)[None],
            jnp.sum(pre_grad, axis=0).reshape(table_rows, model_width),
        ],
        axis=0,
    )
    groups = lax.axis_size(DP)
    block = model_width // groups
    small_rows = small.shape[0]
    small = small.reshape(small_rows, groups, block).swapaxes(0, 1).reshape(groups, -1)
    small = jnp.pad(small, ((0, 0), (0, 128 - small.shape[1])))
    small = lax.all_to_all(small, DP, split_axis=0, concat_axis=0, tiled=True).sum(axis=0)
    norms = small[: 4 * block]
    norms = (norms + shift(small, TENSOR, 1)[: 4 * block]).reshape(4, block)
    small = small[: small_rows * block].reshape(small_rows, block)

    early_x = spread_sum(jnp.concatenate([down_x, up_x], axis=1), (Y, ZH))
    early_y = spread_sum(jnp.concatenate([down_y, up_y], axis=1), (X, ZH))
    late_x = spread_sum(qkv_x, (Y, ZH))
    late_y = spread_sum(qkv_y, (X, ZH))

    qkv_grad = jnp.concatenate([late_x[:, head_cols:], late_y], axis=1)
    dense_grad = late_x[:, :head_cols]
    down_grad = jnp.concatenate([early_x[:, :column], early_y[:, :column]], axis=1)
    up_grad = jnp.concatenate([early_x[:, column:], early_y[:, column:]], axis=1)
    return (
        output,
        input_grad,
        qkv_grad[None],
        dense_grad[None],
        up_grad[None],
        down_grad[None],
        small[5:][None],
        small[4][None],
        norms[:2][None],
        norms[2:][None],
    )


def solution(mesh):
    split = Mesh(
        mesh.devices.reshape(4, 4, 2, 2, mesh.shape["tensor"]),
        (*DP, TENSOR),
    )
    in_specs = (
        P(DP, None),
        P(DP, None),
        P(None, None, "tensor"),
        P(None, None, "tensor"),
        P(None, None, "tensor"),
        P(None, None, "tensor"),
        P(None, "tensor"),
        P(),
        P(),
        P(),
        P(),
        P(),
        P(),
    )
    out_specs = (
        P(DP, None),
        P(DP, None),
        P(None, DP, "tensor"),
        P(None, DP, "tensor"),
        P(None, DP, "tensor"),
        P(None, DP, "tensor"),
        P(None, "tensor", DP),
        P(None, DP),
        P(None, None, DP),
        P(None, None, DP),
    )
    return jax.shard_map(
        shards, mesh=split, in_specs=in_specs, out_specs=out_specs, check_vma=False
    )
```

time: 445 us -> 226 us (0.51)
  waiting for transfers between devices: 332 us -> 44.9 us
  starting transfers between devices: 8.38 us -> 74.5 us
  matrix products: 33.8 us -> 56.5 us
  between operations: 15.1 us -> 1.83 us
  local copies, waits for them, and re-layouts: 30.7 us -> 19.2 us
    reduce_scatter x2 -> x0, waiting for transfers between devices: 327 us -> none  [the longest x1 286 us: sum_by_chip(): return lax.psum_scatter(parts, chips, scatter_dimension=0, tiled=True)[0]]
    ppermute x0 -> x33, starting transfers between devices: none -> 42.7 us  [shift(): lax.ppermute(array, axis, [(i, (i + step) % size) for i in range(size)])]
    dot_general x10 -> x41, matrix products: 26.4 us -> 54.9 us  [the longest x30 36.6 us: part(): return jnp.dot(left[start:stop], right, preferred_element_type=jnp.float32)]
    all_to_all x2 -> x5, starting transfers between devices: 8.3 us -> 31.8 us  [the longest x4 20.4 us: spread_sum(): parts = lax.all_to_all(parts, axes, split_axis=0, concat_axis=0, tiled=True)]
    ppermute x0 -> x33, waiting for transfers between devices: none -> 22.7 us  [shift(): lax.ppermute(array, axis, [(i, (i + step) % size) for i in range(size)])]
    all_to_all x2 -> x5, waiting for transfers between devices: 4.86 us -> 22.2 us  [the longest x4 22.2 us: spread_sum(): parts = lax.all_to_all(parts, axes, split_axis=0, concat_axis=0, tiled=True)]
    transpose x5 -> x0, local copies, waits for them, and re-layouts: 11.6 us -> none  [the longest x1 8.77 us: sum_by_chip(): parts = parts.reshape(*sizes, *inside).swapaxes(0, 1).reshape(-1, *inside)]
    convert_element_type x1 -> x11, other arithmetic: 0.05 us -> 9.8 us  [the longest x3 2.95 us: both(): near.astype(jnp.bfloat16)]
  transfers between devices with their start and end apart: 4 -> 38, of which waited for: 3 -> 7; matrix products, arithmetic and copies ran while one was open for 6% -> 36% of each run, Pallas kernels for 0% -> 0%
where the time goes in v1:
time: 226 us; the launch traced here: 223 us
  starting transfers between devices  74.5 us (33%)
  matrix products  56.5 us (25%)
  waiting for transfers between devices  44.9 us (20%)
  other arithmetic  26.4 us (12%)
  local copies, waits for them, and re-layouts  19.2 us (8%)
    ppermute x33, starting transfers between devices, shift(): lax.ppermute(array, axis, [(i, (i + step) % size) for i in range(size)])  42.7 us
    dot_general x30, matrix products, part(): return jnp.dot(left[start:stop], right, preferred_element_type=jnp.float32)  36.6 us
    ppermute x33, waiting for transfers between devices, shift(): lax.ppermute(array, axis, [(i, (i + step) % size) for i in range(size)])  22.7 us
    all_to_all x4, waiting for transfers between devices, spread_sum(): parts = lax.all_to_all(parts, axes, split_axis=0, concat_axis=0, tiled=True)  22.2 us
    all_to_all x4, starting transfers between devices, spread_sum(): parts = lax.all_to_all(parts, axes, split_axis=0, concat_axis=0, tiled=True)  20.4 us
    all_to_all x1, starting transfers between devices, shards(): lax.all_to_all(small, DP, split_axis=0, concat_axis=0, tiled=True)  11.3 us
    unnamed x76, local copies, waits for them, and re-layouts  7.62 us
  transfers between devices with their start and end apart: 38, of which 7 were waited for; matrix products, arithmetic and copies ran while one was open for 36% of the time, Pallas kernels for 0%

profile of v1, /device:TPU:0, one launch (start us, length us, event | category | flops | bytes accessed | tf_op | source)
XLA Modules:
  0.0 223.4 jit_solution(17078565550006510744)
XLA Ops:
  7.4 4.7 %copy.59 = bf16[1,1024,1536]{1,2,0:T(8,128)(2,1)} copy(bf16[1,1024,1536]{2,1,0:T(8,128)(2,1)} %param.15) | data formatting | bytes 6291456 | tf_op args[2]
  14.6 3.0 %fusion.61 = f32[128,8,3,64]{0,3,2,1:T(8,128)S(1)} fusion(bf16[8,3,64,1024]{3,2,1,0:T(8,128)(2,1)} %bitcast.130, bf16[128,1024]{1,0:T(8,128)(2,1)S(1)} %get-tuple-element.43), kind=kOutput, calls=%fused_computation.139 | convolution fusion | flops 402653184 | bytes 4194304 | tf_op jit(solution)/shard_map/dot_general | solution.py:252
  24.0 2.2 fusion.222
  31.9 11.3 %all-to-all-start.4 = ((f32[64,1,128]{2,1,0:T(1,128)}), f32[64,1,128]{2,1,0:T(1,128)S(1)}, u32[]{:S(2)}, u32[]{:S(2)}) async-start(f32[64,1,128]{2,1,0:T(1,128)} %copy.75), calls=%async_computation.4 | async-start | bytes 65536 | tf_op jit(solution)/shard_map/all_to_all | solution.py:326
  45.9 2.8 %fusion.24 = bf16[1024,256]{1,0:T(8,128)(2,1)} fusion(s32[1024]{0:T(1024)S(1)} %fusion.188, bf16[128,1024]{1,0:T(8,128)(2,1)S(1)} %copy-done.29, bf16[128,1024]{1,0:T(8,128)(2,1)} %copy-done.24), kind=kOutput, calls=%fused_computation.22 | convolution fusion | flops 539230208 | bytes 1052672 | tf_op jit(solution)/shard_map/dot_general | solution.py:141
  94.1 8.7 %collective-permute-done.8 = f32[64,1024]{1,0:T(8,128)S(1)} collective-permute-done((f32[64,1024]{1,0:T(8,128)S(1)}, f32[64,1024]{1,0:T(8,128)S(1)}, u32[]{:S(2)}, u32[]{:S(2)}) %collective-permute-start.8) | collective-permute-done | bytes 262176 | tf_op jit(solution)/shard_map/ppermute | solution.py:20
  102.8 3.2 %collective-permute-start.20 = (f32[128,1024]{1,0:T(8,128)}, f32[128,1024]{1,0:T(8,128)}, u32[]{:S(2)}, u32[]{:S(2)}) collective-permute-start(f32[128,1024]{1,0:T(8,128)} %fusion.102), channel_id=1, source_target_pairs={{0,96},{32,0},{64,32},{96,64},{1,97},{33,1},{65,33},{97,65},{2,98}... | collective-permute-start | bytes 1572872 | tf_op jit(solution)/shard_map/ppermute | solution.py:20
  107.4 6.2 %all-to-all-start = ((f32[8,16,1024]{2,1,0:T(8,128)}), f32[8,16,1024]{2,1,0:T(8,128)}, u32[]{:S(2)}, u32[]{:S(2)}) async-start(f32[8,16,1024]{2,1,0:T(8,128)} %bitcast.136), calls=%async_computation | async-start | bytes 1048576 | tf_op jit(solution)/shard_map/all_to_all | solution.py:170
  121.5 2.6 %collective-permute-start.28 = (f32[128,1024]{1,0:T(8,128)S(1)}, f32[128,1024]{1,0:T(8,128)S(1)}, u32[]{:S(2)}, u32[]{:S(2)}) collective-permute-start(f32[128,1024]{1,0:T(8,128)S(1)} %copy-done.26), channel_id=1, source_target_pairs={{0,24},{8,0},{16,8},{24,16},{1,25},{9,1},{17,9},{25,17},{2,26},{10... | collective-permute-start | bytes 1572872 | tf_op jit(solution)/shard_map/ppermute | solution.py:20
  125.2 8.9 %collective-permute-done.25 = f32[128,1024]{1,0:T(8,128)S(1)} collective-permute-done((f32[128,1024]{1,0:T(8,128)}, f32[128,1024]{1,0:T(8,128)S(1)}, u32[]{:S(2)}, u32[]{:S(2)}) %collective-permute-start.25) | collective-permute-done | bytes 524320 | tf_op jit(solution)/shard_map/ppermute | solution.py:20
  136.0 3.1 %collective-permute-start.13 = (f32[64,1024]{1,0:T(8,128)S(1)}, f32[64,1024]{1,0:T(8,128)S(1)}, u32[]{:S(2)}, u32[]{:S(2)}) collective-permute-start(f32[64,1024]{1,0:T(8,128)S(1)} %copy-done.31), channel_id=1, source_target_pairs={{0,24},{8,0},{16,8},{24,16},{1,25},{9,1},{17,9},{25,17},{2,26},{10... | collective-permute-start | bytes 786440 | tf_op jit(solution)/shard_map/ppermute | solution.py:20
  140.8 3.8 %collective-permute-done.29 = f32[128,1024]{1,0:T(8,128)S(1)} collective-permute-done((f32[128,1024]{1,0:T(8,128)}, f32[128,1024]{1,0:T(8,128)S(1)}, u32[]{:S(2)}, u32[]{:S(2)}) %collective-permute-start.29) | collective-permute-done | bytes 524320 | tf_op jit(solution)/shard_map/ppermute | solution.py:20
  146.3 3.2 %collective-permute-start.18 = (f32[64,1024]{1,0:T(8,128)S(1)}, f32[64,1024]{1,0:T(8,128)S(1)}, u32[]{:S(2)}, u32[]{:S(2)}) collective-permute-start(f32[64,1024]{1,0:T(8,128)S(1)} %slice_add_fusion.6), channel_id=1, source_target_pairs={{0,96},{32,0},{64,32},{96,64},{1,97},{33,1},{65,33},{97,65},{2,98}... | collective-permute-start | bytes 786440 | tf_op jit(solution)/shard_map/ppermute | solution.py:20
  151.3 3.2 %collective-permute-start.23 = (f32[64,1024]{1,0:T(8,128)S(1)}, f32[64,1024]{1,0:T(8,128)}, u32[]{:S(2)}, u32[]{:S(2)}) collective-permute-start(f32[64,1024]{1,0:T(8,128)S(1)} %slice_add_fusion.4), channel_id=1, source_target_pairs={{0,96},{32,0},{64,32},{96,64},{1,97},{33,1},{65,33},{97,65},{2,98}... | collective-permute-start | bytes 786440 | tf_op jit(solution)/shard_map/ppermute | solution.py:20
  161.1 3.2 %collective-permute-start.27 = (f32[64,1024]{1,0:T(8,128)}, f32[64,1024]{1,0:T(8,128)}, u32[]{:S(2)}, u32[]{:S(2)}) collective-permute-start(f32[64,1024]{1,0:T(8,128)} %slice_add_fusion.2), channel_id=1, source_target_pairs={{0,24},{8,0},{16,8},{24,16},{1,25},{9,1},{17,9},{25,17},{2,26},{10... | collective-permute-start | bytes 786440 | tf_op jit(solution)/shard_map/ppermute | solution.py:20
  166.2 3.2 %collective-permute-start.31 = (f32[64,1024]{1,0:T(8,128)}, f32[64,1024]{1,0:T(8,128)}, u32[]{:S(2)}, u32[]{:S(2)}) collective-permute-start(f32[64,1024]{1,0:T(8,128)} %slice_add_fusion), channel_id=1, source_target_pairs={{0,24},{8,0},{16,8},{24,16},{1,25},{9,1},{17,9},{25,17},{2,26},{10... | collective-permute-start | bytes 786440 | tf_op jit(solution)/shard_map/ppermute | solution.py:20
  169.4 4.2 %all-to-all-start.1 = ((f32[8,16,1024]{2,1,0:T(8,128)}), f32[8,16,1024]{2,1,0:T(8,128)}, u32[]{:S(2)}, u32[]{:S(2)}) async-start(f32[8,16,1024]{2,1,0:T(8,128)} %bitcast.131), calls=%async_computation.1 | async-start | bytes 1048576 | tf_op jit(solution)/shard_map/all_to_all | solution.py:170
  177.3 6.3 %all-to-all-done.1 = f32[8,16,1024]{2,1,0:T(8,128)} async-done(((f32[8,16,1024]{2,1,0:T(8,128)}), f32[8,16,1024]{2,1,0:T(8,128)}, u32[]{:S(2)}, u32[]{:S(2)}) %all-to-all-start.1) | async-done | bytes 524320 | tf_op jit(solution)/shard_map/all_to_all | solution.py:170
  183.6 3.6 %all-to-all-start.2 = ((f32[8,16,2048]{2,1,0:T(8,128)}), f32[8,16,2048]{2,1,0:T(8,128)S(1)}, u32[]{:S(2)}, u32[]{:S(2)}) async-start(f32[8,16,2048]{2,1,0:T(8,128)} %bitcast.34), calls=%async_computation.2 | async-start | bytes 2097152 | tf_op jit(solution)/shard_map/all_to_all | solution.py:170
  187.2 2.6 %add_multiply_fusion = (f32[128,1024]{1,0:T(8,128)}, f32[128,1024]{1,0:T(8,128)}) fusion(bf16[128,1024]{1,0:T(8,128)(2,1)S(1)} %copy-done.5, f32[128,1024]{1,0:T(8,128)S(1)} %copy-done.14, f32[128,1024]{1,0:T(8,128)} %get-tuple-element.86, f32[128]{0:T(128)S(1)} %broadcast_multiply_fusion.2, f32[128]{0:T(128)S(1)} %broadcast_multiply_fusion.3, ...), kind=kLoop, calls=%fused_computation.95 | loop fusion | flops 2228224 | bytes 3423744 | tf_op jit(solution)/shard_map/add | solution.py:305
  193.9 9.7 %all-to-all-done.2 = f32[8,16,2048]{2,1,0:T(8,128)S(1)} async-done(((f32[8,16,2048]{2,1,0:T(8,128)}), f32[8,16,2048]{2,1,0:T(8,128)S(1)}, u32[]{:S(2)}, u32[]{:S(2)}) %all-to-all-start.2) | async-done | bytes 1048608 | tf_op jit(solution)/shard_map/all_to_all | solution.py:170
  203.6 6.4 %all-to-all-start.3 = ((f32[8,16,2048]{2,1,0:T(8,128)}), f32[8,16,2048]{2,1,0:T(8,128)S(1)}, u32[]{:S(2)}, u32[]{:S(2)}) async-start(f32[8,16,2048]{2,1,0:T(8,128)} %bitcast.35), calls=%async_computation.3 | async-start | bytes 2097152 | tf_op jit(solution)/shard_map/all_to_all | solution.py:170
  210.0 2.2 add_add_fusion
  215.7 6.3 %all-to-all-done.3 = f32[8,16,2048]{2,1,0:T(8,128)S(1)} async-done(((f32[8,16,2048]{2,1,0:T(8,128)}), f32[8,16,2048]{2,1,0:T(8,128)S(1)}, u32[]{:S(2)}, u32[]{:S(2)}) %all-to-all-start.3) | async-done | bytes 1048608 | tf_op jit(solution)/shard_map/all_to_all | solution.py:170
  (292 shorter events, 107.0 us)
Async XLA Ops:
  31.9 24.6 %all-to-all-start.4 = ((f32[64,1,128]{2,1,0:T(1,128)}), f32[64,1,128]{2,1,0:T(1,128)S(1)}, u32[]{:S(2)}, u32[]{:S(2)}) async-start(f32[64,1,128]{2,1,0:T(1,128)} %copy.75), calls=%async_computation.4 | async-start | bytes 65536 | tf_op jit(solution)/shard_map/all_to_all | solution.py:326
  43.3 27.3 %collective-permute-start.19 = (f32[128,2048]{1,0:T(8,128)}, f32[128,2048]{1,0:T(8,128)}, u32[]{:S(2)}, u32[]{:S(2)}) collective-permute-start(f32[128,2048]{1,0:T(8,128)} %get-tuple-element.81), channel_id=1, source_target_pairs={{0,2},{2,0},{1,3},{3,1},{4,6},{6,4},{5,7},{7,5},{8,10},{10,8},{9,1... | collective-permute-start | bytes 3145736 | tf_op jit(solution)/shard_map/ppermute | solution.py:20
  43.4 28.9 %collective-permute-start.14 = (f32[128,2048]{1,0:T(8,128)}, f32[128,2048]{1,0:T(8,128)}, u32[]{:S(2)}, u32[]{:S(2)}) collective-permute-start(f32[128,2048]{1,0:T(8,128)} %get-tuple-element.32), channel_id=1, source_target_pairs={{0,2},{2,0},{1,3},{3,1},{4,6},{6,4},{5,7},{7,5},{8,10},{10,8},{9,1... | collective-permute-start | bytes 3145736 | tf_op jit(solution)/shard_map/ppermute | solution.py:20
  60.2 126.9 %collective-permute-start = (f32[128,1024]{1,0:T(8,128)}, f32[128,1024]{1,0:T(8,128)}, u32[]{:S(2)}, u32[]{:S(2)}) collective-permute-start(f32[128,1024]{1,0:T(8,128)} %convolution_add_fusion), channel_id=1, source_target_pairs={{0,1},{1,0},{2,3},{3,2},{4,5},{5,4},{6,7},{7,6},{8,9},{9,8},{10,11... | collective-permute-start | bytes 1572872 | tf_op jit(solution)/shard_map/ppermute | solution.py:20
  64.4 19.8 %collective-permute-start.7 = (f32[128,1024]{1,0:T(8,128)S(1)}, f32[128,1024]{1,0:T(8,128)S(1)}, u32[]{:S(2)}, u32[]{:S(2)}) collective-permute-start(f32[128,1024]{1,0:T(8,128)S(1)} %fusion.77), channel_id=1, source_target_pairs={{0,32},{32,64},{64,96},{96,0},{1,33},{33,65},{65,97},{97,1},{2,34}... | collective-permute-start | bytes 1572872 | tf_op jit(solution)/shard_map/ppermute | solution.py:20
  66.5 18.5 %collective-permute-start.6 = (f32[128,1024]{1,0:T(8,128)S(1)}, f32[128,1024]{1,0:T(8,128)S(1)}, u32[]{:S(2)}, u32[]{:S(2)}) collective-permute-start(f32[128,1024]{1,0:T(8,128)S(1)} %fusion.74), channel_id=1, source_target_pairs={{0,96},{32,0},{64,32},{96,64},{1,97},{33,1},{65,33},{97,65},{2,98}... | collective-permute-start | bytes 1572872 | tf_op jit(solution)/shard_map/ppermute | solution.py:20
  72.3 18.4 %collective-permute-start.10 = (f32[128,1024]{1,0:T(8,128)S(1)}, f32[128,1024]{1,0:T(8,128)S(1)}, u32[]{:S(2)}, u32[]{:S(2)}) collective-permute-start(f32[128,1024]{1,0:T(8,128)S(1)} %fusion.118), channel_id=1, source_target_pairs={{0,24},{8,0},{16,8},{24,16},{1,25},{9,1},{17,9},{25,17},{2,26},{10... | collective-permute-start | bytes 1572872 | tf_op jit(solution)/shard_map/ppermute | solution.py:20
  84.2 29.4 %collective-permute-start.16 = (f32[128,1024]{1,0:T(8,128)}, f32[128,1024]{1,0:T(8,128)}, u32[]{:S(2)}, u32[]{:S(2)}) collective-permute-start(f32[128,1024]{1,0:T(8,128)} %fusion.108), channel_id=1, source_target_pairs={{0,32},{32,64},{64,96},{96,0},{1,33},{33,65},{65,97},{97,1},{2,34}... | collective-permute-start | bytes 1572872 | tf_op jit(solution)/shard_map/ppermute | solution.py:20
  85.0 17.8 %collective-permute-start.8 = (f32[64,1024]{1,0:T(8,128)S(1)}, f32[64,1024]{1,0:T(8,128)S(1)}, u32[]{:S(2)}, u32[]{:S(2)}) collective-permute-start(f32[64,1024]{1,0:T(8,128)S(1)} %slice_add_fusion.11), channel_id=1, source_target_pairs={{0,32},{32,64},{64,96},{96,0},{1,33},{33,65},{65,97},{97,1},{2,34}... | collective-permute-start | bytes 786440 | tf_op jit(solution)/shard_map/ppermute | solution.py:20
  90.7 26.2 %collective-permute-start.15 = (f32[128,1024]{1,0:T(8,128)}, f32[128,1024]{1,0:T(8,128)}, u32[]{:S(2)}, u32[]{:S(2)}) collective-permute-start(f32[128,1024]{1,0:T(8,128)} %fusion.110), channel_id=1, source_target_pairs={{0,96},{32,0},{64,32},{96,64},{1,97},{33,1},{65,33},{97,65},{2,98}... | collective-permute-start | bytes 1572872 | tf_op jit(solution)/shard_map/ppermute | solution.py:20
  102.8 18.6 %collective-permute-start.20 = (f32[128,1024]{1,0:T(8,128)}, f32[128,1024]{1,0:T(8,128)}, u32[]{:S(2)}, u32[]{:S(2)}) collective-permute-start(f32[128,1024]{1,0:T(8,128)} %fusion.102), channel_id=1, source_target_pairs={{0,96},{32,0},{64,32},{96,64},{1,97},{33,1},{65,33},{97,65},{2,98}... | collective-permute-start | bytes 1572872 | tf_op jit(solution)/shard_map/ppermute | solution.py:20
  107.4 62.1 %all-to-all-start = ((f32[8,16,1024]{2,1,0:T(8,128)}), f32[8,16,1024]{2,1,0:T(8,128)}, u32[]{:S(2)}, u32[]{:S(2)}) async-start(f32[8,16,1024]{2,1,0:T(8,128)} %bitcast.136), calls=%async_computation | async-start | bytes 1048576 | tf_op jit(solution)/shard_map/all_to_all | solution.py:170
  113.6 20.5 %collective-permute-start.25 = (f32[128,1024]{1,0:T(8,128)}, f32[128,1024]{1,0:T(8,128)S(1)}, u32[]{:S(2)}, u32[]{:S(2)}) collective-permute-start(f32[128,1024]{1,0:T(8,128)} %fusion.92), channel_id=1, source_target_pairs={{0,8},{8,16},{16,24},{24,0},{1,9},{9,17},{17,25},{25,1},{2,10},{10... | collective-permute-start | bytes 1572872 | tf_op jit(solution)/shard_map/ppermute | solution.py:20
  116.9 19.1 %collective-permute-start.24 = (f32[128,1024]{1,0:T(8,128)}, f32[128,1024]{1,0:T(8,128)S(1)}, u32[]{:S(2)}, u32[]{:S(2)}) collective-permute-start(f32[128,1024]{1,0:T(8,128)} %fusion.94), channel_id=1, source_target_pairs={{0,24},{8,0},{16,8},{24,16},{1,25},{9,1},{17,9},{25,17},{2,26},{10... | collective-permute-start | bytes 1572872 | tf_op jit(solution)/shard_map/ppermute | solution.py:20
  119.5 25.1 %collective-permute-start.29 = (f32[128,1024]{1,0:T(8,128)}, f32[128,1024]{1,0:T(8,128)S(1)}, u32[]{:S(2)}, u32[]{:S(2)}) collective-permute-start(f32[128,1024]{1,0:T(8,128)} %fusion.84), channel_id=1, source_target_pairs={{0,8},{8,16},{16,24},{24,0},{1,9},{9,17},{17,25},{25,1},{2,10},{10... | collective-permute-start | bytes 1572872 | tf_op jit(solution)/shard_map/ppermute | solution.py:20
  121.5 24.8 %collective-permute-start.28 = (f32[128,1024]{1,0:T(8,128)S(1)}, f32[128,1024]{1,0:T(8,128)S(1)}, u32[]{:S(2)}, u32[]{:S(2)}) collective-permute-start(f32[128,1024]{1,0:T(8,128)S(1)} %copy-done.26), channel_id=1, source_target_pairs={{0,24},{8,0},{16,8},{24,16},{1,25},{9,1},{17,9},{25,17},{2,26},{10... | collective-permute-start | bytes 1572872 | tf_op jit(solution)/shard_map/ppermute | solution.py:20
  134.1 17.1 %collective-permute-start.12 = (f32[64,1024]{1,0:T(8,128)S(1)}, f32[64,1024]{1,0:T(8,128)S(1)}, u32[]{:S(2)}, u32[]{:S(2)}) collective-permute-start(f32[64,1024]{1,0:T(8,128)S(1)} %copy-done.30), channel_id=1, source_target_pairs={{0,8},{8,16},{16,24},{24,0},{1,9},{9,17},{17,25},{25,1},{2,10},{10... | collective-permute-start | bytes 786440 | tf_op jit(solution)/shard_map/ppermute | solution.py:20
  161.1 29.1 %collective-permute-start.26 = (f32[64,1024]{1,0:T(8,128)}, f32[64,1024]{1,0:T(8,128)}, u32[]{:S(2)}, u32[]{:S(2)}) collective-permute-start(f32[64,1024]{1,0:T(8,128)} %slice_add_fusion.3), channel_id=1, source_target_pairs={{0,8},{8,16},{16,24},{24,0},{1,9},{9,17},{17,25},{25,1},{2,10},{10... | collective-permute-start | bytes 786440 | tf_op jit(solution)/shard_map/ppermute | solution.py:20
  161.1 29.1 %collective-permute-start.27 = (f32[64,1024]{1,0:T(8,128)}, f32[64,1024]{1,0:T(8,128)}, u32[]{:S(2)}, u32[]{:S(2)}) collective-permute-start(f32[64,1024]{1,0:T(8,128)} %slice_add_fusion.2), channel_id=1, source_target_pairs={{0,24},{8,0},{16,8},{24,16},{1,25},{9,1},{17,9},{25,17},{2,26},{10... | collective-permute-start | bytes 786440 | tf_op jit(solution)/shard_map/ppermute | solution.py:20
  166.2 25.3 %collective-permute-start.30 = (f32[64,1024]{1,0:T(8,128)}, f32[64,1024]{1,0:T(8,128)}, u32[]{:S(2)}, u32[]{:S(2)}) collective-permute-start(f32[64,1024]{1,0:T(8,128)} %slice_add_fusion.1), channel_id=1, source_target_pairs={{0,8},{8,16},{16,24},{24,0},{1,9},{9,17},{17,25},{25,1},{2,10},{10... | collective-permute-start | bytes 786440 | tf_op jit(solution)/shard_map/ppermute | solution.py:20
  166.2 25.3 %collective-permute-start.31 = (f32[64,1024]{1,0:T(8,128)}, f32[64,1024]{1,0:T(8,128)}, u32[]{:S(2)}, u32[]{:S(2)}) collective-permute-start(f32[64,1024]{1,0:T(8,128)} %slice_add_fusion), channel_id=1, source_target_pairs={{0,24},{8,0},{16,8},{24,16},{1,25},{9,1},{17,9},{25,17},{2,26},{10... | collective-permute-start | bytes 786440 | tf_op jit(solution)/shard_map/ppermute | solution.py:20
  183.6 20.0 %all-to-all-start.2 = ((f32[8,16,2048]{2,1,0:T(8,128)}), f32[8,16,2048]{2,1,0:T(8,128)S(1)}, u32[]{:S(2)}, u32[]{:S(2)}) async-start(f32[8,16,2048]{2,1,0:T(8,128)} %bitcast.34), calls=%async_computation.2 | async-start | bytes 2097152 | tf_op jit(solution)/shard_map/all_to_all | solution.py:170
  189.8 20.2 %collective-permute-start.1 = (f32[128,1024]{1,0:T(8,128)}, f32[128,1024]{1,0:T(8,128)}, u32[]{:S(2)}, u32[]{:S(2)}) collective-permute-start(f32[128,1024]{1,0:T(8,128)} %get-tuple-element.47), channel_id=1, source_target_pairs={{0,1},{1,0},{2,3},{3,2},{4,5},{5,4},{6,7},{7,6},{8,9},{9,8},{10,11... | collective-permute-start | bytes 1572872 | tf_op jit(solution)/shard_map/ppermute | solution.py:20
  203.6 18.4 %all-to-all-start.3 = ((f32[8,16,2048]{2,1,0:T(8,128)}), f32[8,16,2048]{2,1,0:T(8,128)S(1)}, u32[]{:S(2)}, u32[]{:S(2)}) async-start(f32[8,16,2048]{2,1,0:T(8,128)} %bitcast.35), calls=%async_computation.3 | async-start | bytes 2097152 | tf_op jit(solution)/shard_map/all_to_all | solution.py:170
  (55 other events, 584.6 us)

commit v2 on v1

v2 whole, which is shorter than its diff:
```python
import functools

import jax
import jax.numpy as jnp
from jax import lax
from jax.experimental import pallas as pl
from jax.experimental.pallas import tpu as pltpu
from jax.sharding import Mesh
from jax.sharding import PartitionSpec as P

HEAD_DIM = 64
ROTARY = 16
DP = ("dp_0", "dp_1", "dp_2", "dp_3")
X, Y, ZH, CORE = DP
TENSOR = "tensor"

epsilon = 1e-05

CONTRACT_COLS = (((1,), (1,)), ((), ()))


def shift(array, axis, step):
    size = lax.axis_size(axis)
    return lax.ppermute(array, axis, [(i, (i + step) % size) for i in range(size)])


def layout_rows(lengths, owner_group, row_offset, row_index, group_rows):
    first_row = owner_group * group_rows + row_offset
    inside = (row_index[:, None] >= first_row[None, :]) & (
        row_index[:, None] < (first_row + lengths)[None, :]
    )
    number = jnp.arange(lengths.shape[0], dtype=jnp.int32) + 1
    segment = jnp.sum(jnp.where(inside, number[None, :], 0), axis=1) - 1
    position = jnp.sum(jnp.where(inside, row_index[:, None] - first_row[None, :], 0), axis=1)
    return (segment, position)


def rotary_tables(position):
    lane = jnp.arange(2 * HEAD_DIM, dtype=jnp.int32) % HEAD_DIM
    half_rot = ROTARY // 2
    frequency = 1.0 / 10000.0 ** ((lane % half_rot).astype(jnp.float32) * 2.0 / ROTARY)
    angles = position.astype(jnp.float32)[:, None] * frequency[None, :]
    turned = (lane < ROTARY)[None, :]
    sign = jnp.where(lane < half_rot, -1.0, 1.0)[None, :]
    return (jnp.where(turned, jnp.cos(angles), 1.0), jnp.where(turned, jnp.sin(angles) * sign, 0.0))


def unit(hidden):
    row_mean = jnp.mean(hidden, axis=-1, keepdims=True)
    centred = hidden - row_mean
    inv_scale = lax.rsqrt(jnp.mean(centred * centred, axis=-1, keepdims=True) + epsilon)
    return (centred * inv_scale, inv_scale)


def normalize_back(grad_rows, unit_rows, inv_scale, gain_row):
    scaled = grad_rows * gain_row
    return inv_scale * (
        scaled
        - jnp.mean(scaled, axis=-1, keepdims=True)
        - unit_rows * jnp.mean(scaled * unit_rows, axis=-1, keepdims=True)
    )


def gelu_exact(values):
    return 0.5 * values * (1.0 + lax.erf(values * 0.7071067811865476))


def gelu_slope(values):
    return (
        0.5 * (1.0 + lax.erf(values * 0.7071067811865476))
        + values * jnp.exp(-0.5 * values * values) * 0.3989422804014327
    )


def attention_kernel(
    projected, context_grad, segment_column, segment_row, cosine, sine, context, grad_wide, grad, turned, raw
):
    rows, cols = projected.shape
    heads = cols // (3 * HEAD_DIM)
    lane = lax.broadcasted_iota(jnp.int32, (rows, 128), 1)
    entry = lane % HEAD_DIM
    scale = HEAD_DIM ** (-0.5)
    tables = []
    for kind in range(3):
        halves = [(2 * kind + side) % 3 for side in range(2)]
        cos_t, sin_t = cosine[...], sine[...]
        low = lane < HEAD_DIM
        for side, what in enumerate(halves):
            here = low if side == 0 else jnp.logical_not(low)
            if what == 0:
                cos_t = jnp.where(here, cos_t * scale, cos_t)
                sin_t = jnp.where(here, sin_t * scale, sin_t)
            if what == 2:
                cos_t = jnp.where(here, 1.0, cos_t)
                sin_t = jnp.where(here, 0.0, sin_t)
        tables.append((cos_t, sin_t))

    def swapped(part):
        up = pltpu.roll(part, 128 - ROTARY // 2, 1)
        down = pltpu.roll(part, ROTARY // 2, 1)
        return jnp.where(entry < ROTARY // 2, up, down)

    for chunk in range(cols // 128):
        at = slice(128 * chunk, 128 * (chunk + 1))
        part = projected[:, at]
        cos_t, sin_t = tables[chunk % 3]
        turned[:, at] = (part * cos_t + swapped(part) * sin_t).astype(jnp.bfloat16)

    allowed = (segment_column[...] == segment_row[...]) & (
        lax.broadcasted_iota(jnp.int32, (rows, rows), 1)
        <= lax.broadcasted_iota(jnp.int32, (rows, rows), 0)
    )

    def product(left, right, dims):
        return lax.dot_general(left, right, (dims, ((), ())), preferred_element_type=jnp.float32)

    for head in range(heads):
        base = 3 * HEAD_DIM * head
        query = turned[:, base : base + HEAD_DIM]
        key = turned[:, base + HEAD_DIM : base + 2 * HEAD_DIM]
        value = turned[:, base + 2 * HEAD_DIM : base + 3 * HEAD_DIM]
        at = slice(HEAD_DIM * head, HEAD_DIM * (head + 1))
        out_grad = context_grad[:, at].astype(jnp.bfloat16)
        scores = jnp.where(allowed, product(query, key, ((1,), (1,))), -1e30)
        highest = jnp.max(scores, axis=-1, keepdims=True)
        weights = jnp.where(allowed, jnp.exp(scores - highest), 0.0)
        probs = weights / jnp.sum(weights, axis=-1, keepdims=True)
        probs_low = probs.astype(jnp.bfloat16)
        out = product(probs_low, value, ((1,), (0,))).astype(jnp.bfloat16)
        context[:, at] = out
        offset = jnp.sum(
            out_grad.astype(jnp.float32) * out.astype(jnp.float32), axis=-1, keepdims=True
        )
        probs_grad = product(out_grad, value, ((1,), (1,)))
        score_grad = (probs * (probs_grad - offset)).astype(jnp.bfloat16)
        raw[:, base : base + HEAD_DIM] = product(score_grad, key, ((1,), (0,)))
        raw[:, base + HEAD_DIM : base + 2 * HEAD_DIM] = product(score_grad, query, ((0,), (0,)))
        raw[:, base + 2 * HEAD_DIM : base + 3 * HEAD_DIM] = product(
            probs_low, out_grad, ((0,), (0,))
        )

    for chunk in range(cols // 128):
        at = slice(128 * chunk, 128 * (chunk + 1))
        part = raw[:, at]
        cos_t, sin_t = tables[chunk % 3]
        back = part * cos_t - swapped(part) * sin_t
        grad_wide[:, at] = back
        grad[:, at] = back.astype(jnp.bfloat16)


def attention(projected, context_grad, segment, cosine, sine):
    rows, cols = projected.shape
    return pl.pallas_call(
        attention_kernel,
        out_shape=(
            jax.ShapeDtypeStruct(context_grad.shape, jnp.bfloat16),
            jax.ShapeDtypeStruct((rows, cols), jnp.float32),
            jax.ShapeDtypeStruct((rows, cols), jnp.bfloat16),
        ),
        scratch_shapes=[
            pltpu.VMEM((rows, cols), jnp.bfloat16),
            pltpu.VMEM((rows, cols), jnp.float32),
        ],
        name="attention",
    )(projected, context_grad, segment[:, None], segment[None, :], cosine, sine)


def product_kernel(count, *refs):
    ins, (to_next, to_last, rest) = refs[: 3 * count], refs[3 * count :]
    column = 0
    for i in range(count):
        left, own, near = ins[3 * i : 3 * i + 3]
        right = jnp.concatenate([own[...], near[...].astype(jnp.bfloat16)], axis=0)
        cols = slice(column, column + own.shape[1])
        column += own.shape[1]
        eighth = left.shape[0] // 8
        targets = (
            (rest, 0), (to_next, 0), (to_next, 1), (to_last, 0), (to_last, 1), (rest, 1), (rest, 2), (rest, 3),
        )
        for block, (out, place) in enumerate(targets):
            out[place * eighth : (place + 1) * eighth, cols] = jnp.dot(
                left[block * eighth : (block + 1) * eighth, :],
                right,
                preferred_element_type=jnp.float32,
            )


def products(*groups):
    rows = groups[0][0].shape[0]
    cols = sum(own.shape[1] for _, own, _ in groups)
    sizes = (rows // 4, rows // 4, rows // 2)
    return pl.pallas_call(
        functools.partial(product_kernel, len(groups)),
        out_shape=tuple(jax.ShapeDtypeStruct((size, cols), jnp.float32) for size in sizes),
        name="products",
    )(*(array for group in groups for array in group))


def moves():
    def along(first, step):
        pairs = []
        for index in range(64):
            x, y, rest, core = index // 16, index // 4 % 4, index % 4, index % 2
            if (core == 0) == first:
                x = (x + step) % 4
            else:
                y = (y + step) % 4
            pairs.append((index, x * 16 + y * 4 + rest))
        return pairs

    return {(first, step): along(first, step) for first in (True, False) for step in (1, -1)}


MOVES = moves()


def ring(array, first, step):
    return lax.ppermute(array, DP, MOVES[first, step])


def tie(values, *others):
    return lax.optimization_barrier((values, *others))[0]


def selection(width):
    ix, iy, iz, core = (lax.axis_index(axis) for axis in DP)
    row = jnp.arange(width, dtype=jnp.int32)
    block = width // 64
    inner = row % block
    at_core = core ^ (1 - row // block % 2)
    at_z = iz ^ (1 - row // (2 * block) % 2)
    second = row // (4 * block) % 4 + 1
    first = row // (16 * block) + 1
    at_x = (ix + jnp.where(core == 0, first, second)) % 4
    at_y = (iy + jnp.where(core == 0, second, first)) % 4
    feature = (((at_x * 4 + at_y) * 2 + at_z) * 2 + at_core) * block + inner
    column = jnp.arange(width, dtype=jnp.int32)
    return (feature[:, None] == column[None, :]).astype(jnp.bfloat16)


def pick(chosen, rows):
    return lax.dot_general(
        chosen, rows, CONTRACT_COLS, preferred_element_type=jnp.float32
    ).astype(jnp.bfloat16)


def shards(
    block_input,
    cotangent,
    qkv_weight,
    dense_weight,
    up_weight,
    down_weight,
    up_bias,
    down_bias,
    norm_gain,
    norm_bias,
    lengths,
    owner_group,
    row_offset,
):
    row_count, model_width = block_input.shape
    qkv_weight, dense_weight = qkv_weight[0], dense_weight[0]
    up_weight, down_weight = up_weight[0], down_weight[0]
    norm_gain, norm_bias = norm_gain[0], norm_bias[0]
    hidden_cols = up_weight.shape[1]
    table_rows = hidden_cols // model_width

    group = lax.axis_index(DP)
    core = lax.axis_index(CORE)
    hidden = block_input.astype(jnp.float32)
    grad_rows = cotangent.astype(jnp.float32)
    near_hidden = shift(hidden, CORE, 1)
    near_grad = shift(grad_rows, CORE, 1)
    own_index = group * row_count + jnp.arange(row_count, dtype=jnp.int32)
    near_index = (group ^ 1) * row_count + jnp.arange(row_count, dtype=jnp.int32)
    segment, position = layout_rows(lengths, owner_group, row_offset, own_index, row_count)
    near_segment, _ = layout_rows(lengths, owner_group, row_offset, near_index, row_count)
    valid_rows = (segment >= 0).astype(jnp.float32)[:, None]
    near_valid = (near_segment >= 0).astype(jnp.float32)[:, None]
    cosine_table, sine_table = rotary_tables(position)

    unit_rows, inv_scale = unit(hidden)
    heads_in = (unit_rows * norm_gain[0] + norm_bias[0]).astype(jnp.bfloat16)
    units_in = (unit_rows * norm_gain[1] + norm_bias[1]).astype(jnp.bfloat16)
    branch_grad = grad_rows * valid_rows
    branch_in = branch_grad.astype(jnp.bfloat16)

    near_unit, _ = unit(near_hidden)
    near_heads_in = (near_unit * norm_gain[0] + norm_bias[0]).astype(jnp.bfloat16)
    near_units_in = (near_unit * norm_gain[1] + norm_bias[1]).astype(jnp.bfloat16)
    near_branch_in = (near_grad * near_valid).astype(jnp.bfloat16)

    chosen = selection(model_width)

    def mine_theirs(rows):
        width = rows.shape[1] // 2
        low, high = rows[:, :width], rows[:, width:]
        return jnp.where(core == 0, low, high), jnp.where(core == 0, high, low)

    hidden_pre = jnp.dot(units_in, up_weight, preferred_element_type=jnp.float32) + up_bias
    activated_wide = gelu_exact(hidden_pre)
    activated = activated_wide.astype(jnp.bfloat16)
    mine, theirs = mine_theirs(activated_wide)
    near_activated = shift(theirs, CORE, 1)
    branch_left = pick(chosen, jnp.concatenate([branch_in, near_branch_in], axis=0))
    next_a, last_a, rest_a = products((branch_left, mine.astype(jnp.bfloat16), near_activated))
    minus_a, plus_a = ring(next_a, True, 1), ring(last_a, True, -1)

    pre_grad = jnp.dot(branch_in, down_weight, preferred_element_type=jnp.float32) * gelu_slope(
        hidden_pre
    )
    pre_in = pre_grad.astype(jnp.bfloat16)
    mine, theirs = mine_theirs(pre_grad)
    near_pre = shift(theirs, CORE, 1)
    units_left = pick(chosen, jnp.concatenate([units_in, near_units_in], axis=0))
    next_b, last_b, rest_b = products((units_left, mine.astype(jnp.bfloat16), near_pre))
    minus_b, plus_b = ring(next_b, True, 1), ring(last_b, True, -1)

    def middle(rest, minus, plus):
        half = rest.shape[0] // 4
        low = ring(rest[:half] + minus[half:], True, 1)
        high = ring(rest[half : 2 * half] + plus[:half], True, -1)
        return low, high

    def finish(rest, minus, plus, low, high):
        half = rest.shape[0] // 4
        return (
            rest[2 * half :]
            + jnp.concatenate([plus[half:], minus[:half]], axis=0)
            + jnp.concatenate([low, high], axis=0)
        )

    heads_in = tie(heads_in, next_b, last_b)
    projected = jnp.dot(heads_in, qkv_weight, preferred_element_type=jnp.float32)
    context_grad = jnp.dot(branch_in, dense_weight, preferred_element_type=jnp.float32)
    projected = tie(projected, minus_a, plus_a)
    low_a, high_a = middle(rest_a, minus_a, plus_a)
    context, projected_wide, projected_grad = attention(
        projected, context_grad, segment, cosine_table, sine_table
    )
    mine_c, theirs_c = mine_theirs(context.astype(jnp.float32))
    mine_q, theirs_q = mine_theirs(projected_wide)
    near_right = shift(jnp.concatenate([theirs_c, theirs_q], axis=1), CORE, 1)
    split = mine_c.shape[1]
    heads_left = pick(chosen, jnp.concatenate([heads_in, near_heads_in], axis=0))
    next_c, last_c, rest_c = products(
        (branch_left, mine_c.astype(jnp.bfloat16), near_right[:, :split]),
        (heads_left, mine_q.astype(jnp.bfloat16), near_right[:, split:]),
    )
    low_b, high_b = middle(rest_b, minus_b, plus_b)
    minus_c, plus_c = ring(next_c, True, 1), ring(last_c, True, -1)

    activated = tie(activated, next_c, last_c, minus_b, plus_b)
    partial_rows = lax.dot_general(
        context, dense_weight, CONTRACT_COLS, preferred_element_type=jnp.float32
    ) + lax.dot_general(
        activated, down_weight, CONTRACT_COLS, preferred_element_type=jnp.float32
    )
    branch = partial_rows + shift(partial_rows, TENSOR, 1)
    output = hidden + valid_rows * (branch + down_bias)

    projected_grad = tie(projected_grad, next_c, last_c, low_a, high_a)
    heads_grad = lax.dot_general(
        projected_grad, qkv_weight, CONTRACT_COLS, preferred_element_type=jnp.float32
    )
    units_grad = lax.dot_general(
        pre_in, up_weight, CONTRACT_COLS, preferred_element_type=jnp.float32
    )
    local_back = normalize_back(
        heads_grad, unit_rows, inv_scale, norm_gain[0]
    ) + normalize_back(units_grad, unit_rows, inv_scale, norm_gain[1])

    small = jnp.concatenate(
        [
            jnp.sum(heads_grad * unit_rows, axis=0)[None],
            jnp.sum(units_grad * unit_rows, axis=0)[None],
            jnp.sum(heads_grad, axis=0)[None],
            jnp.sum(units_grad, axis=0)[None],
            jnp.sum(branch_grad, axis=0)[None],
            jnp.sum(pre_grad, axis=0).reshape(table_rows, model_width),
        ],
        axis=0,
    )
    small = jnp.pad(small, ((0, 8 - small.shape[0]), (0, 0)))
    near_back = shift(jnp.concatenate([local_back, small], axis=0), TENSOR, 1)
    input_grad = grad_rows + (local_back + near_back[:row_count])
    summed = jnp.arange(8)[:, None] < 4
    small = small + jnp.where(summed, near_back[row_count:], 0.0)
    minus, plus = ring(small, True, 1), ring(small, True, -1)
    small = small + (minus + plus) + ring(minus, True, 1)

    def second(rows, extra):
        quarter = rows.shape[0] // 4
        half = quarter // 2
        count = extra.shape[0]
        minus = ring(jnp.concatenate([rows[half : 3 * half], extra]), False, 1)
        plus = ring(jnp.concatenate([rows[3 * half : 5 * half], extra]), False, -1)
        low = ring(
            jnp.concatenate([rows[:half] + minus[half:quarter], minus[quarter:]]), False, 1
        )
        high = ring(rows[5 * half : 6 * half] + plus[:half], False, -1)
        rows = (
            rows[6 * half :]
            + jnp.concatenate([plus[half:quarter], minus[:half]], axis=0)
            + jnp.concatenate([low[:half], high], axis=0)
        )
        extra = extra + (minus[quarter:] + plus[quarter:]) + low[half:]
        other = shift(jnp.concatenate([rows[:half], extra]), ZH, 1)
        return rows[half:] + other[:half], extra + other[half:]

    none = jnp.zeros((0, 2 * model_width), jnp.float32)
    sum_a = finish(rest_a, minus_a, plus_a, low_a, high_a)
    sum_b = finish(rest_b, minus_b, plus_b, low_b, high_b)
    early, _ = second(jnp.concatenate([sum_a, sum_b], axis=1), none)
    low_c, high_c = middle(rest_c, minus_c, plus_c)
    sum_c = finish(rest_c, minus_c, plus_c, low_c, high_c)
    late, small = second(sum_c, small)

    keep = early.shape[0] // 2
    near_early = shift(early[:keep], CORE, 1)
    near_late = shift(jnp.concatenate([late[:keep], small]), CORE, 1)
    small = small + near_late[keep:]

    def joined(own, near):
        return jnp.concatenate(
            [jnp.where(core == 0, own, near), jnp.where(core == 0, near, own)], axis=1
        )

    column = hidden_cols // 2
    down_grad = joined(early[keep:, :column], near_early[:, :column])
    up_grad = joined(early[keep:, column:], near_early[:, column:])
    dense_grad = joined(late[keep:, :split], near_late[:keep, :split])
    qkv_grad = joined(late[keep:, split:], near_late[:keep, split:])
    block = model_width // lax.axis_size(DP)
    small = lax.dynamic_slice_in_dim(small, group * block, block, axis=1)
    return (
        output,
        input_grad,
        qkv_grad[None],
        dense_grad[None],
        up_grad[None],
        down_grad[None],
        small[5 : 5 + table_rows][None],
        small[4][None],
        small[:2][None],
        small[2:4][None],
    )


def solution(mesh):
    split = Mesh(
        mesh.devices.reshape(4, 4, 2, 2, mesh.shape["tensor"]),
        (*DP, TENSOR),
    )
    in_specs = (
        P(DP, None),
        P(DP, None),
        P(None, None, "tensor"),
        P(None, None, "tensor"),
        P(None, None, "tensor"),
        P(None, None, "tensor"),
        P(None, "tensor"),
        P(),
        P(),
        P(),
        P(),
        P(),
        P(),
    )
    out_specs = (
        P(DP, None),
        P(DP, None),
        P(None, DP, "tensor"),
        P(None, DP, "tensor"),
        P(None, DP, "tensor"),
        P(None, DP, "tensor"),
        P(None, "tensor", DP),
        P(None, DP),
        P(None, None, DP),
        P(None, None, DP),
    )
    return jax.shard_map(
        shards, mesh=split, in_specs=in_specs, out_specs=out_specs, check_vma=False
    )
```

time: 226 us -> 177 us (0.78)
  starting transfers between devices: 74.5 us -> 45 us
  matrix products: 56.5 us -> 27.9 us
  Pallas kernels: 0 us -> 20 us
  other arithmetic: 26.4 us -> 40.8 us
  local copies, waits for them, and re-layouts: 19.2 us -> 6.83 us
  waiting for transfers between devices: 44.9 us -> 32.7 us
    dot_general x37 -> x1, matrix products: 39.5 us -> 2.63 us  [shards(): lax.dot_general(context, dense_weight, CONTRACT_COLS, preferred_element_t...]
    ppermute x0 -> x23, starting transfers between devices: none -> 32.6 us  [ring(): return lax.ppermute(array, DP, MOVES[first, step])]
    all_to_all x5 -> x0, starting transfers between devices: 31.8 us -> none  [the longest x4 20.4 us: spread_sum(): parts = lax.all_to_all(parts, axes, split_axis=0, concat_axis=0, tiled=True)]
    ppermute x33 -> x11, starting transfers between devices: 42.7 us -> 12.4 us  [shift(): lax.ppermute(array, axis, [(i, (i + step) % size) for i in range(size)])]
    all_to_all x5 -> x0, waiting for transfers between devices: 22.2 us -> none  [the longest x4 22.2 us: spread_sum(): parts = lax.all_to_all(parts, axes, split_axis=0, concat_axis=0, tiled=True)]
    pallas_call x0 -> x4, Pallas kernels: none -> 20 us  [the longest x3 11.2 us: products(): pl.pallas_call(functools.partial(product_kernel, len(groups)), out_shape=...]
    ppermute x0 -> x23, waiting for transfers between devices: none -> 19.7 us  [ring(): return lax.ppermute(array, DP, MOVES[first, step])]
    add x6 -> x21, other arithmetic: 2.28 us -> 14.1 us  [the longest x2 5.23 us: middle(): low = ring(rest[:half] + minus[half:], True, 1)]
  transfers between devices with their start and end apart: 38 -> 34, of which waited for: 7 -> 12; matrix products, arithmetic and copies ran while one was open for 36% -> 38% of each run, Pallas kernels for 0% -> 11%
where the time goes in v2:
time: 177 us; the launch traced here: 175 us
  starting transfers between devices  45 us (25%)
  other arithmetic  40.8 us (23%)
  waiting for transfers between devices  32.7 us (18%)
  matrix products  27.9 us (16%)
  Pallas kernels  20 us (11%)
  local copies, waits for them, and re-layouts  6.83 us (4%)
    ppermute x23, starting transfers between devices, ring(): return lax.ppermute(array, DP, MOVES[first, step])  32.6 us
    ppermute x23, waiting for transfers between devices, ring(): return lax.ppermute(array, DP, MOVES[first, step])  19.7 us
    ppermute x11, waiting for transfers between devices, shift(): lax.ppermute(array, axis, [(i, (i + step) % size) for i in range(size)])  13 us
    ppermute x11, starting transfers between devices, shift(): lax.ppermute(array, axis, [(i, (i + step) % size) for i in range(size)])  12.4 us
    pallas_call x3, Pallas kernels, products(): pl.pallas_call(functools.partial(product_kernel, len(groups)), out_shape=...  11.2 us
    pallas_call x1, Pallas kernels, attention(): pl.pallas_call(attention_kernel, out_shape=(jax.ShapeDtypeStruct(context_...  8.81 us
    dot_general x3, matrix products, pick(): lax.dot_general(chosen, rows, CONTRACT_COLS, preferred_element_type=jnp.f...  5.95 us
    add x2, other arithmetic, middle(): low = ring(rest[:half] + minus[half:], True, 1)  5.23 us
  transfers between devices with their start and end apart: 34, of which 12 were waited for; matrix products, arithmetic and copies ran while one was open for 38% of the time, Pallas kernels for 11%

profile of v2, /device:TPU:0, one launch (start us, length us, event | category | flops | bytes accessed | tf_op | source)
XLA Modules:
  0.0 174.6 jit_solution(15645346731625742814)
XLA Ops:
  20.7 4.0 %fusion.109 = (bf16[128,2048]{1,0:T(8,128)(2,1)}, f32[128,2048]{1,0:T(8,128)S(1)}, f32[128,2048]{1,0:T(8,128)S(1)}) fusion(f32[2048]{0:T(1024)S(1)} %bitcast.77, bf16[128,1024]{1,0:T(8,128)(2,1)S(1)} %get-tuple-element.91, bf16[1,1024,2048]{2,1,0:T(8,128)(2,1)} %param.17), kind=kOutput, calls=%fused_computation.244 | convolution fusion | flops 538443776 | bytes 7086080 | tf_op jit(solution)/shard_map/dot_general | solution.py:301
  31.8 3.7 %products.4 = (f32[256,1024]{1,0:T(8,128)}, f32[256,1024]{1,0:T(8,128)}, f32[512,1024]{1,0:T(8,128)}) custom-call(bf16[1024,256]{1,0:T(8,128)(2,1)} %fusion.25.refs_0_, bf16[128,1024]{1,0:T(8,128)(2,1)} %select_convert_fusion.refs_1_, f32[128,1024]{1,0:T(8,128)} %collective-permute-done.3.refs_2_), custom_call_target="tpu_custom_call" | custom-call | tf_op jit(solution)/shard_map/products/pallas_call | solution.py:192
  38.7 2.7 %fusion.24.refs_0_ = bf16[1024,256]{1,0:T(8,128)(2,1)} fusion(s32[1024]{0:T(1024)S(1)} %fusion.81, bf16[128,1024]{1,0:T(8,128)(2,1)} %get-tuple-element.103, bf16[128,1024]{1,0:T(8,128)(2,1)} %copy-done.22), kind=kOutput, calls=%fused_computation.30 | convolution fusion | flops 539230208 | bytes 1052672 | tf_op jit(solution)/shard_map/dot_general | solution.py:242
  41.4 3.6 %products.3 = (f32[256,1024]{1,0:T(8,128)}, f32[256,1024]{1,0:T(8,128)}, f32[512,1024]{1,0:T(8,128)}) custom-call(bf16[1024,256]{1,0:T(8,128)(2,1)} %fusion.24.refs_0_, bf16[128,1024]{1,0:T(8,128)(2,1)} %select_convert_fusion.1.refs_1_, f32[128,1024]{1,0:T(8,128)} %collective-permute-done.1.refs_2_), custom_call_target="tpu_custom_call" | custom-call | tf_op jit(solution)/shard_map/products/pallas_call | solution.py:192
  45.3 2.9 %collective-permute-start.8 = (f32[256,1024]{1,0:T(8,128)}, f32[256,1024]{1,0:T(8,128)}, u32[]{:S(2)}, u32[]{:S(2)}) collective-permute-start(f32[256,1024]{1,0:T(8,128)} %get-tuple-element.27), channel_id=1, source_target_pairs={{0,96},{2,26},{4,100},{6,30},{8,104},{10,2},{12,108},{14,6},{16,11... | collective-permute-start | bytes 3145736 | tf_op jit(solution)/shard_map/ppermute | solution.py:218
  48.2 4.8 %fusion = f32[128,1024]{1,0:T(8,128)} fusion(bf16[1,1024,2048]{2,1,0:T(8,128)(2,1)} %param.17, f32[128,2048]{1,0:T(8,128)} %copy-done.6), kind=kOutput, calls=%fused_computation | convolution fusion | flops 537133056 | bytes 5767168 | tf_op jit(solution)/shard_map/dot_general | solution.py:367
  56.2 8.8 %attention.1 = (bf16[128,512]{1,0:T(8,128)(2,1)}, f32[128,1536]{1,0:T(8,128)}, bf16[128,1536]{1,0:T(8,128)(2,1)}) custom-call(f32[128,1536]{1,0:T(8,128)} %fusion.13.projected, f32[128,512]{1,0:T(8,128)} %fusion.39.context_grad, s32[128,1]{1,0:T(8,128)} %copy.24.segment_column, s32[1,128]{1,0:T(1,128)} %get-tuple-element.114.segment_row, ...), custom_call_target="tpu_custom_call" | custom-call | tf_op jit(solution)/shard_map/attention/pallas_call | solution.py:153
  70.9 3.2 %collective-permute-start.27 = (f32[128,1024]{1,0:T(8,128)S(1)}, f32[128,1024]{1,0:T(8,128)S(1)}, u32[]{:S(2)}, u32[]{:S(2)}) collective-permute-start(f32[128,1024]{1,0:T(8,128)S(1)} %get-tuple-element.66), channel_id=1, source_target_pairs={{0,96},{2,26},{4,100},{6,30},{8,104},{10,2},{12,108},{14,6},{16,11... | collective-permute-start | bytes 1572872 | tf_op jit(solution)/shard_map/ppermute | solution.py:218
  81.6 4.8 %collective-permute-done.11 = f32[128,1024]{1,0:T(8,128)S(1)} collective-permute-done((f32[128,1024]{1,0:T(8,128)S(1)}, f32[128,1024]{1,0:T(8,128)S(1)}, u32[]{:S(2)}, u32[]{:S(2)}) %collective-permute-start.11) | collective-permute-done | bytes 524320 | tf_op jit(solution)/shard_map/ppermute | solution.py:218
  88.6 3.1 %collective-permute-start.28 = (f32[64,2048]{1,0:T(8,128)}, f32[64,2048]{1,0:T(8,128)}, u32[]{:S(2)}, u32[]{:S(2)}) collective-permute-start(f32[64,2048]{1,0:T(8,128)} %get-tuple-element.63), channel_id=1, source_target_pairs={{0,24},{2,98},{4,28},{6,102},{8,0},{10,106},{12,4},{14,110},{16,8}... | collective-permute-start | bytes 1572872 | tf_op jit(solution)/shard_map/ppermute | solution.py:218
  93.2 3.9 %products.5 = (f32[256,1024]{1,0:T(8,128)}, f32[256,1024]{1,0:T(8,128)}, f32[512,1024]{1,0:T(8,128)}) custom-call(bf16[1024,256]{1,0:T(8,128)(2,1)} %fusion.25.refs_0_, bf16[128,256]{1,0:T(8,128)(2,1)} %select_convert_fusion.3.refs_1_, f32[128,256]{1,0:T(8,128)} %slice.337.refs_2_, bf16[1024,256]{1,0:T(8,128)(2,1)} %fusion.26.refs_3_, ...), custom_call_target="tpu_custom_call" | custom-call | tf_op jit(solution)/shard_map/products/pallas_call | solution.py:192
  97.7 3.0 %collective-permute-start.13 = (f32[256,1024]{1,0:T(8,128)}, f32[256,1024]{1,0:T(8,128)}, u32[]{:S(2)}, u32[]{:S(2)}) collective-permute-start(f32[256,1024]{1,0:T(8,128)} %get-tuple-element.35), channel_id=1, source_target_pairs={{0,96},{2,26},{4,100},{6,30},{8,104},{10,2},{12,108},{14,6},{16,11... | collective-permute-start | bytes 3145736 | tf_op jit(solution)/shard_map/ppermute | solution.py:218
  100.7 3.2 %multiply_reduce_fusion.1 = (f32[1024]{0:T(1024)S(1)}, f32[128]{0:T(128)S(1)}, f32[128]{0:T(128)S(1)}, f32[1024]{0:T(1024)S(1)}, f32[1024]{0:T(1024)S(1)}, /*ind...) fusion(bf16[128,1024]{1,0:T(8,128)(2,1)S(1)} %copy-done.5, f32[128]{0:T(128)S(1)} %add_rsqrt_fusion.1, ...), kind=kOutput, calls=%fused_computation.76 | convolution fusion | flops 404876800 | bytes 4877312 | tf_op jit(solution)/shard_map/dot_general | solution.py:364
  108.3 9.3 %collective-permute-done.9 = f32[128,1024]{1,0:T(8,128)} collective-permute-done((f32[128,1024]{1,0:T(8,128)}, f32[128,1024]{1,0:T(8,128)}, u32[]{:S(2)}, u32[]{:S(2)}) %collective-permute-start.9) | collective-permute-done | bytes 524320 | tf_op jit(solution)/shard_map/ppermute | solution.py:24
  117.6 2.7 %add_multiply_fusion = (f32[128,1024]{1,0:T(8,128)S(1)}, f32[128,1024]{1,0:T(8,128)}) fusion(bf16[128,1024]{1,0:T(8,128)(2,1)S(1)} %copy-done.5, f32[128,1024]{1,0:T(8,128)} %fusion, f32[128,1024]{1,0:T(8,128)} %get-tuple-element.117, f32[128]{0:T(128)S(1)} %broadcast_multiply_fusion, f32[128]{0:T(128)S(1)} %broadcast_multiply_fusion.1, ...), kind=kLoop, calls=%fused_computation.74 | loop fusion | flops 2228224 | bytes 3423744 | tf_op jit(solution)/shard_map/add | solution.py:370
  124.3 3.2 %collective-permute-start.31 = (f32[32,2048]{1,0:T(8,128)}, f32[32,2048]{1,0:T(8,128)}, u32[]{:S(2)}, u32[]{:S(2)}) collective-permute-start(f32[32,2048]{1,0:T(8,128)} %get-tuple-element.62), channel_id=1, source_target_pairs={{0,24},{2,98},{4,28},{6,102},{8,0},{10,106},{12,4},{14,110},{16,8}... | collective-permute-start | bytes 786440 | tf_op jit(solution)/shard_map/ppermute | solution.py:218
  127.6 3.0 %slice_add_fusion.3 = (f32[128,1024]{1,0:T(8,128)}, f32[128,1024]{1,0:T(8,128)}, f32[128,1024]{1,0:T(8,128)}, f32[128,1024]{1,0:T(8,128)}) fusion(f32[256,1024]{1,0:T(8,128)} %collective-permute-done.14, f32[512,1024]{1,0:T(8,128)S(1)} %copy-done.12, f32[256,1024]{1,0:T(8,128)} %collective-permute-done.13), kind=kLoop, calls=%fused_computation.59 | loop fusion | flops 262144 | bytes 5242880 | tf_op jit(solution)/shard_map/add | solution.py:322
  130.8 3.0 %collective-permute-start.16 = (f32[128,1024]{1,0:T(8,128)}, f32[128,1024]{1,0:T(8,128)}, u32[]{:S(2)}, u32[]{:S(2)}) collective-permute-start(f32[128,1024]{1,0:T(8,128)} %get-tuple-element.68), channel_id=1, source_target_pairs={{0,96},{2,26},{4,100},{6,30},{8,104},{10,2},{12,108},{14,6},{16,11... | collective-permute-start | bytes 1572872 | tf_op jit(solution)/shard_map/ppermute | solution.py:218
  134.8 3.3 %collective-permute-start.18 = (f32[8,1024]{1,0:T(8,128)S(1)}, f32[8,1024]{1,0:T(8,128)S(1)}, u32[]{:S(2)}, u32[]{:S(2)}) collective-permute-start(f32[8,1024]{1,0:T(8,128)S(1)} %fusion.64), channel_id=1, source_target_pairs={{0,96},{2,26},{4,100},{6,30},{8,104},{10,2},{12,108},{14,6},{16,11... | collective-permute-start | bytes 98312 | tf_op jit(solution)/shard_map/ppermute | solution.py:218
  138.0 3.5 %collective-permute-done.17 = f32[8,1024]{1,0:T(8,128)S(1)} collective-permute-done((f32[8,1024]{1,0:T(8,128)S(1)}, f32[8,1024]{1,0:T(8,128)S(1)}, u32[]{:S(2)}, u32[]{:S(2)}) %collective-permute-start.17) | collective-permute-done | bytes 32800 | tf_op jit(solution)/shard_map/ppermute | solution.py:218
  142.9 3.7 %collective-permute-start.32 = (f32[32,2048]{1,0:T(8,128)S(1)}, f32[32,2048]{1,0:T(8,128)S(1)}, u32[]{:S(2)}, u32[]{:S(2)}) collective-permute-start(f32[32,2048]{1,0:T(8,128)S(1)} %slice.388), channel_id=1, source_target_pairs={{0,4},{4,0},{1,5},{5,1},{2,6},{6,2},{3,7},{7,3},{8,12},{12,8},{9,1... | collective-permute-start | bytes 786440 | tf_op jit(solution)/shard_map/ppermute | solution.py:24
  152.0 3.2 %collective-permute-done.20 = f32[72,1024]{1,0:T(8,128)S(1)} collective-permute-done((f32[72,1024]{1,0:T(8,128)S(1)}, f32[72,1024]{1,0:T(8,128)S(1)}, u32[]{:S(2)}, u32[]{:S(2)}) %collective-permute-start.20) | collective-permute-done | bytes 294944 | tf_op jit(solution)/shard_map/ppermute | solution.py:218
  159.1 4.5 %collective-permute-done.22 = f32[40,1024]{1,0:T(8,128)S(1)} collective-permute-done((f32[40,1024]{1,0:T(8,128)S(1)}, f32[40,1024]{1,0:T(8,128)S(1)}, u32[]{:S(2)}, u32[]{:S(2)}) %collective-permute-start.22) | collective-permute-done | bytes 163872 | tf_op jit(solution)/shard_map/ppermute | solution.py:218
  163.7 3.7 %collective-permute-start.24 = (f32[40,1024]{1,0:T(8,128)S(1)}, f32[40,1024]{1,0:T(8,128)S(1)}, u32[]{:S(2)}, u32[]{:S(2)}) collective-permute-start(f32[40,1024]{1,0:T(8,128)S(1)} %pad_maximum_fusion.6), channel_id=1, source_target_pairs={{0,4},{4,0},{1,5},{5,1},{2,6},{6,2},{3,7},{7,3},{8,12},{12,8},{9,1... | collective-permute-start | bytes 491528 | tf_op jit(solution)/shard_map/ppermute | solution.py:24
  (209 shorter events, 78.3 us)
Async XLA Ops:
  2.6 13.4 %collective-permute-start = (f32[128,1024]{1,0:T(8,128)}, f32[128,1024]{1,0:T(8,128)}, u32[]{:S(2)}, u32[]{:S(2)}) collective-permute-start(f32[128,1024]{1,0:T(8,128)} %convert_element_type.85), channel_id=1, source_target_pairs={{0,2},{2,0},{1,3},{3,1},{4,6},{6,4},{5,7},{7,5},{8,10},{10,8},{9,1... | collective-permute-start | bytes 1572872 | tf_op jit(solution)/shard_map/ppermute | solution.py:24
  4.4 23.8 %collective-permute-start.2 = (f32[128,1024]{1,0:T(8,128)}, f32[128,1024]{1,0:T(8,128)}, u32[]{:S(2)}, u32[]{:S(2)}) collective-permute-start(f32[128,1024]{1,0:T(8,128)} %convert_element_type.91), channel_id=1, source_target_pairs={{0,2},{2,0},{1,3},{3,1},{4,6},{6,4},{5,7},{7,5},{8,10},{10,8},{9,1... | collective-permute-start | bytes 1572872 | tf_op jit(solution)/shard_map/ppermute | solution.py:24
  27.0 14.4 %collective-permute-start.1 = (f32[128,1024]{1,0:T(8,128)}, f32[128,1024]{1,0:T(8,128)}, u32[]{:S(2)}, u32[]{:S(2)}) collective-permute-start(f32[128,1024]{1,0:T(8,128)} %slice_select_fusion.1), channel_id=1, source_target_pairs={{0,2},{2,0},{1,3},{3,1},{4,6},{6,4},{5,7},{7,5},{8,10},{10,8},{9,1... | collective-permute-start | bytes 1572872 | tf_op jit(solution)/shard_map/ppermute | solution.py:24
  35.4 20.7 %collective-permute-start.4 = (f32[256,1024]{1,0:T(8,128)}, f32[256,1024]{1,0:T(8,128)}, u32[]{:S(2)}, u32[]{:S(2)}) collective-permute-start(f32[256,1024]{1,0:T(8,128)} %get-tuple-element.29), channel_id=1, source_target_pairs={{0,32},{2,10},{4,36},{6,14},{8,40},{10,18},{12,44},{14,22},{16,48}... | collective-permute-start | bytes 3145736 | tf_op jit(solution)/shard_map/ppermute | solution.py:218
  37.0 19.2 %collective-permute-start.5 = (f32[256,1024]{1,0:T(8,128)}, f32[256,1024]{1,0:T(8,128)}, u32[]{:S(2)}, u32[]{:S(2)}) collective-permute-start(f32[256,1024]{1,0:T(8,128)} %get-tuple-element.30), channel_id=1, source_target_pairs={{0,96},{2,26},{4,100},{6,30},{8,104},{10,2},{12,108},{14,6},{16,11... | collective-permute-start | bytes 3145736 | tf_op jit(solution)/shard_map/ppermute | solution.py:218
  45.0 23.6 %collective-permute-start.7 = (f32[256,1024]{1,0:T(8,128)}, f32[256,1024]{1,0:T(8,128)}, u32[]{:S(2)}, u32[]{:S(2)}) collective-permute-start(f32[256,1024]{1,0:T(8,128)} %get-tuple-element.26), channel_id=1, source_target_pairs={{0,32},{2,10},{4,36},{6,14},{8,40},{10,18},{12,44},{14,22},{16,48}... | collective-permute-start | bytes 3145736 | tf_op jit(solution)/shard_map/ppermute | solution.py:218
  45.3 23.2 %collective-permute-start.8 = (f32[256,1024]{1,0:T(8,128)}, f32[256,1024]{1,0:T(8,128)}, u32[]{:S(2)}, u32[]{:S(2)}) collective-permute-start(f32[256,1024]{1,0:T(8,128)} %get-tuple-element.27), channel_id=1, source_target_pairs={{0,96},{2,26},{4,100},{6,30},{8,104},{10,2},{12,108},{14,6},{16,11... | collective-permute-start | bytes 3145736 | tf_op jit(solution)/shard_map/ppermute | solution.py:218
  70.8 10.5 %collective-permute-start.26 = (f32[128,1024]{1,0:T(8,128)S(1)}, f32[128,1024]{1,0:T(8,128)S(1)}, u32[]{:S(2)}, u32[]{:S(2)}) collective-permute-start(f32[128,1024]{1,0:T(8,128)S(1)} %get-tuple-element.65), channel_id=1, source_target_pairs={{0,32},{2,10},{4,36},{6,14},{8,40},{10,18},{12,44},{14,22},{16,48}... | collective-permute-start | bytes 1572872 | tf_op jit(solution)/shard_map/ppermute | solution.py:218
  70.9 10.4 %collective-permute-start.27 = (f32[128,1024]{1,0:T(8,128)S(1)}, f32[128,1024]{1,0:T(8,128)S(1)}, u32[]{:S(2)}, u32[]{:S(2)}) collective-permute-start(f32[128,1024]{1,0:T(8,128)S(1)} %get-tuple-element.66), channel_id=1, source_target_pairs={{0,96},{2,26},{4,100},{6,30},{8,104},{10,2},{12,108},{14,6},{16,11... | collective-permute-start | bytes 1572872 | tf_op jit(solution)/shard_map/ppermute | solution.py:218
  76.1 10.3 %collective-permute-start.11 = (f32[128,1024]{1,0:T(8,128)S(1)}, f32[128,1024]{1,0:T(8,128)S(1)}, u32[]{:S(2)}, u32[]{:S(2)}) collective-permute-start(f32[128,1024]{1,0:T(8,128)S(1)} %get-tuple-element.69), channel_id=1, source_target_pairs={{0,96},{2,26},{4,100},{6,30},{8,104},{10,2},{12,108},{14,6},{16,11... | collective-permute-start | bytes 1572872 | tf_op jit(solution)/shard_map/ppermute | solution.py:218
  76.2 10.7 %collective-permute-start.10 = (f32[128,1024]{1,0:T(8,128)S(1)}, f32[128,1024]{1,0:T(8,128)S(1)}, u32[]{:S(2)}, u32[]{:S(2)}) collective-permute-start(f32[128,1024]{1,0:T(8,128)S(1)} %get-tuple-element.70), channel_id=1, source_target_pairs={{0,32},{2,10},{4,36},{6,14},{8,40},{10,18},{12,44},{14,22},{16,48}... | collective-permute-start | bytes 1572872 | tf_op jit(solution)/shard_map/ppermute | solution.py:218
  78.9 12.8 %collective-permute-start.6 = (f32[128,1024]{1,0:T(8,128)S(1)}, f32[128,1024]{1,0:T(8,128)S(1)}, u32[]{:S(2)}, u32[]{:S(2)}) collective-permute-start(f32[128,1024]{1,0:T(8,128)S(1)} %pad_maximum_fusion.1), channel_id=1, source_target_pairs={{0,2},{2,0},{1,3},{3,1},{4,6},{6,4},{5,7},{7,5},{8,10},{10,8},{9,1... | collective-permute-start | bytes 1572872 | tf_op jit(solution)/shard_map/ppermute | solution.py:24
  88.6 33.6 %collective-permute-start.28 = (f32[64,2048]{1,0:T(8,128)}, f32[64,2048]{1,0:T(8,128)}, u32[]{:S(2)}, u32[]{:S(2)}) collective-permute-start(f32[64,2048]{1,0:T(8,128)} %get-tuple-element.63), channel_id=1, source_target_pairs={{0,24},{2,98},{4,28},{6,102},{8,0},{10,106},{12,4},{14,110},{16,8}... | collective-permute-start | bytes 1572872 | tf_op jit(solution)/shard_map/ppermute | solution.py:218
  91.7 30.5 %collective-permute-start.29 = (f32[64,2048]{1,0:T(8,128)}, f32[64,2048]{1,0:T(8,128)}, u32[]{:S(2)}, u32[]{:S(2)}) collective-permute-start(f32[64,2048]{1,0:T(8,128)} %get-tuple-element.64), channel_id=1, source_target_pairs={{0,8},{2,34},{4,12},{6,38},{8,16},{10,42},{12,20},{14,46},{16,24},... | collective-permute-start | bytes 1572872 | tf_op jit(solution)/shard_map/ppermute | solution.py:218
  97.1 30.5 %collective-permute-start.14 = (f32[256,1024]{1,0:T(8,128)}, f32[256,1024]{1,0:T(8,128)}, u32[]{:S(2)}, u32[]{:S(2)}) collective-permute-start(f32[256,1024]{1,0:T(8,128)} %get-tuple-element.34), channel_id=1, source_target_pairs={{0,32},{2,10},{4,36},{6,14},{8,40},{10,18},{12,44},{14,22},{16,48}... | collective-permute-start | bytes 3145736 | tf_op jit(solution)/shard_map/ppermute | solution.py:218
  97.7 29.9 %collective-permute-start.13 = (f32[256,1024]{1,0:T(8,128)}, f32[256,1024]{1,0:T(8,128)}, u32[]{:S(2)}, u32[]{:S(2)}) collective-permute-start(f32[256,1024]{1,0:T(8,128)} %get-tuple-element.35), channel_id=1, source_target_pairs={{0,96},{2,26},{4,100},{6,30},{8,104},{10,2},{12,108},{14,6},{16,11... | collective-permute-start | bytes 3145736 | tf_op jit(solution)/shard_map/ppermute | solution.py:218
  106.3 11.3 %collective-permute-start.9 = (f32[128,1024]{1,0:T(8,128)}, f32[128,1024]{1,0:T(8,128)}, u32[]{:S(2)}, u32[]{:S(2)}) collective-permute-start(f32[128,1024]{1,0:T(8,128)} %fusion.27), channel_id=1, source_target_pairs={{0,1},{1,0},{2,3},{3,2},{4,5},{5,4},{6,7},{7,6},{8,9},{9,8},{10,11... | collective-permute-start | bytes 1572872 | tf_op jit(solution)/shard_map/ppermute | solution.py:24
  120.4 13.5 %collective-permute-start.12 = (f32[136,1024]{1,0:T(8,128)S(1)}, f32[136,1024]{1,0:T(8,128)S(1)}, u32[]{:S(2)}, u32[]{:S(2)}) collective-permute-start(f32[136,1024]{1,0:T(8,128)S(1)} %pad_maximum_fusion), channel_id=1, source_target_pairs={{0,1},{1,0},{2,3},{3,2},{4,5},{5,4},{6,7},{7,6},{8,9},{9,8},{10,11... | collective-permute-start | bytes 1671176 | tf_op jit(solution)/shard_map/ppermute | solution.py:24
  124.3 10.4 %collective-permute-start.30 = (f32[32,2048]{1,0:T(8,128)}, f32[32,2048]{1,0:T(8,128)}, u32[]{:S(2)}, u32[]{:S(2)}) collective-permute-start(f32[32,2048]{1,0:T(8,128)} %get-tuple-element.61), channel_id=1, source_target_pairs={{0,8},{2,34},{4,12},{6,38},{8,16},{10,42},{12,20},{14,46},{16,24},... | collective-permute-start | bytes 786440 | tf_op jit(solution)/shard_map/ppermute | solution.py:218
  124.3 17.2 %collective-permute-start.31 = (f32[32,2048]{1,0:T(8,128)}, f32[32,2048]{1,0:T(8,128)}, u32[]{:S(2)}, u32[]{:S(2)}) collective-permute-start(f32[32,2048]{1,0:T(8,128)} %get-tuple-element.62), channel_id=1, source_target_pairs={{0,24},{2,98},{4,28},{6,102},{8,0},{10,106},{12,4},{14,110},{16,8}... | collective-permute-start | bytes 786440 | tf_op jit(solution)/shard_map/ppermute | solution.py:218
  130.6 16.1 %collective-permute-start.15 = (f32[128,1024]{1,0:T(8,128)}, f32[128,1024]{1,0:T(8,128)}, u32[]{:S(2)}, u32[]{:S(2)}) collective-permute-start(f32[128,1024]{1,0:T(8,128)} %get-tuple-element.67), channel_id=1, source_target_pairs={{0,32},{2,10},{4,36},{6,14},{8,40},{10,18},{12,44},{14,22},{16,48}... | collective-permute-start | bytes 1572872 | tf_op jit(solution)/shard_map/ppermute | solution.py:218
  130.8 15.9 %collective-permute-start.16 = (f32[128,1024]{1,0:T(8,128)}, f32[128,1024]{1,0:T(8,128)}, u32[]{:S(2)}, u32[]{:S(2)}) collective-permute-start(f32[128,1024]{1,0:T(8,128)} %get-tuple-element.68), channel_id=1, source_target_pairs={{0,96},{2,26},{4,100},{6,30},{8,104},{10,2},{12,108},{14,6},{16,11... | collective-permute-start | bytes 1572872 | tf_op jit(solution)/shard_map/ppermute | solution.py:218
  134.8 11.8 %collective-permute-start.18 = (f32[8,1024]{1,0:T(8,128)S(1)}, f32[8,1024]{1,0:T(8,128)S(1)}, u32[]{:S(2)}, u32[]{:S(2)}) collective-permute-start(f32[8,1024]{1,0:T(8,128)S(1)} %fusion.64), channel_id=1, source_target_pairs={{0,96},{2,26},{4,100},{6,30},{8,104},{10,2},{12,108},{14,6},{16,11... | collective-permute-start | bytes 98312 | tf_op jit(solution)/shard_map/ppermute | solution.py:218
  151.0 8.1 %collective-permute-start.33 = (f32[16,2048]{1,0:T(8,128)S(1)}, f32[16,2048]{1,0:T(8,128)S(1)}, u32[]{:S(2)}, u32[]{:S(2)}) collective-permute-start(f32[16,2048]{1,0:T(8,128)S(1)} %slice.390), channel_id=1, source_target_pairs={{0,2},{2,0},{1,3},{3,1},{4,6},{6,4},{5,7},{7,5},{8,10},{10,8},{9,1... | collective-permute-start | bytes 393224 | tf_op jit(solution)/shard_map/ppermute | solution.py:24
  (40 other events, 339.8 us)

commit v3 on v2

v3 whole, which is shorter than its diff:
```python
import functools

import jax
import jax.numpy as jnp
from jax import lax
from jax.experimental import pallas as pl
from jax.experimental.pallas import tpu as pltpu
from jax.sharding import Mesh
from jax.sharding import PartitionSpec as P

HEAD_DIM = 64
ROTARY = 16
DP = ("dp_0", "dp_1", "dp_2", "dp_3")
X, Y, ZH, CORE = DP
TENSOR = "tensor"

epsilon = 1e-05

CONTRACT_COLS = (((1,), (1,)), ((), ()))


def shift(array, axis, step):
    size = lax.axis_size(axis)
    return lax.ppermute(array, axis, [(i, (i + step) % size) for i in range(size)])


def layout_rows(lengths, owner_group, row_offset, row_index, group_rows):
    first_row = owner_group * group_rows + row_offset
    inside = (row_index[:, None] >= first_row[None, :]) & (
        row_index[:, None] < (first_row + lengths)[None, :]
    )
    number = jnp.arange(lengths.shape[0], dtype=jnp.int32) + 1
    segment = jnp.sum(jnp.where(inside, number[None, :], 0), axis=1) - 1
    position = jnp.sum(jnp.where(inside, row_index[:, None] - first_row[None, :], 0), axis=1)
    return (segment, position)


def rotary_tables(position):
    lane = jnp.arange(2 * HEAD_DIM, dtype=jnp.int32) % HEAD_DIM
    half_rot = ROTARY // 2
    frequency = 1.0 / 10000.0 ** ((lane % half_rot).astype(jnp.float32) * 2.0 / ROTARY)
    angles = position.astype(jnp.float32)[:, None] * frequency[None, :]
    turned = (lane < ROTARY)[None, :]
    sign = jnp.where(lane < half_rot, -1.0, 1.0)[None, :]
    return (jnp.where(turned, jnp.cos(angles), 1.0), jnp.where(turned, jnp.sin(angles) * sign, 0.0))


def normalize_back(grad_rows, unit_rows, inv_scale, gain_row):
    scaled = grad_rows * gain_row
    return inv_scale * (
        scaled
        - jnp.mean(scaled, axis=-1, keepdims=True)
        - unit_rows * jnp.mean(scaled * unit_rows, axis=-1, keepdims=True)
    )


def attention_kernel(
    core,
    projected,
    context_grad,
    segment_column,
    segment_row,
    cosine,
    sine,
    context,
    grad,
    mine,
    theirs,
    turned,
    raw,
):
    rows, cols = projected.shape
    heads = cols // (3 * HEAD_DIM)
    lane = lax.broadcasted_iota(jnp.int32, (rows, 128), 1)
    entry = lane % HEAD_DIM
    scale = HEAD_DIM ** (-0.5)
    tables = []
    for kind in range(3):
        halves = [(2 * kind + side) % 3 for side in range(2)]
        cos_t, sin_t = cosine[...], sine[...]
        low = lane < HEAD_DIM
        for side, what in enumerate(halves):
            here = low if side == 0 else jnp.logical_not(low)
            if what == 0:
                cos_t = jnp.where(here, cos_t * scale, cos_t)
                sin_t = jnp.where(here, sin_t * scale, sin_t)
            if what == 2:
                cos_t = jnp.where(here, 1.0, cos_t)
                sin_t = jnp.where(here, 0.0, sin_t)
        tables.append((cos_t, sin_t))

    def swapped(part):
        up = pltpu.roll(part, 128 - ROTARY // 2, 1)
        down = pltpu.roll(part, ROTARY // 2, 1)
        return jnp.where(entry < ROTARY // 2, up, down)

    for chunk in range(cols // 128):
        at = slice(128 * chunk, 128 * (chunk + 1))
        part = projected[:, at]
        cos_t, sin_t = tables[chunk % 3]
        turned[:, at] = (part * cos_t + swapped(part) * sin_t).astype(jnp.bfloat16)

    allowed = (segment_column[...] == segment_row[...]) & (
        lax.broadcasted_iota(jnp.int32, (rows, rows), 1)
        <= lax.broadcasted_iota(jnp.int32, (rows, rows), 0)
    )

    def product(left, right, dims):
        return lax.dot_general(left, right, (dims, ((), ())), preferred_element_type=jnp.float32)

    for head in range(heads):
        base = 3 * HEAD_DIM * head
        query = turned[:, base : base + HEAD_DIM]
        key = turned[:, base + HEAD_DIM : base + 2 * HEAD_DIM]
        value = turned[:, base + 2 * HEAD_DIM : base + 3 * HEAD_DIM]
        at = slice(HEAD_DIM * head, HEAD_DIM * (head + 1))
        out_grad = context_grad[:, at].astype(jnp.bfloat16)
        scores = jnp.where(allowed, product(query, key, ((1,), (1,))), -1e30)
        highest = jnp.max(scores, axis=-1, keepdims=True)
        weights = jnp.where(allowed, jnp.exp(scores - highest), 0.0)
        probs = weights / jnp.sum(weights, axis=-1, keepdims=True)
        probs_low = probs.astype(jnp.bfloat16)
        out = product(probs_low, value, ((1,), (0,))).astype(jnp.bfloat16)
        context[:, at] = out
        offset = jnp.sum(
            out_grad.astype(jnp.float32) * out.astype(jnp.float32), axis=-1, keepdims=True
        )
        probs_grad = product(out_grad, value, ((1,), (1,)))
        score_grad = (probs * (probs_grad - offset)).astype(jnp.bfloat16)
        raw[:, base : base + HEAD_DIM] = product(score_grad, key, ((1,), (0,)))
        raw[:, base + HEAD_DIM : base + 2 * HEAD_DIM] = product(score_grad, query, ((0,), (0,)))
        raw[:, base + 2 * HEAD_DIM : base + 3 * HEAD_DIM] = product(
            probs_low, out_grad, ((0,), (0,))
        )

    for chunk in range(cols // 128):
        at = slice(128 * chunk, 128 * (chunk + 1))
        part = raw[:, at]
        cos_t, sin_t = tables[chunk % 3]
        back = part * cos_t - swapped(part) * sin_t
        raw[:, at] = back
        grad[:, at] = back.astype(jnp.bfloat16)

    for side in range(2):

        @pl.when(core[0] == side)
        def _():
            for out, half in ((mine, side), (theirs, 1 - side)):
                for whole, start in ((context, 0), (raw, context.shape[1] // 2)):
                    width = whole.shape[1] // 2
                    out[:, start : start + width] = whole[
                        :, half * width : (half + 1) * width
                    ].astype(out.dtype)


def attention(core, projected, context_grad, segment, cosine, sine):
    rows, cols = projected.shape
    width = (cols + context_grad.shape[1]) // 2
    vmem = pl.BlockSpec(memory_space=pltpu.VMEM)
    return pl.pallas_call(
        attention_kernel,
        in_specs=[pl.BlockSpec(memory_space=pltpu.SMEM)] + [vmem] * 6,
        out_shape=(
            jax.ShapeDtypeStruct(context_grad.shape, jnp.bfloat16),
            jax.ShapeDtypeStruct((rows, cols), jnp.bfloat16),
            jax.ShapeDtypeStruct((rows, width), jnp.bfloat16),
            jax.ShapeDtypeStruct((rows, width), jnp.float32),
        ),
        scratch_shapes=[
            pltpu.VMEM((rows, cols), jnp.bfloat16),
            pltpu.VMEM((rows, cols), jnp.float32),
        ],
        name="attention",
    )(core, projected, context_grad, segment[:, None], segment[None, :], cosine, sine)


def prologue_kernel(
    rows_in, grads_in, valid, gain, bias, message, branch_in, units_in, heads_in, unit_rows, inv_scale
):
    width = rows_in.shape[1]
    hidden = rows_in[...].astype(jnp.float32)
    centred = hidden - jnp.mean(hidden, axis=-1, keepdims=True)
    inv = lax.rsqrt(jnp.mean(centred * centred, axis=-1, keepdims=True) + epsilon)
    unit = centred * inv
    inv_scale[...] = inv
    unit_rows[...] = unit
    branch = grads_in[...].astype(jnp.float32) * valid[...]
    message[:, :width] = branch
    branch_in[...] = branch.astype(jnp.bfloat16)
    heads = unit * gain[0:1, :] + bias[0:1, :]
    units = unit * gain[1:2, :] + bias[1:2, :]
    message[:, width : 2 * width] = units
    units_in[...] = units.astype(jnp.bfloat16)
    message[:, 2 * width :] = heads
    heads_in[...] = heads.astype(jnp.bfloat16)


def prologue(rows_in, grads_in, valid, gain, bias):
    rows, width = rows_in.shape
    low = jax.ShapeDtypeStruct((rows, width), jnp.bfloat16)
    return pl.pallas_call(
        prologue_kernel,
        out_shape=(
            jax.ShapeDtypeStruct((rows, 3 * width), jnp.float32),
            low,
            low,
            low,
            jax.ShapeDtypeStruct((rows, width), jnp.float32),
            jax.ShapeDtypeStruct((rows, 1), jnp.float32),
        ),
        name="prologue",
    )(rows_in, grads_in, valid, gain, bias)


PIECES = 4


def order(step, core):
    return ((1 - core[0]) * (PIECES // 2) + step) % PIECES


def first_half(step, core):
    return (0, jnp.minimum(step, PIECES // 2 - 1))


def second_half(step, core):
    return (0, jnp.maximum(step - PIECES // 2, 0))


def up_kernel(core, units_in, weight, bias, activated, slope, mine, theirs):
    before = jnp.dot(units_in[...], weight[...], preferred_element_type=jnp.float32) + bias[...]
    rise = 0.5 * (1.0 + lax.erf(before * 0.7071067811865476))
    after = before * rise
    low = after.astype(jnp.bfloat16)
    activated[...] = low
    slope[...] = rise + before * jnp.exp(-0.5 * before * before) * 0.3989422804014327

    @pl.when(pl.program_id(0) < PIECES // 2)
    def _():
        theirs[...] = after

    @pl.when(pl.program_id(0) >= PIECES // 2)
    def _():
        mine[...] = low


def down_kernel(core, branch_in, weight, slope, pre_in, sums, mine, theirs):
    grad = jnp.dot(branch_in[...], weight[...], preferred_element_type=jnp.float32) * slope[...]
    low = grad.astype(jnp.bfloat16)
    pre_in[...] = low
    sums[...] = jnp.sum(grad, axis=0, keepdims=True)

    @pl.when(pl.program_id(0) < PIECES // 2)
    def _():
        theirs[...] = grad

    @pl.when(pl.program_id(0) >= PIECES // 2)
    def _():
        mine[...] = low


def hidden_call(kernel, name, core, rows_in, weight, extra, outs):
    rows, width = rows_in.shape
    cols = weight.shape[1]
    piece = cols // PIECES

    def whole(height):
        return pl.BlockSpec((height, piece), lambda step, core: (0, order(step, core)))

    return pl.pallas_call(
        kernel,
        grid_spec=pltpu.PrefetchScalarGridSpec(
            num_scalar_prefetch=1,
            grid=(PIECES,),
            in_specs=[
                pl.BlockSpec((rows, width), lambda step, core: (0, 0)),
                whole(width),
                whole(extra.shape[0]),
            ],
            out_specs=[whole(height) for height, _ in outs]
            + [pl.BlockSpec((rows, piece), second_half), pl.BlockSpec((rows, piece), first_half)],
        ),
        out_shape=[jax.ShapeDtypeStruct((height, cols), dtype) for height, dtype in outs]
        + [
            jax.ShapeDtypeStruct((rows, cols // 2), jnp.bfloat16),
            jax.ShapeDtypeStruct((rows, cols // 2), jnp.float32),
        ],
        name=name,
    )(core, rows_in, weight, extra)


def product_kernel(splits, *refs):
    lefts, (own, near) = refs[: len(splits)], refs[len(splits) : len(splits) + 2]
    low, high, kept, to_next, to_last = refs[len(splits) + 2 :]
    right = jnp.concatenate([own[...], near[...].astype(jnp.bfloat16)], axis=0)
    for left, (start, stop) in zip(lefts, splits):
        eighth = left.shape[0] // 8
        targets = (
            (low, 0), (to_next, 0), (to_next, 1), (to_last, 0), (to_last, 1), (high, 0), (kept, 0), (kept, 1),
        )
        for block, (out, place) in enumerate(targets):
            out[place * eighth : (place + 1) * eighth, start:stop] = jnp.dot(
                left[block * eighth : (block + 1) * eighth, :],
                right[:, start:stop],
                preferred_element_type=jnp.float32,
            )


def products(lefts, splits, own, near):
    rows, cols = lefts[0].shape[0], own.shape[1]
    sizes = (rows // 8, rows // 8, rows // 4, rows // 4, rows // 4)
    return pl.pallas_call(
        functools.partial(product_kernel, splits),
        out_shape=tuple(jax.ShapeDtypeStruct((size, cols), jnp.float32) for size in sizes),
        name="products",
    )(*lefts, own, near)


def middle_kernel(low, high, minus, plus, low_out, high_out):
    low_out[...] = low[...] + minus[...]
    high_out[...] = high[...] + plus[...]


def middle(low, high, minus, plus):
    half, cols = low.shape
    pieces = 4
    block = (half, cols // pieces)
    same = pl.BlockSpec(block, lambda i: (0, i))
    shape = jax.ShapeDtypeStruct(low.shape, jnp.float32)
    return pl.pallas_call(
        middle_kernel,
        grid=(pieces,),
        in_specs=[same, same, pl.BlockSpec(block, lambda i: (1, i)), same],
        out_specs=[same, same],
        out_shape=(shape, shape),
        name="middle",
    )(low, high, minus, plus)


def finish(kept, minus, plus, low, high):
    half = kept.shape[0] // 2
    return (
        kept
        + jnp.concatenate([plus[half:], minus[:half]], axis=0)
        + jnp.concatenate([low, high], axis=0)
    )


def moves():
    def along(first, step):
        pairs = []
        for index in range(64):
            x, y, rest, core = index // 16, index // 4 % 4, index % 4, index % 2
            if (core == 0) == first:
                x = (x + step) % 4
            else:
                y = (y + step) % 4
            pairs.append((index, x * 16 + y * 4 + rest))
        return pairs

    return {(first, step): along(first, step) for first in (True, False) for step in (1, -1)}


MOVES = moves()


def ring(array, first, step):
    return lax.ppermute(array, DP, MOVES[first, step])


def tie(values, *others):
    return lax.optimization_barrier((values, *others))[0]


def selection(width):
    ix, iy, iz, core = (lax.axis_index(axis) for axis in DP)
    row = jnp.arange(width, dtype=jnp.int32)
    block = width // 64
    inner = row % block
    at_core = core ^ (1 - row // block % 2)
    at_z = iz ^ (1 - row // (2 * block) % 2)
    second = row // (4 * block) % 4 + 1
    first = row // (16 * block) + 1
    at_x = (ix + jnp.where(core == 0, first, second)) % 4
    at_y = (iy + jnp.where(core == 0, second, first)) % 4
    feature = (((at_x * 4 + at_y) * 2 + at_z) * 2 + at_core) * block + inner
    column = jnp.arange(width, dtype=jnp.int32)
    return (feature[:, None] == column[None, :]).astype(jnp.bfloat16)


def pick_kernel(chosen, own, near, out):
    rows = jnp.concatenate([own[...], near[...].astype(jnp.bfloat16)], axis=0)
    out[...] = lax.dot_general(
        chosen[...], rows, CONTRACT_COLS, preferred_element_type=jnp.float32
    ).astype(jnp.bfloat16)


def pick(chosen, own, near, place):
    width = chosen.shape[0]
    rows = own.shape[0]
    pieces = 4
    return pl.pallas_call(
        pick_kernel,
        grid=(pieces,),
        in_specs=[
            pl.BlockSpec((width // pieces, width), lambda i: (i, 0)),
            pl.BlockSpec((rows, width), lambda i: (0, 0)),
            pl.BlockSpec((rows, width), lambda i: (0, place)),
        ],
        out_specs=pl.BlockSpec((width // pieces, 2 * rows), lambda i: (i, 0)),
        out_shape=jax.ShapeDtypeStruct((width, 2 * rows), jnp.bfloat16),
        name="pick",
    )(chosen, own, near)


def shards(
    block_input,
    cotangent,
    qkv_weight,
    dense_weight,
    up_weight,
    down_weight,
    up_bias,
    down_bias,
    norm_gain,
    norm_bias,
    lengths,
    owner_group,
    row_offset,
):
    row_count, model_width = block_input.shape
    qkv_weight, dense_weight = qkv_weight[0], dense_weight[0]
    up_weight, down_weight = up_weight[0], down_weight[0]
    norm_gain, norm_bias = norm_gain[0], norm_bias[0]
    hidden_cols = up_weight.shape[1]
    table_rows = hidden_cols // model_width

    group = lax.axis_index(DP)
    core = lax.axis_index(CORE)
    core_ref = core.astype(jnp.int32)[None]
    own_index = group * row_count + jnp.arange(row_count, dtype=jnp.int32)
    segment, position = layout_rows(lengths, owner_group, row_offset, own_index, row_count)
    valid_rows = (segment >= 0).astype(jnp.float32)[:, None]

    message, branch_in, units_in, heads_in, unit_rows, inv_scale = prologue(
        block_input, cotangent, valid_rows, norm_gain, norm_bias
    )
    near_rows = shift(message, CORE, 1)
    chosen = selection(model_width)

    def left_of(own, place):
        return pick(chosen, own, near_rows, place)

    activated, slope, mine_a, theirs_a = hidden_call(
        up_kernel,
        "up",
        core_ref,
        units_in,
        up_weight,
        up_bias,
        ((row_count, jnp.bfloat16), (row_count, jnp.float32)),
    )
    near_a = shift(theirs_a, CORE, 1)
    branch_left = left_of(tie(branch_in, theirs_a), 0)
    every = (0, mine_a.shape[1])
    low_a, high_a, kept_a, next_a, last_a = products((branch_left,), (every,), mine_a, near_a)
    minus_a, plus_a = ring(next_a, True, 1), ring(last_a, True, -1)

    pre_in, pre_sums, mine_b, theirs_b = hidden_call(
        down_kernel,
        "down",
        core_ref,
        tie(branch_in, next_a, last_a),
        down_weight,
        slope,
        ((row_count, jnp.bfloat16), (1, jnp.float32)),
    )
    near_b = shift(theirs_b, CORE, 1)
    units_left = left_of(tie(units_in, theirs_b), 1)
    low_b, high_b, kept_b, next_b, last_b = products((units_left,), (every,), mine_b, near_b)
    minus_b, plus_b = ring(next_b, True, 1), ring(last_b, True, -1)

    cosine_table, sine_table = rotary_tables(tie(position, next_b))
    heads_now, branch_now = tie((heads_in, branch_in), next_b, last_b)
    projected = jnp.dot(heads_now, qkv_weight, preferred_element_type=jnp.float32)
    context_grad = jnp.dot(branch_now, dense_weight, preferred_element_type=jnp.float32)
    low_a, high_a = middle(low_a, high_a, *tie((minus_a, plus_a), projected, context_grad))
    projected = tie(projected, low_a, high_a)
    low_a, high_a = ring(low_a, True, 1), ring(high_a, True, -1)
    context, projected_grad, mine_c, theirs_c = attention(
        core_ref, projected, context_grad, segment, cosine_table, sine_table
    )
    near_c = shift(theirs_c, CORE, 1)
    split = context.shape[1] // 2
    low_b, high_b = middle(low_b, high_b, *tie((minus_b, plus_b), theirs_c))
    heads_left = left_of(tie(heads_in, low_b, high_b), 2)
    low_b, high_b = ring(low_b, True, 1), ring(high_b, True, -1)
    low_c, high_c, kept_c, next_c, last_c = products(
        (branch_left, heads_left), ((0, split), (split, every[1])), mine_c, near_c
    )
    minus_c, plus_c = ring(next_c, True, 1), ring(last_c, True, -1)

    def second_send(rows, extra):
        half = rows.shape[0] // 8
        up = jnp.concatenate([rows[half : 3 * half], extra])
        down = jnp.concatenate([rows[3 * half : 5 * half], extra])
        return up, down

    def second_middle(rows, minus, plus):
        half = rows.shape[0] // 8
        low = jnp.concatenate([rows[:half] + minus[half : 2 * half], minus[2 * half :]])
        high = rows[5 * half : 6 * half] + plus[:half]
        return low, high

    def second_finish(rows, extra, minus, plus, low, high):
        half = rows.shape[0] // 8
        rows = (
            rows[6 * half :]
            + jnp.concatenate([plus[half : 2 * half], minus[:half]], axis=0)
            + jnp.concatenate([low[:half], high], axis=0)
        )
        return rows, extra + (minus[2 * half :] + plus[2 * half :]) + low[half:]

    low_a, high_a, low_b, high_b = tie((low_a, high_a, low_b, high_b), next_c, last_c)
    early = jnp.concatenate(
        [
            finish(kept_a, minus_a, plus_a, low_a, high_a),
            finish(kept_b, minus_b, plus_b, low_b, high_b),
        ],
        axis=1,
    )
    none = jnp.zeros((0, early.shape[1]), jnp.float32)
    up_early, down_early = second_send(early, none)
    projected_grad, pre_in = tie((projected_grad, pre_in), up_early, down_early)
    minus_e, plus_e = ring(up_early, False, 1), ring(down_early, False, -1)

    heads_grad = lax.dot_general(
        projected_grad, qkv_weight, CONTRACT_COLS, preferred_element_type=jnp.float32
    )
    units_grad = lax.dot_general(
        pre_in, up_weight, CONTRACT_COLS, preferred_element_type=jnp.float32
    )
    local_back = normalize_back(
        heads_grad, unit_rows, inv_scale, norm_gain[0]
    ) + normalize_back(units_grad, unit_rows, inv_scale, norm_gain[1])
    grad_rows = cotangent.astype(jnp.float32)

    small = jnp.concatenate(
        [
            jnp.sum(heads_grad * unit_rows, axis=0)[None],
            jnp.sum(units_grad * unit_rows, axis=0)[None],
            jnp.sum(heads_grad, axis=0)[None],
            jnp.sum(units_grad, axis=0)[None],
            jnp.sum(message[:, :model_width], axis=0)[None],
            pre_sums.reshape(table_rows, model_width),
        ],
        axis=0,
    )
    small = jnp.pad(small, ((0, 8 - small.shape[0]), (0, 0)))
    back_out = jnp.concatenate([local_back, small], axis=0)
    near_back = shift(back_out, TENSOR, 1)

    low_c, high_c = middle(low_c, high_c, *tie((minus_c, plus_c), back_out))
    activated = tie(activated, low_c, high_c)
    low_c, high_c = ring(low_c, True, 1), ring(high_c, True, -1)
    minus_e, plus_e = tie((minus_e, plus_e), activated)
    low_e, high_e = second_middle(early, minus_e, plus_e)
    activated = tie(activated, low_e, high_e)
    low_e, high_e = ring(low_e, False, 1), ring(high_e, False, -1)
    partial_rows = lax.dot_general(
        context, dense_weight, CONTRACT_COLS, preferred_element_type=jnp.float32
    ) + lax.dot_general(
        activated, down_weight, CONTRACT_COLS, preferred_element_type=jnp.float32
    )
    near_back = tie(near_back, partial_rows)
    near_partial = shift(partial_rows, TENSOR, 1)

    summed = jnp.arange(8)[:, None] < 4
    small = small + jnp.where(summed, near_back[row_count:], 0.0)
    small_minus, small_plus = ring(small, True, 1), ring(small, True, -1)
    low_c, high_c = tie((low_c, high_c), small)
    late = finish(kept_c, minus_c, plus_c, low_c, high_c)
    small = small + (small_minus + small_plus) + ring(small_minus, True, 1)
    up_late, down_late = second_send(late, small)
    minus_l, plus_l = ring(up_late, False, 1), ring(down_late, False, -1)

    low_e, high_e, near_partial, near_back = tie(
        (low_e, high_e, near_partial, near_back), up_late, down_late
    )
    early, _ = second_finish(early, none, minus_e, plus_e, low_e, high_e)
    keep = early.shape[0] // 2
    other_early = shift(early[:keep], ZH, 1)
    input_grad = grad_rows + (local_back + near_back[:row_count])
    minus_l, plus_l = tie((minus_l, plus_l), early)
    low_l, high_l = second_middle(late, minus_l, plus_l)
    near_partial = tie(near_partial, low_l, high_l)
    low_l, high_l = ring(low_l, False, 1), ring(high_l, False, -1)
    output = block_input.astype(jnp.float32) + valid_rows * (
        (partial_rows + near_partial) + down_bias
    )
    early = early[keep:] + other_early
    half = keep // 2
    near_early = shift(early[:half], CORE, 1)
    late, small = second_finish(late, small, minus_l, plus_l, low_l, high_l)
    other_late = shift(jnp.concatenate([late[:keep], small]), ZH, 1)
    late = late[keep:] + other_late[:keep]
    small = small + other_late[keep:]
    near_late = shift(jnp.concatenate([late[:half], small]), CORE, 1)
    small = small + near_late[half:]

    def joined(own, near):
        return jnp.concatenate(
            [jnp.where(core == 0, own, near), jnp.where(core == 0, near, own)], axis=1
        )

    column = hidden_cols // 2
    down_grad = joined(early[half:, :column], near_early[:, :column])
    up_grad = joined(early[half:, column:], near_early[:, column:])
    dense_grad = joined(late[half:, :split], near_late[:half, :split])
    qkv_grad = joined(late[half:, split:], near_late[:half, split:])
    block = model_width // lax.axis_size(DP)
    small = lax.dynamic_slice_in_dim(small, group * block, block, axis=1)
    return (
        output,
        input_grad,
        qkv_grad[None],
        dense_grad[None],
        up_grad[None],
        down_grad[None],
        small[5 : 5 + table_rows][None],
        small[4][None],
        small[:2][None],
        small[2:4][None],
    )


def solution(mesh):
    split = Mesh(
        mesh.devices.reshape(4, 4, 2, 2, mesh.shape["tensor"]),
        (*DP, TENSOR),
    )
    in_specs = (
        P(DP, None),
        P(DP, None),
        P(None, None, "tensor"),
        P(None, None, "tensor"),
        P(None, None, "tensor"),
        P(None, None, "tensor"),
        P(None, "tensor"),
        P(),
        P(),
        P(),
        P(),
        P(),
        P(),
    )
    out_specs = (
        P(DP, None),
        P(DP, None),
        P(None, DP, "tensor"),
        P(None, DP, "tensor"),
        P(None, DP, "tensor"),
        P(None, DP, "tensor"),
        P(None, "tensor", DP),
        P(None, DP),
        P(None, None, DP),
        P(None, None, DP),
    )
    return jax.shard_map(
        shards, mesh=split, in_specs=in_specs, out_specs=out_specs, check_vma=False
    )
```

time: 177 us -> 177 us (level)
  Pallas kernels: 20 us -> 56.6 us
  other arithmetic: 40.8 us -> 23.8 us
  matrix products: 27.9 us -> 11.5 us
  waiting for transfers between devices: 32.7 us -> 21.2 us
  local copies, waits for them, and re-layouts: 6.83 us -> 11.8 us
  starting transfers between devices: 45 us -> 48.7 us
    pallas_call x4 -> x13, Pallas kernels: 20 us -> 56.6 us  [the longest x3 13 us: pick(): pl.pallas_call(pick_kernel, grid=(pieces,), in_specs=[pl.BlockSpec((width...]
    dot_general x7 -> x2, matrix products: 14.9 us -> 4.68 us  [the longest x1 2.44 us: shards(): jnp.dot(heads_now, qkv_weight, preferred_element_type=jnp.float32)]
    convert_element_type x10 -> x1, other arithmetic: 10.9 us -> 1.75 us  [selection(): return (feature[:, None] == column[None, :]).astype(jnp.bfloat16)]
    ppermute x23, waiting for transfers between devices: 19.7 us -> 12 us  [ring(): return lax.ppermute(array, DP, MOVES[first, step])]
    slice x12 -> x15, local copies, waits for them, and re-layouts: 3.13 us -> 9.91 us  [the longest x3 4.93 us: finish(): minus[:half]]
    reduce_sum x5 -> x1, other arithmetic: 5.71 us -> 1.09 us  [shards(): jnp.sum(message[:, :model_width], axis=0)[None]]
    add x18 -> x14, other arithmetic: 13.1 us -> 9.24 us  [the longest x3 5.76 us: finish(): kept + jnp.concatenate([plus[half:], minus[:half]], axis=0)]
    ppermute x11 -> x10, waiting for transfers between devices: 13 us -> 9.24 us  [shift(): lax.ppermute(array, axis, [(i, (i + step) % size) for i in range(size)])]
  transfers between devices with their start and end apart: 34 -> 33, of which waited for: 12 -> 10; matrix products, arithmetic and copies ran while one was open for 38% -> 24% of each run, Pallas kernels for 11% -> 26%
where the time goes in v3:
time: 177 us; the launch traced here: 175 us
  Pallas kernels  56.6 us (32%)
  starting transfers between devices  48.7 us (28%)
  other arithmetic  23.8 us (13%)
  waiting for transfers between devices  21.2 us (12%)
  local copies, waits for them, and re-layouts  11.8 us (7%)
  matrix products  11.5 us (6%)
    ppermute x23, starting transfers between devices, ring(): return lax.ppermute(array, DP, MOVES[first, step])  34.8 us
    ppermute x10, starting transfers between devices, shift(): lax.ppermute(array, axis, [(i, (i + step) % size) for i in range(size)])  13.9 us
    pallas_call x3, Pallas kernels, pick(): pl.pallas_call(pick_kernel, grid=(pieces,), in_specs=[pl.BlockSpec((width...  13 us
    ppermute x23, waiting for transfers between devices, ring(): return lax.ppermute(array, DP, MOVES[first, step])  12 us
    pallas_call x3, Pallas kernels, middle(): pl.pallas_call(middle_kernel, grid=(pieces,), in_specs=[same, same, pl.Bl...  11 us
    pallas_call x3, Pallas kernels, products(): pl.pallas_call(functools.partial(product_kernel, splits), out_shape=tuple...  10.7 us
    pallas_call x2, Pallas kernels, hidden_call(): pl.pallas_call(kernel, grid_spec=pltpu.PrefetchScalarGridSpec(num_scalar_...  10.2 us
    ppermute x10, waiting for transfers between devices, shift(): lax.ppermute(array, axis, [(i, (i + step) % size) for i in range(size)])  9.24 us
  transfers between devices with their start and end apart: 33, of which 10 were waited for; matrix products, arithmetic and copies ran while one was open for 24% of the time, Pallas kernels for 26%

profile of v3, /device:TPU:0, one launch (start us, length us, event | category | flops | bytes accessed | tf_op | source)
XLA Modules:
  0.0 174.9 jit_solution(3292461305175822518)
XLA Ops:
  5.9 5.2 %up.1 = (bf16[128,2048]{1,0:T(8,128)(2,1)}, f32[128,2048]{1,0:T(8,128)}, bf16[128,1024]{1,0:T(8,128)(2,1)}, f32[128,1024]{1,0:T(8,128)}) custom-call(s32[1]{0:T(128)} %bitcast.core, bf16[128,1024]{1,0:T(8,128)(2,1)} %get-tuple-element.95.units_in.own, bf16[1024,2048]{1,0:T(8,128)(2,1)} %bitcast.53, f32[1,2048]{1,0:T(1,128)} %bias.1), custom_call_target="tpu_custom_call" | custom-call | tf_op jit(solution)/shard_map/up/pallas_call | solution.py:270
  13.3 4.4 %pick.3.refs_0_ = bf16[1024,256]{1,0:T(8,128)(2,1)} custom-call(bf16[1024,1024]{1,0:T(8,128)(2,1)} %fusion.chosen, bf16[128,1024]{1,0:T(8,128)(2,1)} %get-tuple-element.102.own.branch_in, f32[128,3072]{1,0:T(8,128)} %collective-permute-done.near), custom_call_target="tpu_custom_call" | custom-call | tf_op jit(solution)/shard_map/pick/pallas_call | solution.py:402
  17.7 3.5 %products.3 = (f32[128,1024]{1,0:T(8,128)}, f32[128,1024]{1,0:T(8,128)}, f32[256,1024]{1,0:T(8,128)}, f32[256,1024]{1,0:T(8,128)}, f32[256,1024]{1,0:T(8,128)}) custom-call(bf16[1024,256]{1,0:T(8,128)(2,1)} %pick.3.refs_0_, bf16[128,1024]{1,0:T(8,128)(2,1)} %get-tuple-element.89.refs_1_, f32[128,1024]{1,0:T(8,128)} %collective-permute-done.1.refs_2_), custom_call_target="tpu_custom_call" | custom-call | tf_op jit(solution)/shard_map/products/pallas_call | solution.py:312
  21.2 5.0 %down.1 = (bf16[128,2048]{1,0:T(8,128)(2,1)}, f32[1,2048]{1,0:T(1,128)}, bf16[128,1024]{1,0:T(8,128)(2,1)}, f32[128,1024]{1,0:T(8,128)}) custom-call(s32[1]{0:T(128)} %bitcast.core, bf16[128,1024]{1,0:T(8,128)(2,1)} %get-tuple-element.102.own.branch_in, bf16[1024,2048]{1,0:T(8,128)(2,1)} %bitcast.54, f32[128,2048]{1,0:T(8,128)} %get-tuple-element.93.slope), custom_call_target="tpu_custom_call" | custom-call | tf_op jit(solution)/shard_map/down/pallas_call | solution.py:270
  29.6 4.3 %pick.4.refs_0_ = bf16[1024,256]{1,0:T(8,128)(2,1)} custom-call(bf16[1024,1024]{1,0:T(8,128)(2,1)} %fusion.chosen, bf16[128,1024]{1,0:T(8,128)(2,1)} %get-tuple-element.95.units_in.own, f32[128,3072]{1,0:T(8,128)} %collective-permute-done.near), custom_call_target="tpu_custom_call" | custom-call | tf_op jit(solution)/shard_map/pick/pallas_call | solution.py:402
  33.9 3.4 %products.4 = (f32[128,1024]{1,0:T(8,128)}, f32[128,1024]{1,0:T(8,128)}, f32[256,1024]{1,0:T(8,128)}, f32[256,1024]{1,0:T(8,128)}, f32[256,1024]{1,0:T(8,128)}) custom-call(bf16[1024,256]{1,0:T(8,128)(2,1)} %pick.4.refs_0_, bf16[128,1024]{1,0:T(8,128)(2,1)} %get-tuple-element.96.refs_1_, f32[128,1024]{1,0:T(8,128)} %collective-permute-done.2.refs_2_), custom_call_target="tpu_custom_call" | custom-call | tf_op jit(solution)/shard_map/products/pallas_call | solution.py:312
  45.1 3.7 %middle.3 = (f32[128,1024]{1,0:T(8,128)}, f32[128,1024]{1,0:T(8,128)}) custom-call(f32[128,1024]{1,0:T(8,128)} %get-tuple-element.100.low, f32[128,1024]{1,0:T(8,128)} %get-tuple-element.101.high, f32[256,1024]{1,0:T(8,128)} %collective-permute-done.3.minus, f32[256,1024]{1,0:T(8,128)} %collective-permute-done.4.plus), custom_call_target="tpu_custom_call" | custom-call | tf_op jit(solution)/shard_map/middle/pallas_call | solution.py:330
  52.1 8.7 %attention.1 = (bf16[128,512]{1,0:T(8,128)(2,1)}, bf16[128,1536]{1,0:T(8,128)(2,1)}, bf16[128,1024]{1,0:T(8,128)(2,1)}, f32[128,1024]{1,0:T(8,128)}) custom-call(s32[1]{0:T(128)} %bitcast.core, f32[128,1536]{1,0:T(8,128)} %fusion.3.projected, f32[128,512]{1,0:T(8,128)} %fusion.9.context_grad, s32[128,1]{1,0:T(8,128)} %copy-done.18, ...), custom_call_target="tpu_custom_call" | custom-call | tf_op jit(solution)/shard_map/attention/pallas_call | solution.py:160
  60.8 3.7 %middle.4 = (f32[128,1024]{1,0:T(8,128)}, f32[128,1024]{1,0:T(8,128)}) custom-call(f32[128,1024]{1,0:T(8,128)} %get-tuple-element.111.low, f32[128,1024]{1,0:T(8,128)} %get-tuple-element.112.high, f32[256,1024]{1,0:T(8,128)} %collective-permute-done.5.minus, f32[256,1024]{1,0:T(8,128)} %collective-permute-done.6.plus), custom_call_target="tpu_custom_call" | custom-call | tf_op jit(solution)/shard_map/middle/pallas_call | solution.py:330
  77.8 4.3 %pick.5.refs_1_ = bf16[1024,256]{1,0:T(8,128)(2,1)} custom-call(bf16[1024,1024]{1,0:T(8,128)(2,1)} %fusion.chosen, bf16[128,1024]{1,0:T(8,128)(2,1)} %get-tuple-element.118.own, f32[128,3072]{1,0:T(8,128)} %collective-permute-done.near), custom_call_target="tpu_custom_call" | custom-call | tf_op jit(solution)/shard_map/pick/pallas_call | solution.py:402
  82.2 3.8 %products.5 = (f32[128,1024]{1,0:T(8,128)}, f32[128,1024]{1,0:T(8,128)}, f32[256,1024]{1,0:T(8,128)}, f32[256,1024]{1,0:T(8,128)}, f32[256,1024]{1,0:T(8,128)}) custom-call(bf16[1024,256]{1,0:T(8,128)(2,1)} %pick.3.refs_0_, bf16[1024,256]{1,0:T(8,128)(2,1)} %pick.5.refs_1_, bf16[128,1024]{1,0:T(8,128)(2,1)} %get-tuple-element.119.refs_2_, ...), custom_call_target="tpu_custom_call" | custom-call | tf_op jit(solution)/shard_map/products/pallas_call | solution.py:312
  86.0 3.2 %collective-permute-start.9 = (f32[256,1024]{1,0:T(8,128)}, f32[256,1024]{1,0:T(8,128)}, u32[]{:S(2)}, u32[]{:S(2)}) collective-permute-start(f32[256,1024]{1,0:T(8,128)} %get-tuple-element.123), channel_id=1, source_target_pairs={{0,96},{2,26},{4,100},{6,30},{8,104},{10,2},{12,108},{14,6},{16,11... | collective-permute-start | bytes 3145736 | tf_op jit(solution)/shard_map/ppermute | solution.py:368
  94.4 3.1 %collective-permute-start.15 = (f32[64,2048]{1,0:T(8,128)}, f32[64,2048]{1,0:T(8,128)}, u32[]{:S(2)}, u32[]{:S(2)}) collective-permute-start(f32[64,2048]{1,0:T(8,128)} %get-tuple-element.172), channel_id=1, source_target_pairs={{0,24},{2,98},{4,28},{6,102},{8,0},{10,106},{12,4},{14,110},{16,8}... | collective-permute-start | bytes 1572872 | tf_op jit(solution)/shard_map/ppermute | solution.py:368
  107.5 3.6 %middle.5 = (f32[128,1024]{1,0:T(8,128)}, f32[128,1024]{1,0:T(8,128)}) custom-call(f32[128,1024]{1,0:T(8,128)} %get-tuple-element.120.low, f32[128,1024]{1,0:T(8,128)} %get-tuple-element.121.high, f32[256,1024]{1,0:T(8,128)} %collective-permute-done.8.minus, f32[256,1024]{1,0:T(8,128)} %collective-permute-done.9.plus), custom_call_target="tpu_custom_call" | custom-call | tf_op jit(solution)/shard_map/middle/pallas_call | solution.py:330
  111.2 3.8 %collective-permute-start.21 = (f32[128,1024]{1,0:T(8,128)}, f32[128,1024]{1,0:T(8,128)}, u32[]{:S(2)}, u32[]{:S(2)}) collective-permute-start(f32[128,1024]{1,0:T(8,128)} %get-tuple-element.140), channel_id=1, source_target_pairs={{0,96},{2,26},{4,100},{6,30},{8,104},{10,2},{12,108},{14,6},{16,11... | collective-permute-start | bytes 1572872 | tf_op jit(solution)/shard_map/ppermute | solution.py:368
  121.9 3.2 %collective-permute-start.23 = (f32[8,1024]{1,0:T(8,128)S(1)}, f32[8,1024]{1,0:T(8,128)S(1)}, u32[]{:S(2)}, u32[]{:S(2)}) collective-permute-start(f32[8,1024]{1,0:T(8,128)S(1)} %select_add_fusion), channel_id=1, source_target_pairs={{0,96},{2,26},{4,100},{6,30},{8,104},{10,2},{12,108},{14,6},{16,11... | collective-permute-start | bytes 98312 | tf_op jit(solution)/shard_map/ppermute | solution.py:368
  127.1 3.2 %collective-permute-start.17 = (f32[32,2048]{1,0:T(8,128)}, f32[32,2048]{1,0:T(8,128)S(1)}, u32[]{:S(2)}, u32[]{:S(2)}) collective-permute-start(f32[32,2048]{1,0:T(8,128)} %get-tuple-element.170), channel_id=1, source_target_pairs={{0,24},{2,98},{4,28},{6,102},{8,0},{10,106},{12,4},{14,110},{16,8}... | collective-permute-start | bytes 786440 | tf_op jit(solution)/shard_map/ppermute | solution.py:368
  136.5 3.1 %collective-permute-start.26 = (f32[72,1024]{1,0:T(8,128)S(1)}, f32[72,1024]{1,0:T(8,128)S(1)}, u32[]{:S(2)}, u32[]{:S(2)}) collective-permute-start(f32[72,1024]{1,0:T(8,128)S(1)} %get-tuple-element.192), channel_id=1, source_target_pairs={{0,24},{2,98},{4,28},{6,102},{8,0},{10,106},{12,4},{14,110},{16,8}... | collective-permute-start | bytes 884744 | tf_op jit(solution)/shard_map/ppermute | solution.py:368
  140.3 3.1 %collective-permute-done.18 = f32[128,1024]{1,0:T(8,128)S(1)} collective-permute-done((f32[128,1024]{1,0:T(8,128)}, f32[128,1024]{1,0:T(8,128)S(1)}, u32[]{:S(2)}, u32[]{:S(2)}) %collective-permute-start.18) | collective-permute-done | bytes 524320 | tf_op jit(solution)/shard_map/ppermute | solution.py:24
  143.6 5.6 %collective-permute-start.31 = (f32[32,2048]{1,0:T(8,128)S(1)}, f32[32,2048]{1,0:T(8,128)S(1)}, u32[]{:S(2)}, u32[]{:S(2)}) collective-permute-start(f32[32,2048]{1,0:T(8,128)S(1)} %slice.250), channel_id=1, source_target_pairs={{0,4},{4,0},{1,5},{5,1},{2,6},{6,2},{3,7},{7,3},{8,12},{12,8},{9,1... | collective-permute-start | bytes 786440 | tf_op jit(solution)/shard_map/ppermute | solution.py:24
  153.8 3.1 %collective-permute-start.28 = (f32[32,1024]{1,0:T(8,128)S(1)}, f32[32,1024]{1,0:T(8,128)S(1)}, u32[]{:S(2)}, u32[]{:S(2)}) collective-permute-start(f32[32,1024]{1,0:T(8,128)S(1)} %get-tuple-element.174), channel_id=1, source_target_pairs={{0,24},{2,98},{4,28},{6,102},{8,0},{10,106},{12,4},{14,110},{16,8}... | collective-permute-start | bytes 393224 | tf_op jit(solution)/shard_map/ppermute | solution.py:368
  158.0 5.5 %collective-permute-done.27 = f32[40,1024]{1,0:T(8,128)S(1)} collective-permute-done((f32[40,1024]{1,0:T(8,128)S(1)}, f32[40,1024]{1,0:T(8,128)S(1)}, u32[]{:S(2)}, u32[]{:S(2)}) %collective-permute-start.27) | collective-permute-done | bytes 163872 | tf_op jit(solution)/shard_map/ppermute | solution.py:368
  163.7 3.6 %collective-permute-start.29 = (f32[40,1024]{1,0:T(8,128)S(1)}, f32[40,1024]{1,0:T(8,128)S(1)}, u32[]{:S(2)}, u32[]{:S(2)}) collective-permute-start(f32[40,1024]{1,0:T(8,128)S(1)} %pad_maximum_fusion.5), channel_id=1, source_target_pairs={{0,4},{4,0},{1,5},{5,1},{2,6},{6,2},{3,7},{7,3},{8,12},{12,8},{9,1... | collective-permute-start | bytes 491528 | tf_op jit(solution)/shard_map/ppermute | solution.py:24
  168.0 3.1 %collective-permute-done.29 = f32[40,1024]{1,0:T(8,128)S(1)} collective-permute-done((f32[40,1024]{1,0:T(8,128)S(1)}, f32[40,1024]{1,0:T(8,128)S(1)}, u32[]{:S(2)}, u32[]{:S(2)}) %collective-permute-start.29) | collective-permute-done | bytes 163872 | tf_op jit(solution)/shard_map/ppermute | solution.py:24
  (185 shorter events, 76.3 us)
Async XLA Ops:
  26.3 18.7 %collective-permute-start.3 = (f32[256,1024]{1,0:T(8,128)}, f32[256,1024]{1,0:T(8,128)}, u32[]{:S(2)}, u32[]{:S(2)}) collective-permute-start(f32[256,1024]{1,0:T(8,128)} %get-tuple-element.90), channel_id=1, source_target_pairs={{0,32},{2,10},{4,36},{6,14},{8,40},{10,18},{12,44},{14,22},{16,48}... | collective-permute-start | bytes 3145736 | tf_op jit(solution)/shard_map/ppermute | solution.py:368
  27.9 17.1 %collective-permute-start.4 = (f32[256,1024]{1,0:T(8,128)}, f32[256,1024]{1,0:T(8,128)}, u32[]{:S(2)}, u32[]{:S(2)}) collective-permute-start(f32[256,1024]{1,0:T(8,128)} %get-tuple-element.91), channel_id=1, source_target_pairs={{0,96},{2,26},{4,100},{6,30},{8,104},{10,2},{12,108},{14,6},{16,11... | collective-permute-start | bytes 3145736 | tf_op jit(solution)/shard_map/ppermute | solution.py:368
  37.4 23.4 %collective-permute-start.6 = (f32[256,1024]{1,0:T(8,128)}, f32[256,1024]{1,0:T(8,128)}, u32[]{:S(2)}, u32[]{:S(2)}) collective-permute-start(f32[256,1024]{1,0:T(8,128)} %get-tuple-element.98), channel_id=1, source_target_pairs={{0,96},{2,26},{4,100},{6,30},{8,104},{10,2},{12,108},{14,6},{16,11... | collective-permute-start | bytes 3145736 | tf_op jit(solution)/shard_map/ppermute | solution.py:368
  39.0 21.8 %collective-permute-start.5 = (f32[256,1024]{1,0:T(8,128)}, f32[256,1024]{1,0:T(8,128)}, u32[]{:S(2)}, u32[]{:S(2)}) collective-permute-start(f32[256,1024]{1,0:T(8,128)} %get-tuple-element.97), channel_id=1, source_target_pairs={{0,32},{2,10},{4,36},{6,14},{8,40},{10,18},{12,44},{14,22},{16,48}... | collective-permute-start | bytes 3145736 | tf_op jit(solution)/shard_map/ppermute | solution.py:368
  48.8 37.2 %collective-permute-start.10 = (f32[128,1024]{1,0:T(8,128)}, f32[128,1024]{1,0:T(8,128)}, u32[]{:S(2)}, u32[]{:S(2)}) collective-permute-start(f32[128,1024]{1,0:T(8,128)} %get-tuple-element.105), channel_id=1, source_target_pairs={{0,32},{2,10},{4,36},{6,14},{8,40},{10,18},{12,44},{14,22},{16,48}... | collective-permute-start | bytes 1572872 | tf_op jit(solution)/shard_map/ppermute | solution.py:368
  49.2 40.0 %collective-permute-start.11 = (f32[128,1024]{1,0:T(8,128)}, f32[128,1024]{1,0:T(8,128)}, u32[]{:S(2)}, u32[]{:S(2)}) collective-permute-start(f32[128,1024]{1,0:T(8,128)} %get-tuple-element.106), channel_id=1, source_target_pairs={{0,96},{2,26},{4,100},{6,30},{8,104},{10,2},{12,108},{14,6},{16,11... | collective-permute-start | bytes 1572872 | tf_op jit(solution)/shard_map/ppermute | solution.py:368
  60.8 21.4 %collective-permute-start.7 = (f32[128,1024]{1,0:T(8,128)}, f32[128,1024]{1,0:T(8,128)}, u32[]{:S(2)}, u32[]{:S(2)}) collective-permute-start(f32[128,1024]{1,0:T(8,128)} %get-tuple-element.113), channel_id=1, source_target_pairs={{0,2},{2,0},{1,3},{3,1},{4,6},{6,4},{5,7},{7,5},{8,10},{10,8},{9,1... | collective-permute-start | bytes 1572872 | tf_op jit(solution)/shard_map/ppermute | solution.py:24
  64.5 24.8 %collective-permute-start.12 = (f32[128,1024]{1,0:T(8,128)}, f32[128,1024]{1,0:T(8,128)}, u32[]{:S(2)}, u32[]{:S(2)}) collective-permute-start(f32[128,1024]{1,0:T(8,128)} %get-tuple-element.116), channel_id=1, source_target_pairs={{0,32},{2,10},{4,36},{6,14},{8,40},{10,18},{12,44},{14,22},{16,48}... | collective-permute-start | bytes 1572872 | tf_op jit(solution)/shard_map/ppermute | solution.py:368
  64.9 24.3 %collective-permute-start.13 = (f32[128,1024]{1,0:T(8,128)}, f32[128,1024]{1,0:T(8,128)}, u32[]{:S(2)}, u32[]{:S(2)}) collective-permute-start(f32[128,1024]{1,0:T(8,128)} %get-tuple-element.117), channel_id=1, source_target_pairs={{0,96},{2,26},{4,100},{6,30},{8,104},{10,2},{12,108},{14,6},{16,11... | collective-permute-start | bytes 1572872 | tf_op jit(solution)/shard_map/ppermute | solution.py:368
  85.9 19.1 %collective-permute-start.8 = (f32[256,1024]{1,0:T(8,128)}, f32[256,1024]{1,0:T(8,128)}, u32[]{:S(2)}, u32[]{:S(2)}) collective-permute-start(f32[256,1024]{1,0:T(8,128)} %get-tuple-element.122), channel_id=1, source_target_pairs={{0,32},{2,10},{4,36},{6,14},{8,40},{10,18},{12,44},{14,22},{16,48}... | collective-permute-start | bytes 3145736 | tf_op jit(solution)/shard_map/ppermute | solution.py:368
  86.0 21.5 %collective-permute-start.9 = (f32[256,1024]{1,0:T(8,128)}, f32[256,1024]{1,0:T(8,128)}, u32[]{:S(2)}, u32[]{:S(2)}) collective-permute-start(f32[256,1024]{1,0:T(8,128)} %get-tuple-element.123), channel_id=1, source_target_pairs={{0,96},{2,26},{4,100},{6,30},{8,104},{10,2},{12,108},{14,6},{16,11... | collective-permute-start | bytes 3145736 | tf_op jit(solution)/shard_map/ppermute | solution.py:368
  94.4 20.6 %collective-permute-start.15 = (f32[64,2048]{1,0:T(8,128)}, f32[64,2048]{1,0:T(8,128)}, u32[]{:S(2)}, u32[]{:S(2)}) collective-permute-start(f32[64,2048]{1,0:T(8,128)} %get-tuple-element.172), channel_id=1, source_target_pairs={{0,24},{2,98},{4,28},{6,102},{8,0},{10,106},{12,4},{14,110},{16,8}... | collective-permute-start | bytes 1572872 | tf_op jit(solution)/shard_map/ppermute | solution.py:368
  97.5 17.5 %collective-permute-start.14 = (f32[64,2048]{1,0:T(8,128)}, f32[64,2048]{1,0:T(8,128)}, u32[]{:S(2)}, u32[]{:S(2)}) collective-permute-start(f32[64,2048]{1,0:T(8,128)} %get-tuple-element.173), channel_id=1, source_target_pairs={{0,8},{2,34},{4,12},{6,38},{8,16},{10,42},{12,20},{14,46},{16,24},... | collective-permute-start | bytes 1572872 | tf_op jit(solution)/shard_map/ppermute | solution.py:368
  101.7 19.4 %collective-permute-start.19 = (f32[136,1024]{1,0:T(8,128)}, f32[136,1024]{1,0:T(8,128)}, u32[]{:S(2)}, u32[]{:S(2)}) collective-permute-start(f32[136,1024]{1,0:T(8,128)} %pad_maximum_fusion), channel_id=1, source_target_pairs={{0,1},{1,0},{2,3},{3,2},{4,5},{5,4},{6,7},{7,6},{8,9},{9,8},{10,11... | collective-permute-start | bytes 1671176 | tf_op jit(solution)/shard_map/ppermute | solution.py:24
  111.1 23.5 %collective-permute-start.20 = (f32[128,1024]{1,0:T(8,128)}, f32[128,1024]{1,0:T(8,128)}, u32[]{:S(2)}, u32[]{:S(2)}) collective-permute-start(f32[128,1024]{1,0:T(8,128)} %get-tuple-element.139), channel_id=1, source_target_pairs={{0,32},{2,10},{4,36},{6,14},{8,40},{10,18},{12,44},{14,22},{16,48}... | collective-permute-start | bytes 1572872 | tf_op jit(solution)/shard_map/ppermute | solution.py:368
  111.2 23.4 %collective-permute-start.21 = (f32[128,1024]{1,0:T(8,128)}, f32[128,1024]{1,0:T(8,128)}, u32[]{:S(2)}, u32[]{:S(2)}) collective-permute-start(f32[128,1024]{1,0:T(8,128)} %get-tuple-element.140), channel_id=1, source_target_pairs={{0,96},{2,26},{4,100},{6,30},{8,104},{10,2},{12,108},{14,6},{16,11... | collective-permute-start | bytes 1572872 | tf_op jit(solution)/shard_map/ppermute | solution.py:368
  121.9 10.5 %collective-permute-start.23 = (f32[8,1024]{1,0:T(8,128)S(1)}, f32[8,1024]{1,0:T(8,128)S(1)}, u32[]{:S(2)}, u32[]{:S(2)}) collective-permute-start(f32[8,1024]{1,0:T(8,128)S(1)} %select_add_fusion), channel_id=1, source_target_pairs={{0,96},{2,26},{4,100},{6,30},{8,104},{10,2},{12,108},{14,6},{16,11... | collective-permute-start | bytes 98312 | tf_op jit(solution)/shard_map/ppermute | solution.py:368
  127.1 12.6 %collective-permute-start.17 = (f32[32,2048]{1,0:T(8,128)}, f32[32,2048]{1,0:T(8,128)S(1)}, u32[]{:S(2)}, u32[]{:S(2)}) collective-permute-start(f32[32,2048]{1,0:T(8,128)} %get-tuple-element.170), channel_id=1, source_target_pairs={{0,24},{2,98},{4,28},{6,102},{8,0},{10,106},{12,4},{14,110},{16,8}... | collective-permute-start | bytes 786440 | tf_op jit(solution)/shard_map/ppermute | solution.py:368
  132.4 7.9 %collective-permute-start.16 = (f32[32,2048]{1,0:T(8,128)}, f32[32,2048]{1,0:T(8,128)S(1)}, u32[]{:S(2)}, u32[]{:S(2)}) collective-permute-start(f32[32,2048]{1,0:T(8,128)} %get-tuple-element.171), channel_id=1, source_target_pairs={{0,8},{2,34},{4,12},{6,38},{8,16},{10,42},{12,20},{14,46},{16,24},... | collective-permute-start | bytes 786440 | tf_op jit(solution)/shard_map/ppermute | solution.py:368
  132.5 10.8 %collective-permute-start.18 = (f32[128,1024]{1,0:T(8,128)}, f32[128,1024]{1,0:T(8,128)S(1)}, u32[]{:S(2)}, u32[]{:S(2)}) collective-permute-start(f32[128,1024]{1,0:T(8,128)} %convolution_add_fusion), channel_id=1, source_target_pairs={{0,1},{1,0},{2,3},{3,2},{4,5},{5,4},{6,7},{7,6},{8,9},{9,8},{10,11... | collective-permute-start | bytes 1572872 | tf_op jit(solution)/shard_map/ppermute | solution.py:24
  136.5 17.2 %collective-permute-start.26 = (f32[72,1024]{1,0:T(8,128)S(1)}, f32[72,1024]{1,0:T(8,128)S(1)}, u32[]{:S(2)}, u32[]{:S(2)}) collective-permute-start(f32[72,1024]{1,0:T(8,128)S(1)} %get-tuple-element.192), channel_id=1, source_target_pairs={{0,24},{2,98},{4,28},{6,102},{8,0},{10,106},{12,4},{14,110},{16,8}... | collective-permute-start | bytes 884744 | tf_op jit(solution)/shard_map/ppermute | solution.py:368
  139.7 14.1 %collective-permute-start.25 = (f32[72,1024]{1,0:T(8,128)S(1)}, f32[72,1024]{1,0:T(8,128)S(1)}, u32[]{:S(2)}, u32[]{:S(2)}) collective-permute-start(f32[72,1024]{1,0:T(8,128)S(1)} %get-tuple-element.193), channel_id=1, source_target_pairs={{0,8},{2,34},{4,12},{6,38},{8,16},{10,42},{12,20},{14,46},{16,24},... | collective-permute-start | bytes 884744 | tf_op jit(solution)/shard_map/ppermute | solution.py:368
  143.6 10.0 %collective-permute-start.31 = (f32[32,2048]{1,0:T(8,128)S(1)}, f32[32,2048]{1,0:T(8,128)S(1)}, u32[]{:S(2)}, u32[]{:S(2)}) collective-permute-start(f32[32,2048]{1,0:T(8,128)S(1)} %slice.250), channel_id=1, source_target_pairs={{0,4},{4,0},{1,5},{5,1},{2,6},{6,2},{3,7},{7,3},{8,12},{12,8},{9,1... | collective-permute-start | bytes 786440 | tf_op jit(solution)/shard_map/ppermute | solution.py:24
  153.8 9.8 %collective-permute-start.28 = (f32[32,1024]{1,0:T(8,128)S(1)}, f32[32,1024]{1,0:T(8,128)S(1)}, u32[]{:S(2)}, u32[]{:S(2)}) collective-permute-start(f32[32,1024]{1,0:T(8,128)S(1)} %get-tuple-element.174), channel_id=1, source_target_pairs={{0,24},{2,98},{4,28},{6,102},{8,0},{10,106},{12,4},{14,110},{16,8}... | collective-permute-start | bytes 393224 | tf_op jit(solution)/shard_map/ppermute | solution.py:368
  (35 other events, 350.1 us)

commit v4 on v3

--- a/solution.py
+++ b/solution.py
@@ -175,7 +175,7 @@
 
 
 def prologue_kernel(
-    rows_in, grads_in, valid, gain, bias, message, branch_in, units_in, heads_in, unit_rows, inv_scale
+    rows_in, grads_in, valid, gain, bias, message, branch_in, units_in, heads_in, unit_rows, inv_scale, sums
 ):
     width = rows_in.shape[1]
     hidden = rows_in[...].astype(jnp.float32)
@@ -186,6 +186,7 @@
     unit_rows[...] = unit
     branch = grads_in[...].astype(jnp.float32) * valid[...]
     message[:, :width] = branch
+    sums[...] = jnp.sum(branch, axis=0, keepdims=True)
     branch_in[...] = branch.astype(jnp.bfloat16)
     heads = unit * gain[0:1, :] + bias[0:1, :]
     units = unit * gain[1:2, :] + bias[1:2, :]
@@ -207,6 +208,7 @@
             low,
             jax.ShapeDtypeStruct((rows, width), jnp.float32),
             jax.ShapeDtypeStruct((rows, 1), jnp.float32),
+            jax.ShapeDtypeStruct((1, width), jnp.float32),
         ),
         name="prologue",
     )(rows_in, grads_in, valid, gain, bias)
@@ -316,34 +318,16 @@
     )(*lefts, own, near)
 
 
-def middle_kernel(low, high, minus, plus, low_out, high_out):
-    low_out[...] = low[...] + minus[...]
-    high_out[...] = high[...] + plus[...]
-
-
 def middle(low, high, minus, plus):
-    half, cols = low.shape
-    pieces = 4
-    block = (half, cols // pieces)
-    same = pl.BlockSpec(block, lambda i: (0, i))
-    shape = jax.ShapeDtypeStruct(low.shape, jnp.float32)
-    return pl.pallas_call(
-        middle_kernel,
-        grid=(pieces,),
-        in_specs=[same, same, pl.BlockSpec(block, lambda i: (1, i)), same],
-        out_specs=[same, same],
-        out_shape=(shape, shape),
-        name="middle",
-    )(low, high, minus, plus)
+    half = low.shape[0]
+    return low + minus[half:], high + plus[:half]
 
 
 def finish(kept, minus, plus, low, high):
     half = kept.shape[0] // 2
-    return (
-        kept
-        + jnp.concatenate([plus[half:], minus[:half]], axis=0)
-        + jnp.concatenate([low, high], axis=0)
-    )
+    first = kept[:half] + plus[half:] + low
+    last = kept[half:] + minus[:half] + high
+    return jnp.concatenate(lax.optimization_barrier((first, last)), axis=0)
 
 
 def moves():
@@ -442,7 +426,7 @@
     segment, position = layout_rows(lengths, owner_group, row_offset, own_index, row_count)
     valid_rows = (segment >= 0).astype(jnp.float32)[:, None]
 
-    message, branch_in, units_in, heads_in, unit_rows, inv_scale = prologue(
+    message, branch_in, units_in, heads_in, unit_rows, inv_scale, branch_sums = prologue(
         block_input, cotangent, valid_rows, norm_gain, norm_bias
     )
     near_rows = shift(message, CORE, 1)
@@ -551,7 +535,7 @@
             jnp.sum(units_grad * unit_rows, axis=0)[None],
             jnp.sum(heads_grad, axis=0)[None],
             jnp.sum(units_grad, axis=0)[None],
-            jnp.sum(message[:, :model_width], axis=0)[None],
+            branch_sums,
             pre_sums.reshape(table_rows, model_width),
         ],
         axis=0,

time: 177 us -> 159 us (0.90)
  Pallas kernels: 56.6 us -> 45.7 us
  other arithmetic: 23.8 us -> 31.8 us
  local copies, waits for them, and re-layouts: 11.8 us -> 4.69 us
  waiting for transfers between devices: 21.2 us -> 15 us
    add x3 -> x9, other arithmetic: 5.76 us -> 18.5 us  [the longest x6 12 us: middle(): return (low + minus[half:], high + plus[:half])]
    pallas_call x3 -> x0, Pallas kernels: 11 us -> none  [middle(): pl.pallas_call(middle_kernel, grid=(pieces,), in_specs=[same, same, pl.Bl...]
    slice x6 -> x1, local copies, waits for them, and re-layouts: 9.8 us -> 0.02 us  [second_send(): up = jnp.concatenate([rows[half:3 * half], extra])]
    ppermute x23, waiting for transfers between devices: 12 us -> 7.44 us  [ring(): return lax.ppermute(array, DP, MOVES[first, step])]
  transfers between devices with their start and end apart: 33 -> 33, of which waited for: 10 -> 6; matrix products, arithmetic and copies ran while one was open for 24% -> 26% of each run, Pallas kernels for 26% -> 22%
where the time goes in v4:
time: 159 us; the launch traced here: 157 us
  starting transfers between devices  48.5 us (31%)
  Pallas kernels  45.7 us (29%)
  other arithmetic  31.8 us (20%)
  waiting for transfers between devices  15 us (9%)
  matrix products  10.3 us (6%)
  local copies, waits for them, and re-layouts  4.69 us (3%)
    ppermute x23, starting transfers between devices, ring(): return lax.ppermute(array, DP, MOVES[first, step])  36.2 us
    pallas_call x3, Pallas kernels, pick(): pl.pallas_call(pick_kernel, grid=(pieces,), in_specs=[pl.BlockSpec((width...  13 us
    ppermute x10, starting transfers between devices, shift(): lax.ppermute(array, axis, [(i, (i + step) % size) for i in range(size)])  12.3 us
    add x6, other arithmetic, middle(): return (low + minus[half:], high + plus[:half])  12 us
    pallas_call x3, Pallas kernels, products(): pl.pallas_call(functools.partial(product_kernel, splits), out_shape=tuple...  10.7 us
    pallas_call x2, Pallas kernels, hidden_call(): pl.pallas_call(kernel, grid_spec=pltpu.PrefetchScalarGridSpec(num_scalar_...  10.3 us
    pallas_call x1, Pallas kernels, attention(): pl.pallas_call(attention_kernel, in_specs=[pl.BlockSpec(memory_space=pltp...  8.64 us
    ppermute x10, waiting for transfers between devices, shift(): lax.ppermute(array, axis, [(i, (i + step) % size) for i in range(size)])  7.58 us
  transfers between devices with their start and end apart: 33, of which 6 were waited for; matrix products, arithmetic and copies ran while one was open for 26% of the time, Pallas kernels for 22%

profile of v4, /device:TPU:0, one launch (start us, length us, event | category | flops | bytes accessed | tf_op | source)
XLA Modules:
  0.0 157.5 jit_solution(3585940355734750266)
XLA Ops:
  2.9 3.0 %prologue.1 = (f32[128,3072]{1,0:T(8,128)}, bf16[128,1024]{1,0:T(8,128)(2,1)}, bf16[128,1024]{1,0:T(8,128)(2,1)}, bf16[128,1024]{1,0:T(8,128)(2,1)}, f32[128,102...) custom-call(bf16[128,1024]{1,0:T(8,128)(2,1)} %rows_in.1, bf16[128,1024]{1,0:T(8,128)(2,1)} %grads_in.1, ...), custom_call_target="tpu_custom_call" | custom-call | tf_op jit(solution)/shard_map/prologue/pallas_call | solution.py:202
  6.0 5.2 %up.1 = (bf16[128,2048]{1,0:T(8,128)(2,1)}, f32[128,2048]{1,0:T(8,128)}, bf16[128,1024]{1,0:T(8,128)(2,1)}, f32[128,1024]{1,0:T(8,128)}) custom-call(s32[1]{0:T(128)} %bitcast.core, bf16[128,1024]{1,0:T(8,128)(2,1)} %get-tuple-element.96.units_in.own, bf16[1024,2048]{1,0:T(8,128)(2,1)} %bitcast.52, f32[1,2048]{1,0:T(1,128)} %bias.1), custom_call_target="tpu_custom_call" | custom-call | tf_op jit(solution)/shard_map/up/pallas_call | solution.py:272
  13.5 4.3 %pick.3.refs_0_ = bf16[1024,256]{1,0:T(8,128)(2,1)} custom-call(bf16[1024,1024]{1,0:T(8,128)(2,1)} %fusion.chosen, bf16[128,1024]{1,0:T(8,128)(2,1)} %get-tuple-element.102.own.branch_in, f32[128,3072]{1,0:T(8,128)} %collective-permute-done.near), custom_call_target="tpu_custom_call" | custom-call | tf_op jit(solution)/shard_map/pick/pallas_call | solution.py:386
  17.8 3.5 %products.3 = (f32[128,1024]{1,0:T(8,128)}, f32[128,1024]{1,0:T(8,128)}, f32[256,1024]{1,0:T(8,128)}, f32[256,1024]{1,0:T(8,128)}, f32[256,1024]{1,0:T(8,128)}) custom-call(bf16[1024,256]{1,0:T(8,128)(2,1)} %pick.3.refs_0_, bf16[128,1024]{1,0:T(8,128)(2,1)} %get-tuple-element.90.refs_1_, f32[128,1024]{1,0:T(8,128)} %collective-permute-done.1.refs_2_), custom_call_target="tpu_custom_call" | custom-call | tf_op jit(solution)/shard_map/products/pallas_call | solution.py:314
  21.3 5.1 %down.1 = (bf16[128,2048]{1,0:T(8,128)(2,1)}, f32[1,2048]{1,0:T(1,128)}, bf16[128,1024]{1,0:T(8,128)(2,1)}, f32[128,1024]{1,0:T(8,128)}) custom-call(s32[1]{0:T(128)} %bitcast.core, bf16[128,1024]{1,0:T(8,128)(2,1)} %get-tuple-element.102.own.branch_in, bf16[1024,2048]{1,0:T(8,128)(2,1)} %bitcast.53, f32[128,2048]{1,0:T(8,128)} %get-tuple-element.94.slope), custom_call_target="tpu_custom_call" | custom-call | tf_op jit(solution)/shard_map/down/pallas_call | solution.py:272
  29.7 4.4 %pick.4.refs_0_ = bf16[1024,256]{1,0:T(8,128)(2,1)} custom-call(bf16[1024,1024]{1,0:T(8,128)(2,1)} %fusion.chosen, bf16[128,1024]{1,0:T(8,128)(2,1)} %get-tuple-element.96.units_in.own, f32[128,3072]{1,0:T(8,128)} %collective-permute-done.near), custom_call_target="tpu_custom_call" | custom-call | tf_op jit(solution)/shard_map/pick/pallas_call | solution.py:386
  34.1 3.5 %products.4 = (f32[128,1024]{1,0:T(8,128)}, f32[128,1024]{1,0:T(8,128)}, f32[256,1024]{1,0:T(8,128)}, f32[256,1024]{1,0:T(8,128)}, f32[256,1024]{1,0:T(8,128)}) custom-call(bf16[1024,256]{1,0:T(8,128)(2,1)} %pick.4.refs_0_, bf16[128,1024]{1,0:T(8,128)(2,1)} %get-tuple-element.97.refs_1_, f32[128,1024]{1,0:T(8,128)} %collective-permute-done.2.refs_2_), custom_call_target="tpu_custom_call" | custom-call | tf_op jit(solution)/shard_map/products/pallas_call | solution.py:314
  38.0 2.9 %collective-permute-start.6 = (f32[256,1024]{1,0:T(8,128)}, f32[256,1024]{1,0:T(8,128)}, u32[]{:S(2)}, u32[]{:S(2)}) collective-permute-start(f32[256,1024]{1,0:T(8,128)} %get-tuple-element.99), channel_id=1, source_target_pairs={{0,96},{2,26},{4,100},{6,30},{8,104},{10,2},{12,108},{14,6},{16,11... | collective-permute-start | bytes 3145736 | tf_op jit(solution)/shard_map/ppermute | solution.py:352
  40.8 2.2 %fusion.6.context_grad = f32[128,512]{1,0:T(8,128)} fusion(bf16[128,1024]{1,0:T(8,128)(2,1)S(1)} %copy-done.13, bf16[1,1024,512]{2,1,0:T(8,128)(2,1)} %param.16), kind=kOutput, calls=%fused_computation.9 | convolution fusion | flops 134217728 | bytes 1572864 | tf_op jit(solution)/shard_map/dot_general | solution.py:470
  44.1 2.4 %fusion.3.projected = f32[128,1536]{1,0:T(8,128)} fusion(bf16[128,1024]{1,0:T(8,128)(2,1)} %get-tuple-element.115.own, bf16[1,1024,1536]{2,1,0:T(8,128)(2,1)S(1)} %copy-done), kind=kOutput, calls=%fused_computation.4 | convolution fusion | flops 402653184 | bytes 4194304 | tf_op jit(solution)/shard_map/dot_general | solution.py:469
  52.3 8.6 %attention.1 = (bf16[128,512]{1,0:T(8,128)(2,1)}, bf16[128,1536]{1,0:T(8,128)(2,1)}, bf16[128,1024]{1,0:T(8,128)(2,1)}, f32[128,1024]{1,0:T(8,128)}) custom-call(s32[1]{0:T(128)} %bitcast.core, f32[128,1536]{1,0:T(8,128)} %fusion.3.projected, f32[128,512]{1,0:T(8,128)} %fusion.6.context_grad, s32[128,1]{1,0:T(8,128)} %copy-done.20, ...), custom_call_target="tpu_custom_call" | custom-call | tf_op jit(solution)/shard_map/attention/pallas_call | solution.py:160
  68.5 4.3 %pick.5.refs_1_ = bf16[1024,256]{1,0:T(8,128)(2,1)} custom-call(bf16[1024,1024]{1,0:T(8,128)(2,1)} %fusion.chosen, bf16[128,1024]{1,0:T(8,128)(2,1)} %get-tuple-element.115.own, f32[128,3072]{1,0:T(8,128)} %collective-permute-done.near), custom_call_target="tpu_custom_call" | custom-call | tf_op jit(solution)/shard_map/pick/pallas_call | solution.py:386
  72.9 3.8 %products.5 = (f32[128,1024]{1,0:T(8,128)}, f32[128,1024]{1,0:T(8,128)}, f32[256,1024]{1,0:T(8,128)}, f32[256,1024]{1,0:T(8,128)}, f32[256,1024]{1,0:T(8,128)}) custom-call(bf16[1024,256]{1,0:T(8,128)(2,1)} %pick.3.refs_0_, bf16[1024,256]{1,0:T(8,128)(2,1)} %pick.5.refs_1_, bf16[128,1024]{1,0:T(8,128)(2,1)} %get-tuple-element.116.refs_2_, ...), custom_call_target="tpu_custom_call" | custom-call | tf_op jit(solution)/shard_map/products/pallas_call | solution.py:314
  77.0 2.8 %collective-permute-start.9 = (f32[256,1024]{1,0:T(8,128)}, f32[256,1024]{1,0:T(8,128)}, u32[]{:S(2)}, u32[]{:S(2)}) collective-permute-start(f32[256,1024]{1,0:T(8,128)} %get-tuple-element.119), channel_id=1, source_target_pairs={{0,96},{2,26},{4,100},{6,30},{8,104},{10,2},{12,108},{14,6},{16,11... | collective-permute-start | bytes 3145736 | tf_op jit(solution)/shard_map/ppermute | solution.py:352
  97.1 3.0 %collective-permute-start.21 = (f32[128,1024]{1,0:T(8,128)}, f32[128,1024]{1,0:T(8,128)}, u32[]{:S(2)}, u32[]{:S(2)}) collective-permute-start(f32[128,1024]{1,0:T(8,128)} %slice_add_fusion.6), channel_id=1, source_target_pairs={{0,96},{2,26},{4,100},{6,30},{8,104},{10,2},{12,108},{14,6},{16,11... | collective-permute-start | bytes 1572872 | tf_op jit(solution)/shard_map/ppermute | solution.py:352
  109.4 2.8 %collective-permute-start.23 = (f32[8,1024]{1,0:T(8,128)S(1)}, f32[8,1024]{1,0:T(8,128)S(1)}, u32[]{:S(2)}, u32[]{:S(2)}) collective-permute-start(f32[8,1024]{1,0:T(8,128)S(1)} %select_add_fusion), channel_id=1, source_target_pairs={{0,96},{2,26},{4,100},{6,30},{8,104},{10,2},{12,108},{14,6},{16,11... | collective-permute-start | bytes 98312 | tf_op jit(solution)/shard_map/ppermute | solution.py:352
  115.9 3.8 %collective-permute-start.16 = (f32[32,2048]{1,0:T(8,128)}, f32[32,2048]{1,0:T(8,128)S(1)}, u32[]{:S(2)}, u32[]{:S(2)}) collective-permute-start(f32[32,2048]{1,0:T(8,128)} %get-tuple-element.173), channel_id=1, source_target_pairs={{0,8},{2,34},{4,12},{6,38},{8,16},{10,42},{12,20},{14,46},{16,24},... | collective-permute-start | bytes 786440 | tf_op jit(solution)/shard_map/ppermute | solution.py:352
  119.7 3.7 %collective-permute-start.17 = (f32[32,2048]{1,0:T(8,128)S(1)}, f32[32,2048]{1,0:T(8,128)S(1)}, u32[]{:S(2)}, u32[]{:S(2)}) collective-permute-start(f32[32,2048]{1,0:T(8,128)S(1)} %get-tuple-element.172), channel_id=1, source_target_pairs={{0,24},{2,98},{4,28},{6,102},{8,0},{10,106},{12,4},{14,110},{16,8}... | collective-permute-start | bytes 786440 | tf_op jit(solution)/shard_map/ppermute | solution.py:352
  125.8 3.2 %collective-permute-start.26 = (f32[72,1024]{1,0:T(8,128)S(1)}, f32[72,1024]{1,0:T(8,128)S(1)}, u32[]{:S(2)}, u32[]{:S(2)}) collective-permute-start(f32[72,1024]{1,0:T(8,128)S(1)} %get-tuple-element.198), channel_id=1, source_target_pairs={{0,24},{2,98},{4,28},{6,102},{8,0},{10,106},{12,4},{14,110},{16,8}... | collective-permute-start | bytes 884744 | tf_op jit(solution)/shard_map/ppermute | solution.py:352
  129.2 4.1 %collective-permute-start.31 = (f32[32,2048]{1,0:T(8,128)S(1)}, f32[32,2048]{1,0:T(8,128)S(1)}, u32[]{:S(2)}, u32[]{:S(2)}) collective-permute-start(f32[32,2048]{1,0:T(8,128)S(1)} %slice.283), channel_id=1, source_target_pairs={{0,4},{4,0},{1,5},{5,1},{2,6},{6,2},{3,7},{7,3},{8,12},{12,8},{9,1... | collective-permute-start | bytes 786440 | tf_op jit(solution)/shard_map/ppermute | solution.py:24
  134.2 3.4 %collective-permute-done.31 = f32[32,2048]{1,0:T(8,128)S(1)} collective-permute-done((f32[32,2048]{1,0:T(8,128)S(1)}, f32[32,2048]{1,0:T(8,128)S(1)}, u32[]{:S(2)}, u32[]{:S(2)}) %collective-permute-start.31) | collective-permute-done | bytes 262176 | tf_op jit(solution)/shard_map/ppermute | solution.py:24
  141.0 5.5 %collective-permute-done.27 = f32[40,1024]{1,0:T(8,128)S(1)} collective-permute-done((f32[40,1024]{1,0:T(8,128)S(1)}, f32[40,1024]{1,0:T(8,128)S(1)}, u32[]{:S(2)}, u32[]{:S(2)}) %collective-permute-start.27) | collective-permute-done | bytes 163872 | tf_op jit(solution)/shard_map/ppermute | solution.py:352
  146.7 3.6 %collective-permute-start.29 = (f32[40,1024]{1,0:T(8,128)S(1)}, f32[40,1024]{1,0:T(8,128)S(1)}, u32[]{:S(2)}, u32[]{:S(2)}) collective-permute-start(f32[40,1024]{1,0:T(8,128)S(1)} %pad_maximum_fusion.4), channel_id=1, source_target_pairs={{0,4},{4,0},{1,5},{5,1},{2,6},{6,2},{3,7},{7,3},{8,12},{12,8},{9,1... | collective-permute-start | bytes 491528 | tf_op jit(solution)/shard_map/ppermute | solution.py:24
  150.9 2.6 %collective-permute-done.29 = f32[40,1024]{1,0:T(8,128)S(1)} collective-permute-done((f32[40,1024]{1,0:T(8,128)S(1)}, f32[40,1024]{1,0:T(8,128)S(1)}, u32[]{:S(2)}, u32[]{:S(2)}) %collective-permute-start.29) | collective-permute-done | bytes 163872 | tf_op jit(solution)/shard_map/ppermute | solution.py:24
  (199 shorter events, 64.3 us)
Async XLA Ops:
  26.4 7.7 %collective-permute-start.2 = (f32[128,1024]{1,0:T(8,128)}, f32[128,1024]{1,0:T(8,128)}, u32[]{:S(2)}, u32[]{:S(2)}) collective-permute-start(f32[128,1024]{1,0:T(8,128)} %get-tuple-element.95), channel_id=1, source_target_pairs={{0,2},{2,0},{1,3},{3,1},{4,6},{6,4},{5,7},{7,5},{8,10},{10,8},{9,1... | collective-permute-start | bytes 1572872 | tf_op jit(solution)/shard_map/ppermute | solution.py:24
  26.5 20.0 %collective-permute-start.3 = (f32[256,1024]{1,0:T(8,128)}, f32[256,1024]{1,0:T(8,128)}, u32[]{:S(2)}, u32[]{:S(2)}) collective-permute-start(f32[256,1024]{1,0:T(8,128)} %get-tuple-element.91), channel_id=1, source_target_pairs={{0,32},{2,10},{4,36},{6,14},{8,40},{10,18},{12,44},{14,22},{16,48}... | collective-permute-start | bytes 3145736 | tf_op jit(solution)/shard_map/ppermute | solution.py:352
  28.1 18.4 %collective-permute-start.4 = (f32[256,1024]{1,0:T(8,128)}, f32[256,1024]{1,0:T(8,128)}, u32[]{:S(2)}, u32[]{:S(2)}) collective-permute-start(f32[256,1024]{1,0:T(8,128)} %get-tuple-element.92), channel_id=1, source_target_pairs={{0,96},{2,26},{4,100},{6,30},{8,104},{10,2},{12,108},{14,6},{16,11... | collective-permute-start | bytes 3145736 | tf_op jit(solution)/shard_map/ppermute | solution.py:352
  37.6 23.4 %collective-permute-start.5 = (f32[256,1024]{1,0:T(8,128)}, f32[256,1024]{1,0:T(8,128)}, u32[]{:S(2)}, u32[]{:S(2)}) collective-permute-start(f32[256,1024]{1,0:T(8,128)} %get-tuple-element.98), channel_id=1, source_target_pairs={{0,32},{2,10},{4,36},{6,14},{8,40},{10,18},{12,44},{14,22},{16,48}... | collective-permute-start | bytes 3145736 | tf_op jit(solution)/shard_map/ppermute | solution.py:352
  38.0 23.0 %collective-permute-start.6 = (f32[256,1024]{1,0:T(8,128)}, f32[256,1024]{1,0:T(8,128)}, u32[]{:S(2)}, u32[]{:S(2)}) collective-permute-start(f32[256,1024]{1,0:T(8,128)} %get-tuple-element.99), channel_id=1, source_target_pairs={{0,96},{2,26},{4,100},{6,30},{8,104},{10,2},{12,108},{14,6},{16,11... | collective-permute-start | bytes 3145736 | tf_op jit(solution)/shard_map/ppermute | solution.py:352
  48.4 28.6 %collective-permute-start.11 = (f32[128,1024]{1,0:T(8,128)}, f32[128,1024]{1,0:T(8,128)}, u32[]{:S(2)}, u32[]{:S(2)}) collective-permute-start(f32[128,1024]{1,0:T(8,128)} %slice_add_fusion.10), channel_id=1, source_target_pairs={{0,96},{2,26},{4,100},{6,30},{8,104},{10,2},{12,108},{14,6},{16,11... | collective-permute-start | bytes 1572872 | tf_op jit(solution)/shard_map/ppermute | solution.py:352
  50.7 29.1 %collective-permute-start.10 = (f32[128,1024]{1,0:T(8,128)}, f32[128,1024]{1,0:T(8,128)}, u32[]{:S(2)}, u32[]{:S(2)}) collective-permute-start(f32[128,1024]{1,0:T(8,128)} %slice_add_fusion.11), channel_id=1, source_target_pairs={{0,32},{2,10},{4,36},{6,14},{8,40},{10,18},{12,44},{14,22},{16,48}... | collective-permute-start | bytes 1572872 | tf_op jit(solution)/shard_map/ppermute | solution.py:352
  61.0 11.9 %collective-permute-start.7 = (f32[128,1024]{1,0:T(8,128)}, f32[128,1024]{1,0:T(8,128)}, u32[]{:S(2)}, u32[]{:S(2)}) collective-permute-start(f32[128,1024]{1,0:T(8,128)} %get-tuple-element.111), channel_id=1, source_target_pairs={{0,2},{2,0},{1,3},{3,1},{4,6},{6,4},{5,7},{7,5},{8,10},{10,8},{9,1... | collective-permute-start | bytes 1572872 | tf_op jit(solution)/shard_map/ppermute | solution.py:24
  63.1 16.8 %collective-permute-start.13 = (f32[128,1024]{1,0:T(8,128)}, f32[128,1024]{1,0:T(8,128)}, u32[]{:S(2)}, u32[]{:S(2)}) collective-permute-start(f32[128,1024]{1,0:T(8,128)} %slice_add_fusion.8), channel_id=1, source_target_pairs={{0,96},{2,26},{4,100},{6,30},{8,104},{10,2},{12,108},{14,6},{16,11... | collective-permute-start | bytes 1572872 | tf_op jit(solution)/shard_map/ppermute | solution.py:352
  66.8 13.1 %collective-permute-start.12 = (f32[128,1024]{1,0:T(8,128)}, f32[128,1024]{1,0:T(8,128)}, u32[]{:S(2)}, u32[]{:S(2)}) collective-permute-start(f32[128,1024]{1,0:T(8,128)} %slice_add_fusion.9), channel_id=1, source_target_pairs={{0,32},{2,10},{4,36},{6,14},{8,40},{10,18},{12,44},{14,22},{16,48}... | collective-permute-start | bytes 1572872 | tf_op jit(solution)/shard_map/ppermute | solution.py:352
  76.6 18.4 %collective-permute-start.8 = (f32[256,1024]{1,0:T(8,128)}, f32[256,1024]{1,0:T(8,128)}, u32[]{:S(2)}, u32[]{:S(2)}) collective-permute-start(f32[256,1024]{1,0:T(8,128)} %get-tuple-element.118), channel_id=1, source_target_pairs={{0,32},{2,10},{4,36},{6,14},{8,40},{10,18},{12,44},{14,22},{16,48}... | collective-permute-start | bytes 3145736 | tf_op jit(solution)/shard_map/ppermute | solution.py:352
  77.0 18.1 %collective-permute-start.9 = (f32[256,1024]{1,0:T(8,128)}, f32[256,1024]{1,0:T(8,128)}, u32[]{:S(2)}, u32[]{:S(2)}) collective-permute-start(f32[256,1024]{1,0:T(8,128)} %get-tuple-element.119), channel_id=1, source_target_pairs={{0,96},{2,26},{4,100},{6,30},{8,104},{10,2},{12,108},{14,6},{16,11... | collective-permute-start | bytes 3145736 | tf_op jit(solution)/shard_map/ppermute | solution.py:352
  86.3 15.9 %collective-permute-start.14 = (f32[64,2048]{1,0:T(8,128)}, f32[64,2048]{1,0:T(8,128)}, u32[]{:S(2)}, u32[]{:S(2)}) collective-permute-start(f32[64,2048]{1,0:T(8,128)} %get-tuple-element.175), channel_id=1, source_target_pairs={{0,8},{2,34},{4,12},{6,38},{8,16},{10,42},{12,20},{14,46},{16,24},... | collective-permute-start | bytes 1572872 | tf_op jit(solution)/shard_map/ppermute | solution.py:352
  88.0 14.2 %collective-permute-start.15 = (f32[64,2048]{1,0:T(8,128)}, f32[64,2048]{1,0:T(8,128)}, u32[]{:S(2)}, u32[]{:S(2)}) collective-permute-start(f32[64,2048]{1,0:T(8,128)} %get-tuple-element.174), channel_id=1, source_target_pairs={{0,24},{2,98},{4,28},{6,102},{8,0},{10,106},{12,4},{14,110},{16,8}... | collective-permute-start | bytes 1572872 | tf_op jit(solution)/shard_map/ppermute | solution.py:352
  93.0 15.1 %collective-permute-start.19 = (f32[136,1024]{1,0:T(8,128)S(1)}, f32[136,1024]{1,0:T(8,128)S(1)}, u32[]{:S(2)}, u32[]{:S(2)}) collective-permute-start(f32[136,1024]{1,0:T(8,128)S(1)} %pad_maximum_fusion), channel_id=1, source_target_pairs={{0,1},{1,0},{2,3},{3,2},{4,5},{5,4},{6,7},{7,6},{8,9},{9,8},{10,11... | collective-permute-start | bytes 1671176 | tf_op jit(solution)/shard_map/ppermute | solution.py:24
  97.1 26.2 %collective-permute-start.21 = (f32[128,1024]{1,0:T(8,128)}, f32[128,1024]{1,0:T(8,128)}, u32[]{:S(2)}, u32[]{:S(2)}) collective-permute-start(f32[128,1024]{1,0:T(8,128)} %slice_add_fusion.6), channel_id=1, source_target_pairs={{0,96},{2,26},{4,100},{6,30},{8,104},{10,2},{12,108},{14,6},{16,11... | collective-permute-start | bytes 1572872 | tf_op jit(solution)/shard_map/ppermute | solution.py:352
  102.2 21.2 %collective-permute-start.20 = (f32[128,1024]{1,0:T(8,128)}, f32[128,1024]{1,0:T(8,128)}, u32[]{:S(2)}, u32[]{:S(2)}) collective-permute-start(f32[128,1024]{1,0:T(8,128)} %slice_add_fusion.7), channel_id=1, source_target_pairs={{0,32},{2,10},{4,36},{6,14},{8,40},{10,18},{12,44},{14,22},{16,48}... | collective-permute-start | bytes 1572872 | tf_op jit(solution)/shard_map/ppermute | solution.py:352
  114.1 14.9 %collective-permute-start.18 = (f32[128,1024]{1,0:T(8,128)}, f32[128,1024]{1,0:T(8,128)S(1)}, u32[]{:S(2)}, u32[]{:S(2)}) collective-permute-start(f32[128,1024]{1,0:T(8,128)} %convolution_add_fusion), channel_id=1, source_target_pairs={{0,1},{1,0},{2,3},{3,2},{4,5},{5,4},{6,7},{7,6},{8,9},{9,8},{10,11... | collective-permute-start | bytes 1572872 | tf_op jit(solution)/shard_map/ppermute | solution.py:24
  115.9 13.1 %collective-permute-start.16 = (f32[32,2048]{1,0:T(8,128)}, f32[32,2048]{1,0:T(8,128)S(1)}, u32[]{:S(2)}, u32[]{:S(2)}) collective-permute-start(f32[32,2048]{1,0:T(8,128)} %get-tuple-element.173), channel_id=1, source_target_pairs={{0,8},{2,34},{4,12},{6,38},{8,16},{10,42},{12,20},{14,46},{16,24},... | collective-permute-start | bytes 786440 | tf_op jit(solution)/shard_map/ppermute | solution.py:352
  119.7 9.3 %collective-permute-start.17 = (f32[32,2048]{1,0:T(8,128)S(1)}, f32[32,2048]{1,0:T(8,128)S(1)}, u32[]{:S(2)}, u32[]{:S(2)}) collective-permute-start(f32[32,2048]{1,0:T(8,128)S(1)} %get-tuple-element.172), channel_id=1, source_target_pairs={{0,24},{2,98},{4,28},{6,102},{8,0},{10,106},{12,4},{14,110},{16,8}... | collective-permute-start | bytes 786440 | tf_op jit(solution)/shard_map/ppermute | solution.py:352
  125.7 12.1 %collective-permute-start.25 = (f32[72,1024]{1,0:T(8,128)S(1)}, f32[72,1024]{1,0:T(8,128)S(1)}, u32[]{:S(2)}, u32[]{:S(2)}) collective-permute-start(f32[72,1024]{1,0:T(8,128)S(1)} %get-tuple-element.199), channel_id=1, source_target_pairs={{0,8},{2,34},{4,12},{6,38},{8,16},{10,42},{12,20},{14,46},{16,24},... | collective-permute-start | bytes 884744 | tf_op jit(solution)/shard_map/ppermute | solution.py:352
  125.8 12.0 %collective-permute-start.26 = (f32[72,1024]{1,0:T(8,128)S(1)}, f32[72,1024]{1,0:T(8,128)S(1)}, u32[]{:S(2)}, u32[]{:S(2)}) collective-permute-start(f32[72,1024]{1,0:T(8,128)S(1)} %get-tuple-element.198), channel_id=1, source_target_pairs={{0,24},{2,98},{4,28},{6,102},{8,0},{10,106},{12,4},{14,110},{16,8}... | collective-permute-start | bytes 884744 | tf_op jit(solution)/shard_map/ppermute | solution.py:352
  129.2 8.5 %collective-permute-start.31 = (f32[32,2048]{1,0:T(8,128)S(1)}, f32[32,2048]{1,0:T(8,128)S(1)}, u32[]{:S(2)}, u32[]{:S(2)}) collective-permute-start(f32[32,2048]{1,0:T(8,128)S(1)} %slice.283), channel_id=1, source_target_pairs={{0,4},{4,0},{1,5},{5,1},{2,6},{6,2},{3,7},{7,3},{8,12},{12,8},{9,1... | collective-permute-start | bytes 786440 | tf_op jit(solution)/shard_map/ppermute | solution.py:24
  137.9 8.7 %collective-permute-start.28 = (f32[32,1024]{1,0:T(8,128)S(1)}, f32[32,1024]{1,0:T(8,128)S(1)}, u32[]{:S(2)}, u32[]{:S(2)}) collective-permute-start(f32[32,1024]{1,0:T(8,128)S(1)} %get-tuple-element.191), channel_id=1, source_target_pairs={{0,24},{2,98},{4,28},{6,102},{8,0},{10,106},{12,4},{14,110},{16,8}... | collective-permute-start | bytes 393224 | tf_op jit(solution)/shard_map/ppermute | solution.py:352
  (43 other events, 356.4 us)
